TPU v7x, 256 devices: a whole 4x4x8 slice. The times are simulated.
256 devices in a mesh: span: 16 (over x_hi, z), seq: 16 (over x_lo, y, core).
Axes of the slice: x: 4 (x_hi: 2, x_lo: 2; x = x_hi * 2 + x_lo), y: 4, z: 8, core: 2. Of those that a mesh axis runs over, the one named last changes fastest.
Arguments:
- queries: bfloat16 [16, 2048, 4096], P('span', 'seq')
- keys: bfloat16 [16, 2048, 4096], P('span', 'seq')
- values: bfloat16 [16, 2048, 4096], P('span', 'seq'), may hold values from -6 to 6
- audio: bfloat16 [16, 1024, 1024], P('span', 'seq'), may hold values from -6 to 6
- audio_wk: bfloat16 [1024, 4096], P(None, 'seq'), may hold values from -0.1875 to 0.1875
- audio_wv: bfloat16 [1024, 4096], P(None, 'seq'), may hold values from -0.1875 to 0.1875
- frame_ids: int32 [16, 2048], P('span'), may hold values from 0 to 15, never falling along the last dimension, each value on 1 to 256 neighbouring positions
- windows: int32 [16, 16, 2], P('span'), may hold values from 0 to 1024, as said below
- video_start: int32 [16], P('span'), may hold values from 0 to 1, as said below
Outputs:
- attended: bfloat16 [16, 2048, 4096], P('span', 'seq')
Inputs may be any that keep to these rules, and one draw needn't show every extreme that they name: windows[c, f] = (start, end) with 1 <= end - start <= 128; in every span frame 0's window is [0, 128) and the last frame's ends at 1024. video_start[0] = 1, and at least one of the spans 1 to 15 begins a new video.
All inputs are finite; a program needn't handle non-finite values.
Results may differ from a plain program's by a relative error of at most 0.0072.
Values may be sent and summed in bfloat16 or wider, within the bound.
A program may use at most 64 MiB of HBM per device.

v0:
```python
import jax
import jax.numpy as jnp
from jax import lax
from jax.sharding import PartitionSpec as P

HEADS = 32
HD = 128


def shifted(value, axis, steps):
    count = lax.axis_size(axis)
    leading, last = (max(0, -steps), min(count, count - steps))
    return lax.ppermute(value, axis, [(source, source + steps) for source in range(leading, last)])


def attend(query, key_rows, value_rows, allowed, scale):
    scores = jnp.einsum("qhd,khd->hqk", query, key_rows, preferred_element_type=jnp.float32) * scale
    scores = jnp.where(allowed[None, :, :], scores, -1e30)
    top = jnp.max(scores, axis=-1, keepdims=True)
    weights = jnp.exp(scores - top)
    den = jnp.sum(weights, axis=-1, keepdims=True)
    numer = jnp.einsum(
        "hqk,khd->qhd", weights.astype(jnp.bfloat16), value_rows, preferred_element_type=jnp.float32
    )
    return numer / jnp.transpose(den, (1, 0, 2))


def local(queries, keys, values, audio, audio_wk, audio_wv, frame_ids, windows, video_start):
    tok_rows = queries.shape[1]
    scale = HD ** (-0.5)
    q_local = queries.reshape(tok_rows, HEADS, HD)
    k_local = keys.reshape(tok_rows, HEADS, HD)
    v_local = values.reshape(tok_rows, HEADS, HD)
    prev_k, prev_v = shifted((k_local, v_local), "span", 1)
    q_heads, k_heads, v_heads, prev_kh, prev_vh = (
        lax.all_to_all(q_local, "seq", split_axis=1, concat_axis=0, tiled=True),
        lax.all_to_all(k_local, "seq", split_axis=1, concat_axis=0, tiled=True),
        lax.all_to_all(v_local, "seq", split_axis=1, concat_axis=0, tiled=True),
        lax.all_to_all(prev_k, "seq", split_axis=1, concat_axis=0, tiled=True),
        lax.all_to_all(prev_v, "seq", split_axis=1, concat_axis=0, tiled=True),
    )
    span_rows = q_heads.shape[0]
    head_count = q_heads.shape[1]
    joint_w = jnp.concatenate([audio_wk, audio_wv], axis=1)
    projected = jnp.dot(
        lax.all_gather(audio, "seq", axis=1, tiled=True)[0],
        joint_w,
        preferred_element_type=jnp.float32,
    ).astype(jnp.bfloat16)[None][0]
    aud_rows = projected.shape[0]
    audio_keys = projected[:, : head_count * HD].reshape(aud_rows, head_count, HD)
    audio_vals = projected[:, head_count * HD :].reshape(aud_rows, head_count, HD)
    has_prev = jnp.logical_and(lax.axis_index("span") > 0, video_start[0] == 0)
    frames = frame_ids[0]
    table = windows[0]
    onehot = frames[:, None] == jnp.arange(table.shape[0], dtype=jnp.int32)[None, :]
    lower = jnp.sum(jnp.where(onehot, table[None, :, 0], 0), axis=1)
    upper = jnp.sum(jnp.where(onehot, table[None, :, 1], 0), axis=1)
    all_keys = jnp.concatenate([prev_kh, k_heads], axis=0)
    all_vals = jnp.concatenate([prev_vh, v_heads], axis=0)
    positions = jnp.arange(aud_rows, dtype=jnp.int32)
    block = min(512, span_rows)

    def one_block(index):
        begin = index * block
        q_block = lax.dynamic_slice_in_dim(q_heads, begin, block, 0)
        f_block = lax.dynamic_slice_in_dim(frames, begin, block, 0)
        lo_block = lax.dynamic_slice_in_dim(lower, begin, block, 0)
        hi_block = lax.dynamic_slice_in_dim(upper, begin, block, 0)
        own = frames[None, :] <= f_block[:, None]
        before = jnp.broadcast_to(has_prev, (block, span_rows))
        self_mask = jnp.concatenate([before, own], axis=1)
        audio_mask = jnp.logical_and(
            positions[None, :] >= lo_block[:, None], positions[None, :] < hi_block[:, None]
        )
        self_out = attend(q_block, all_keys, all_vals, self_mask, scale)
        audio_out = attend(q_block, audio_keys, audio_vals, audio_mask, scale)
        return (self_out + audio_out).astype(jnp.bfloat16)

    blocks = lax.map(one_block, jnp.arange(span_rows // block, dtype=jnp.int32))
    mixed = blocks.reshape(span_rows, head_count, HD)
    back = lax.all_to_all(mixed, "seq", split_axis=0, concat_axis=1, tiled=True)
    return back.reshape(1, tok_rows, HEADS * HD)


def solution(mesh):
    placed = (
        P("span", "seq", None),
        P("span", "seq", None),
        P("span", "seq", None),
        P("span", "seq", None),
        P(None, "seq"),
        P(None, "seq"),
        P("span", None),
        P("span", None, None),
        P("span"),
    )
    return jax.shard_map(
        local, mesh=mesh, in_specs=placed, out_specs=P("span", "seq", None), check_vma=False
    )
```

profile of v0, /device:TPU:1, one launch (start us, length us, event | category | flops | bytes accessed | tf_op | source)
XLA Modules:
  0.0 304.1 jit_solution(1894020677160159355)
XLA Ops:
  6.5 2.3 copy.53
  8.9 6.9 %all-to-all-start = ((bf16[128,32,128]{0,2,1:T(8,128)(2,1)}), bf16[128,32,128]{0,2,1:T(8,128)(2,1)S(1)}, u32[]{:S(2)}, u32[]{:S(2)}) async-start(bf16[128,32,128]{0,2,1:T(8,128)(2,1)} %bitcast.2), calls=%async_computation | async-start | bytes 2097152 | tf_op jit(solution)/shard_map/all_to_all | solution.py:36
  15.8 1.3 copy.56
  17.1 14.4 %all-to-all-done = bf16[128,32,128]{0,2,1:T(8,128)(2,1)S(1)} async-done(((bf16[128,32,128]{0,2,1:T(8,128)(2,1)}), bf16[128,32,128]{0,2,1:T(8,128)(2,1)S(1)}, u32[]{:S(2)}, u32[]{:S(2)}) %all-to-all-start) | async-done | bytes 1048608 | tf_op jit(solution)/shard_map/all_to_all | solution.py:36
  31.5 4.4 %all-to-all-start.2 = ((bf16[128,32,128]{0,2,1:T(8,128)(2,1)}), bf16[128,32,128]{0,2,1:T(8,128)(2,1)S(1)}, u32[]{:S(2)}, u32[]{:S(2)}) async-start(bf16[128,32,128]{0,2,1:T(8,128)(2,1)} %bitcast.7), calls=%async_computation.2 | async-start | bytes 2097152 | tf_op jit(solution)/shard_map/all_to_all | solution.py:37
  36.6 2.3 copy.61
  38.9 4.5 %collective-permute-start.1 = (bf16[128,32,128]{0,2,1:T(8,128)(2,1)}, bf16[128,32,128]{0,2,1:T(8,128)(2,1)}, u32[]{:S(2)}, u32[]{:S(2)}) collective-permute-start(bf16[128,32,128]{0,2,1:T(8,128)(2,1)} %bitcast.16), channel_id=1, source_target_pairs={{0,16},{16,32},{32,48},{48,64},{64,80},{80,96},{96,112},{112,128},... | collective-permute-start | bytes 3145736 | tf_op jit(solution)/shard_map/ppermute | solution.py:13
  43.4 53.6 %all-to-all-done.2 = bf16[128,32,128]{0,2,1:T(8,128)(2,1)S(1)} async-done(((bf16[128,32,128]{0,2,1:T(8,128)(2,1)}), bf16[128,32,128]{0,2,1:T(8,128)(2,1)S(1)}, u32[]{:S(2)}, u32[]{:S(2)}) %all-to-all-start.2) | async-done | bytes 1048608 | tf_op jit(solution)/shard_map/all_to_all | solution.py:37
  97.0 5.5 %all-to-all-start.4 = ((bf16[128,32,128]{0,2,1:T(8,128)(2,1)}), bf16[128,32,128]{0,2,1:T(8,128)(2,1)S(1)}, u32[]{:S(2)}, u32[]{:S(2)}) async-start(bf16[128,32,128]{0,2,1:T(8,128)(2,1)} %bitcast.16), calls=%async_computation.4 | async-start | bytes 2097152 | tf_op jit(solution)/shard_map/all_to_all | solution.py:38
  102.5 2.3 collective-permute-start
  104.8 16.9 %all-to-all-done.4 = bf16[128,32,128]{0,2,1:T(8,128)(2,1)S(1)} async-done(((bf16[128,32,128]{0,2,1:T(8,128)(2,1)}), bf16[128,32,128]{0,2,1:T(8,128)(2,1)S(1)}, u32[]{:S(2)}, u32[]{:S(2)}) %all-to-all-start.4) | async-done | bytes 1048608 | tf_op jit(solution)/shard_map/all_to_all | solution.py:38
  121.7 4.9 %all-to-all-start.3 = ((bf16[128,32,128]{0,2,1:T(8,128)(2,1)}), bf16[128,32,128]{0,2,1:T(8,128)(2,1)}, u32[]{:S(2)}, u32[]{:S(2)}) async-start(bf16[128,32,128]{0,2,1:T(8,128)(2,1)} %collective-permute-done.1), calls=%async_computation.3 | async-start | bytes 2097152 | tf_op jit(solution)/shard_map/all_to_all | solution.py:40
  126.7 15.8 %all-to-all-done.3 = bf16[128,32,128]{0,2,1:T(8,128)(2,1)} async-done(((bf16[128,32,128]{0,2,1:T(8,128)(2,1)}), bf16[128,32,128]{0,2,1:T(8,128)(2,1)}, u32[]{:S(2)}, u32[]{:S(2)}) %all-to-all-start.3) | async-done | bytes 1048608 | tf_op jit(solution)/shard_map/all_to_all | solution.py:40
  142.5 5.0 %all-to-all-start.1 = ((bf16[128,32,128]{0,2,1:T(8,128)(2,1)}), bf16[128,32,128]{0,2,1:T(8,128)(2,1)}, u32[]{:S(2)}, u32[]{:S(2)}) async-start(bf16[128,32,128]{0,2,1:T(8,128)(2,1)} %collective-permute-done), calls=%async_computation.1 | async-start | bytes 2097152 | tf_op jit(solution)/shard_map/all_to_all | solution.py:39
  149.7 1.6 copy.65
  151.4 2.3 copy.63
  153.6 9.8 %all-to-all-done.1 = bf16[128,32,128]{0,2,1:T(8,128)(2,1)} async-done(((bf16[128,32,128]{0,2,1:T(8,128)(2,1)}), bf16[128,32,128]{0,2,1:T(8,128)(2,1)}, u32[]{:S(2)}, u32[]{:S(2)}) %all-to-all-start.1) | async-done | bytes 1048608 | tf_op jit(solution)/shard_map/all_to_all | solution.py:39
  163.4 2.3 copy.58
  165.7 3.9 %pad_maximum_fusion = (bf16[4096,2,128]{2,0,1:T(8,128)(2,1)}, bf16[4096,2,128]{2,0,1:T(8,128)(2,1)}) fusion(bf16[2048,2,128]{2,0,1:T(8,128)(2,1)S(1)} %bitcast.112, bf16[2048,2,128]{2,0,1:T(8,128)(2,1)} %bitcast.115, bf16[2048,2,128]{2,0,1:T(8,128)(2,1)S(1)} %bitcast.113, bf16[2048,2,128]{2,0,1:T(8,128)(2,1)} %bitcast.114), kind=kLoop, calls=%fused_computation.37 | loop fusion | flops 8388608 | bytes 8388608 | tf_op jit(solution)/shard_map/concatenate | solution.py:59
  169.6 3.2 %fusion.54 = bf16[1024,512]{0,1:T(8,128)(2,1)S(1)} fusion(bf16[1,1024,1024]{2,1,0:T(8,128)(2,1)} %all-gather.2.cloned.1.call-done, bf16[1024,256]{1,0:T(8,128)(2,1)} %param.16, bf16[1024,256]{1,0:T(8,128)(2,1)} %param.15), kind=kOutput, calls=%fused_computation.42 | convolution fusion | flops 1076363264 | bytes 4194304 | tf_op jit(solution)/shard_map/dot_general | solution.py:45
  174.2 93.2 %while.12 = (s32[]{:T(128)}, bf16[4,512,2,128]{3,1,0,2:T(8,128)(2,1)S(1)}, s32[1,2048]{1,0:T(1,128)S(1)}, s32[4]{0:T(128)S(1)}, s32[2048]{0:T(1024)S(1)}, /*inde...) while((s32[]{:T(128)}, ...), condition=%wide.region_7.8_spmd.clone.clone, body=%wide.region_2.7_spmd.clone.clone.sunk | while | flops 2745167872 | bytes 95226192 | solution.py:80
  177.8 1.1 fusion.86
  178.9 1.2 fusion.87
  180.1 1.9 fusion.88
  182.1 5.3 %fusion.89 = (f32[2,512]{1,0:T(2,128)S(1)}, f32[2,512,4096]{2,1,0:T(8,128)S(1)}) fusion(pred[512,4096]{1,0:T(8,128)(4,1)S(1)} %concatenate.18, bf16[4096,2,128]{2,0,1:T(8,128)(2,1)} %get-tuple-element.372, bf16[2048,2,128]{2,0,1:T(8,128)(2,1)S(1)} %get-tuple-element.371, s32[]{:T(128)S(6)} %select_n.80), kind=kOutput, calls=%fused_computation.3.clone.1 | convolution fusion | flops 1086323712 | bytes 21237764 | tf_op jit(solution)/shard_map/while/body/eval_jaxpr/qhd,khd->hqk/dot_general | solution.py:17
  187.4 4.6 %fusion.90 = f32[2,512]{1,0:T(2,128)S(1)} fusion(f32[2,512,4096]{2,1,0:T(8,128)S(1)} %get-tuple-element.329, f32[2,512]{1,0:T(2,128)S(1)} %get-tuple-element.330, pred[512,4096]{1,0:T(8,128)(4,1)S(1)} %concatenate.18), kind=kLoop, calls=%fused_computation.4.clone.1 | loop fusion | flops 16776192 | bytes 18882560 | tf_op jit(solution)/shard_map/while/body/eval_jaxpr/reduce_sum | solution.py:21
  192.1 5.6 %fusion.91 = bf16[4,512,2,128]{3,1,0,2:T(8,128)(2,1)S(1)} fusion(bf16[4,512,2,128]{3,1,0,2:T(8,128)(2,1)S(1)} %get-tuple-element.349, s32[]{:T(128)S(6)} %copy.83, f32[512,2,128]{2,0,1:T(8,128)S(1)} %copy-done.7, bf16[4096,2,128]{2,0,1:T(8,128)(2,1)S(1)} %copy-done.1, f32[2,512,4096]{2,1,0:T(8,128)S(1)} %get-tuple-element.329, ...), kind=kOutput, calls=%fused_computation.25.clone.1 | convolution fusion | flops 1090912256 | bytes 21766148 | tf_op jit(solution)/shard_map/while/body/eval_jaxpr/hqk,khd->qhd/dot_general | solution.py:22
  201.1 1.1 fusion.86
  202.1 1.2 fusion.87
  203.4 1.9 fusion.88
  205.3 5.3 %fusion.89 = (f32[2,512]{1,0:T(2,128)S(1)}, f32[2,512,4096]{2,1,0:T(8,128)S(1)}) fusion(pred[512,4096]{1,0:T(8,128)(4,1)S(1)} %concatenate.18, bf16[4096,2,128]{2,0,1:T(8,128)(2,1)} %get-tuple-element.372, bf16[2048,2,128]{2,0,1:T(8,128)(2,1)S(1)} %get-tuple-element.371, s32[]{:T(128)S(6)} %select_n.80), kind=kOutput, calls=%fused_computation.3.clone.1 | convolution fusion | flops 1086323712 | bytes 21237764 | tf_op jit(solution)/shard_map/while/body/eval_jaxpr/qhd,khd->hqk/dot_general | solution.py:17
  210.7 4.6 %fusion.90 = f32[2,512]{1,0:T(2,128)S(1)} fusion(f32[2,512,4096]{2,1,0:T(8,128)S(1)} %get-tuple-element.329, f32[2,512]{1,0:T(2,128)S(1)} %get-tuple-element.330, pred[512,4096]{1,0:T(8,128)(4,1)S(1)} %concatenate.18), kind=kLoop, calls=%fused_computation.4.clone.1 | loop fusion | flops 16776192 | bytes 18882560 | tf_op jit(solution)/shard_map/while/body/eval_jaxpr/reduce_sum | solution.py:21
  215.3 5.6 %fusion.91 = bf16[4,512,2,128]{3,1,0,2:T(8,128)(2,1)S(1)} fusion(bf16[4,512,2,128]{3,1,0,2:T(8,128)(2,1)S(1)} %get-tuple-element.349, s32[]{:T(128)S(6)} %copy.83, f32[512,2,128]{2,0,1:T(8,128)S(1)} %copy-done.7, bf16[4096,2,128]{2,0,1:T(8,128)(2,1)S(1)} %copy-done.1, f32[2,512,4096]{2,1,0:T(8,128)S(1)} %get-tuple-element.329, ...), kind=kOutput, calls=%fused_computation.25.clone.1 | convolution fusion | flops 1090912256 | bytes 21766148 | tf_op jit(solution)/shard_map/while/body/eval_jaxpr/hqk,khd->qhd/dot_general | solution.py:22
  224.3 1.1 fusion.86
  225.4 1.2 fusion.87
  226.6 1.9 fusion.88
  228.6 5.3 %fusion.89 = (f32[2,512]{1,0:T(2,128)S(1)}, f32[2,512,4096]{2,1,0:T(8,128)S(1)}) fusion(pred[512,4096]{1,0:T(8,128)(4,1)S(1)} %concatenate.18, bf16[4096,2,128]{2,0,1:T(8,128)(2,1)} %get-tuple-element.372, bf16[2048,2,128]{2,0,1:T(8,128)(2,1)S(1)} %get-tuple-element.371, s32[]{:T(128)S(6)} %select_n.80), kind=kOutput, calls=%fused_computation.3.clone.1 | convolution fusion | flops 1086323712 | bytes 21237764 | tf_op jit(solution)/shard_map/while/body/eval_jaxpr/qhd,khd->hqk/dot_general | solution.py:17
  233.9 4.6 %fusion.90 = f32[2,512]{1,0:T(2,128)S(1)} fusion(f32[2,512,4096]{2,1,0:T(8,128)S(1)} %get-tuple-element.329, f32[2,512]{1,0:T(2,128)S(1)} %get-tuple-element.330, pred[512,4096]{1,0:T(8,128)(4,1)S(1)} %concatenate.18), kind=kLoop, calls=%fused_computation.4.clone.1 | loop fusion | flops 16776192 | bytes 18882560 | tf_op jit(solution)/shard_map/while/body/eval_jaxpr/reduce_sum | solution.py:21
  238.6 5.6 %fusion.91 = bf16[4,512,2,128]{3,1,0,2:T(8,128)(2,1)S(1)} fusion(bf16[4,512,2,128]{3,1,0,2:T(8,128)(2,1)S(1)} %get-tuple-element.349, s32[]{:T(128)S(6)} %copy.83, f32[512,2,128]{2,0,1:T(8,128)S(1)} %copy-done.7, bf16[4096,2,128]{2,0,1:T(8,128)(2,1)S(1)} %copy-done.1, f32[2,512,4096]{2,1,0:T(8,128)S(1)} %get-tuple-element.329, ...), kind=kOutput, calls=%fused_computation.25.clone.1 | convolution fusion | flops 1090912256 | bytes 21766148 | tf_op jit(solution)/shard_map/while/body/eval_jaxpr/hqk,khd->qhd/dot_general | solution.py:22
  247.6 1.1 fusion.86
  248.7 1.2 fusion.87
  249.9 1.9 fusion.88
  251.8 5.3 %fusion.89 = (f32[2,512]{1,0:T(2,128)S(1)}, f32[2,512,4096]{2,1,0:T(8,128)S(1)}) fusion(pred[512,4096]{1,0:T(8,128)(4,1)S(1)} %concatenate.18, bf16[4096,2,128]{2,0,1:T(8,128)(2,1)} %get-tuple-element.372, bf16[2048,2,128]{2,0,1:T(8,128)(2,1)S(1)} %get-tuple-element.371, s32[]{:T(128)S(6)} %select_n.80), kind=kOutput, calls=%fused_computation.3.clone.1 | convolution fusion | flops 1086323712 | bytes 21237764 | tf_op jit(solution)/shard_map/while/body/eval_jaxpr/qhd,khd->hqk/dot_general | solution.py:17
  257.2 4.6 %fusion.90 = f32[2,512]{1,0:T(2,128)S(1)} fusion(f32[2,512,4096]{2,1,0:T(8,128)S(1)} %get-tuple-element.329, f32[2,512]{1,0:T(2,128)S(1)} %get-tuple-element.330, pred[512,4096]{1,0:T(8,128)(4,1)S(1)} %concatenate.18), kind=kLoop, calls=%fused_computation.4.clone.1 | loop fusion | flops 16776192 | bytes 18882560 | tf_op jit(solution)/shard_map/while/body/eval_jaxpr/reduce_sum | solution.py:21
  261.9 5.6 %fusion.91 = bf16[4,512,2,128]{3,1,0,2:T(8,128)(2,1)S(1)} fusion(bf16[4,512,2,128]{3,1,0,2:T(8,128)(2,1)S(1)} %get-tuple-element.349, s32[]{:T(128)S(6)} %copy.83, f32[512,2,128]{2,0,1:T(8,128)S(1)} %copy-done.7, bf16[4096,2,128]{2,0,1:T(8,128)(2,1)S(1)} %copy-done.1, f32[2,512,4096]{2,1,0:T(8,128)S(1)} %get-tuple-element.329, ...), kind=kOutput, calls=%fused_computation.25.clone.1 | convolution fusion | flops 1090912256 | bytes 21766148 | tf_op jit(solution)/shard_map/while/body/eval_jaxpr/hqk,khd->qhd/dot_general | solution.py:22
  267.5 8.9 %copy.69 = bf16[2048,2,128]{2,1,0:T(2,128)(2,1)S(1)} copy(bf16[2048,2,128]{2,0,1:T(8,128)(2,1)S(1)} %bitcast.118) | data formatting | bytes 2097152 | tf_op jit(solution)/shard_map/reshape | solution.py:81
  276.4 18.8 %all_to_all.105 = bf16[2048,2,128]{2,1,0:T(2,128)(2,1)S(1)} all-to-all(bf16[2048,2,128]{2,1,0:T(2,128)(2,1)S(1)} %copy.69), channel_id=1, replica_groups=mesh['span'=16,'seq'=16] {'seq'}, dimensions={0} | all-to-all | bytes 2097152 | tf_op jit(solution)/shard_map/all_to_all | solution.py:82
  295.9 1.3 copy.72
  (78 shorter events, 15.3 us)
Async XLA Ops:
  6.5 9.3 %copy-start.2 = (bf16[1,128,4096]{2,1,0:T(8,128)(2,1)S(1)}, bf16[1,128,4096]{2,1,0:T(8,128)(2,1)}, u32[]{:S(2)}) copy-start(bf16[1,128,4096]{2,1,0:T(8,128)(2,1)} %param.12) | copy-start | bytes 3145732
  8.9 22.6 %all-to-all-start = ((bf16[128,32,128]{0,2,1:T(8,128)(2,1)}), bf16[128,32,128]{0,2,1:T(8,128)(2,1)S(1)}, u32[]{:S(2)}, u32[]{:S(2)}) async-start(bf16[128,32,128]{0,2,1:T(8,128)(2,1)} %bitcast.2), calls=%async_computation | async-start | bytes 2097152 | tf_op jit(solution)/shard_map/all_to_all | solution.py:36
  31.5 65.5 %all-to-all-start.2 = ((bf16[128,32,128]{0,2,1:T(8,128)(2,1)}), bf16[128,32,128]{0,2,1:T(8,128)(2,1)S(1)}, u32[]{:S(2)}, u32[]{:S(2)}) async-start(bf16[128,32,128]{0,2,1:T(8,128)(2,1)} %bitcast.7), calls=%async_computation.2 | async-start | bytes 2097152 | tf_op jit(solution)/shard_map/all_to_all | solution.py:37
  35.9 133.7 %all-gather.2.cloned.1.call-start = ((), (), s32[]{:S(2)}) async-start(), calls=%async_computation.6 | async-start | bytes 2228224 | tf_op jit(solution)/shard_map/all_gather | solution.py:46
  36.6 111.6 %copy-start.6 = (s32[1,16,2]{1,2,0:T(2,128)S(1)}, s32[1,16,2]{1,2,0:T(2,128)}, u32[]{:S(2)}) copy-start(s32[1,16,2]{1,2,0:T(2,128)} %param.18) | copy-start | bytes 388
  36.6 111.6 %copy-start.5 = (s32[1,2048]{1,0:T(1,128)S(1)}, s32[1,2048]{1,0:T(1,128)}, u32[]{:S(2)}) copy-start(s32[1,2048]{1,0:T(1,128)} %param.17) | copy-start | bytes 24580
  38.9 82.8 %collective-permute-start.1 = (bf16[128,32,128]{0,2,1:T(8,128)(2,1)}, bf16[128,32,128]{0,2,1:T(8,128)(2,1)}, u32[]{:S(2)}, u32[]{:S(2)}) collective-permute-start(bf16[128,32,128]{0,2,1:T(8,128)(2,1)} %bitcast.16), channel_id=1, source_target_pairs={{0,16},{16,32},{32,48},{48,64},{64,80},{80,96},{96,112},{112,128},... | collective-permute-start | bytes 3145736 | tf_op jit(solution)/shard_map/ppermute | solution.py:13
  97.0 24.7 %all-to-all-start.4 = ((bf16[128,32,128]{0,2,1:T(8,128)(2,1)}), bf16[128,32,128]{0,2,1:T(8,128)(2,1)S(1)}, u32[]{:S(2)}, u32[]{:S(2)}) async-start(bf16[128,32,128]{0,2,1:T(8,128)(2,1)} %bitcast.16), calls=%async_computation.4 | async-start | bytes 2097152 | tf_op jit(solution)/shard_map/all_to_all | solution.py:38
  102.5 24.1 %collective-permute-start = (bf16[128,32,128]{0,2,1:T(8,128)(2,1)}, bf16[128,32,128]{0,2,1:T(8,128)(2,1)}, u32[]{:S(2)}, u32[]{:S(2)}) collective-permute-start(bf16[128,32,128]{0,2,1:T(8,128)(2,1)} %bitcast.7), channel_id=1, source_target_pairs={{0,16},{16,32},{32,48},{48,64},{64,80},{80,96},{96,112},{112,128},... | collective-permute-start | bytes 3145736 | tf_op jit(solution)/shard_map/ppermute | solution.py:13
  121.7 26.7 %copy-start = (bf16[128,32,128]{0,2,1:T(8,128)(2,1)}, bf16[128,32,128]{0,2,1:T(8,128)(2,1)S(1)}, u32[]{:S(2)}) copy-start(bf16[128,32,128]{0,2,1:T(8,128)(2,1)S(1)} %all-to-all-done.4) | copy-start | bytes 3145732
  121.7 20.8 %all-to-all-start.3 = ((bf16[128,32,128]{0,2,1:T(8,128)(2,1)}), bf16[128,32,128]{0,2,1:T(8,128)(2,1)}, u32[]{:S(2)}, u32[]{:S(2)}) async-start(bf16[128,32,128]{0,2,1:T(8,128)(2,1)} %collective-permute-done.1), calls=%async_computation.3 | async-start | bytes 2097152 | tf_op jit(solution)/shard_map/all_to_all | solution.py:40
  142.5 20.9 %all-to-all-start.1 = ((bf16[128,32,128]{0,2,1:T(8,128)(2,1)}), bf16[128,32,128]{0,2,1:T(8,128)(2,1)}, u32[]{:S(2)}, u32[]{:S(2)}) async-start(bf16[128,32,128]{0,2,1:T(8,128)(2,1)} %collective-permute-done), calls=%async_computation.1 | async-start | bytes 2097152 | tf_op jit(solution)/shard_map/all_to_all | solution.py:39
  172.8 1.4 copy-start.3
  177.8 2.3 copy-start.4
  187.4 4.7 %copy-start.1 = (bf16[4096,2,128]{2,0,1:T(8,128)(2,1)S(1)}, bf16[4096,2,128]{2,0,1:T(8,128)(2,1)}, u32[]{:S(2)}) copy-start(bf16[4096,2,128]{2,0,1:T(8,128)(2,1)} %get-tuple-element.373) | copy-start | bytes 6291460 | tf_op jit(solution)/shard_map/while
  187.4 4.7 %copy-start.7 = (f32[512,2,128]{2,0,1:T(8,128)S(1)}, f32[512,2,128]{2,0,1:T(8,128)}, u32[]{:S(2)}) copy-start(f32[512,2,128]{2,0,1:T(8,128)} %fusion.88) | copy-start | bytes 1572868 | tf_op jit(solution)/shard_map/while
  201.1 2.3 copy-start.4
  210.7 4.7 %copy-start.1 = (bf16[4096,2,128]{2,0,1:T(8,128)(2,1)S(1)}, bf16[4096,2,128]{2,0,1:T(8,128)(2,1)}, u32[]{:S(2)}) copy-start(bf16[4096,2,128]{2,0,1:T(8,128)(2,1)} %get-tuple-element.373) | copy-start | bytes 6291460 | tf_op jit(solution)/shard_map/while
  210.7 4.7 %copy-start.7 = (f32[512,2,128]{2,0,1:T(8,128)S(1)}, f32[512,2,128]{2,0,1:T(8,128)}, u32[]{:S(2)}) copy-start(f32[512,2,128]{2,0,1:T(8,128)} %fusion.88) | copy-start | bytes 1572868 | tf_op jit(solution)/shard_map/while
  224.3 2.3 copy-start.4
  233.9 4.7 %copy-start.1 = (bf16[4096,2,128]{2,0,1:T(8,128)(2,1)S(1)}, bf16[4096,2,128]{2,0,1:T(8,128)(2,1)}, u32[]{:S(2)}) copy-start(bf16[4096,2,128]{2,0,1:T(8,128)(2,1)} %get-tuple-element.373) | copy-start | bytes 6291460 | tf_op jit(solution)/shard_map/while
  233.9 4.7 %copy-start.7 = (f32[512,2,128]{2,0,1:T(8,128)S(1)}, f32[512,2,128]{2,0,1:T(8,128)}, u32[]{:S(2)}) copy-start(f32[512,2,128]{2,0,1:T(8,128)} %fusion.88) | copy-start | bytes 1572868 | tf_op jit(solution)/shard_map/while
  247.6 2.3 copy-start.4
  257.2 4.7 %copy-start.1 = (bf16[4096,2,128]{2,0,1:T(8,128)(2,1)S(1)}, bf16[4096,2,128]{2,0,1:T(8,128)(2,1)}, u32[]{:S(2)}) copy-start(bf16[4096,2,128]{2,0,1:T(8,128)(2,1)} %get-tuple-element.373) | copy-start | bytes 6291460 | tf_op jit(solution)/shard_map/while
  257.2 4.7 %copy-start.7 = (f32[512,2,128]{2,0,1:T(8,128)S(1)}, f32[512,2,128]{2,0,1:T(8,128)}, u32[]{:S(2)}) copy-start(f32[512,2,128]{2,0,1:T(8,128)} %fusion.88) | copy-start | bytes 1572868 | tf_op jit(solution)/shard_map/while
Sparse Core Ops, SparseCore 0:
  38.5 86.6 all-gather.1
where the time goes:
time: 305 us; the launch traced here: 304 us
  waiting for transfers between devices  111 us (36%)
  matrix products  58.8 us (19%)
  starting transfers between devices  33.6 us (11%)
  other arithmetic  32.5 us (11%)
  local copies, waits for them, and re-layouts  31.8 us (10%)
  blocking collectives  18.8 us (6%)
  between operations  14.2 us (5%)
  loops' own time  3.2 us (1%)
    all_to_all x1, waiting for transfers between devices, local(): lax.all_to_all(k_local, 'seq', split_axis=1, concat_axis=0, tiled=True)  53.6 us
    dot_general x8, matrix products, attend(): jnp.einsum('hqk,khd->qhd', weights.astype(jnp.bfloat16), value_rows, pref...  30 us
    dot_general x8, matrix products, attend(): jnp.einsum('qhd,khd->hqk', query, key_rows, preferred_element_type=jnp.fl...  25.6 us
    reduce_sum x8, other arithmetic, attend(): den = jnp.sum(weights, axis=-1, keepdims=True)  23.5 us
    all_to_all x1, blocking collectives, local(): back = lax.all_to_all(mixed, 'seq', split_axis=0, concat_axis=1, tiled=True)  18.8 us
    all_to_all x1, waiting for transfers between devices, local(): lax.all_to_all(v_local, 'seq', split_axis=1, concat_axis=0, tiled=True)  16.9 us
    all_to_all x1, waiting for transfers between devices, local(): lax.all_to_all(prev_v, 'seq', split_axis=1, concat_axis=0, tiled=True)  15.8 us
    all_to_all x1, waiting for transfers between devices, local(): lax.all_to_all(q_local, 'seq', split_axis=1, concat_axis=0, tiled=True)  14.4 us
  transfers between devices with their start and end apart: 8, of which 5 were waited for; matrix products, arithmetic and copies ran while one was open for 5% of the time, Pallas kernels for 0%

commit v1 on v0

--- a/solution.py
+++ b/solution.py
@@ -31,14 +31,12 @@
     q_local = queries.reshape(tok_rows, HEADS, HD)
     k_local = keys.reshape(tok_rows, HEADS, HD)
     v_local = values.reshape(tok_rows, HEADS, HD)
-    prev_k, prev_v = shifted((k_local, v_local), "span", 1)
-    q_heads, k_heads, v_heads, prev_kh, prev_vh = (
-        lax.all_to_all(q_local, "seq", split_axis=1, concat_axis=0, tiled=True),
+    k_heads, v_heads, q_heads = (
         lax.all_to_all(k_local, "seq", split_axis=1, concat_axis=0, tiled=True),
         lax.all_to_all(v_local, "seq", split_axis=1, concat_axis=0, tiled=True),
-        lax.all_to_all(prev_k, "seq", split_axis=1, concat_axis=0, tiled=True),
-        lax.all_to_all(prev_v, "seq", split_axis=1, concat_axis=0, tiled=True),
+        lax.all_to_all(q_local, "seq", split_axis=1, concat_axis=0, tiled=True),
     )
+    prev_kh, prev_vh = shifted((k_heads, v_heads), "span", 1)
     span_rows = q_heads.shape[0]
     head_count = q_heads.shape[1]
     joint_w = jnp.concatenate([audio_wk, audio_wv], axis=1)

time: 305 us -> 274 us (0.90)
  waiting for transfers between devices: 111 us -> 92.1 us
  starting transfers between devices: 33.6 us -> 22.6 us
  local copies, waits for them, and re-layouts: 31.8 us -> 26.6 us
    all_to_all x2 -> x0, waiting for transfers between devices: 25.6 us -> none  [the longest x1 15.8 us: local(): lax.all_to_all(prev_v, 'seq', split_axis=1, concat_axis=0, tiled=True)]
    all_to_all x2 -> x0, starting transfers between devices: 9.97 us -> none  [the longest x1 5.04 us: local(): lax.all_to_all(prev_k, 'seq', split_axis=1, concat_axis=0, tiled=True)]
    all_to_all x1, waiting for transfers between devices: 53.6 us -> 60.5 us  [local(): lax.all_to_all(k_local, 'seq', split_axis=1, concat_axis=0, tiled=True)]
    ppermute x2, waiting for transfers between devices: 0.04 us -> 5.92 us  [shifted(): lax.ppermute(value, axis, [(source, source + steps) for source in range(l...]
    all_to_all x2 -> x0, local copies, waits for them, and re-layouts: 4.6 us -> none  [the longest x1 2.32 us: local(): lax.all_to_all(prev_k, 'seq', split_axis=1, concat_axis=0, tiled=True)]
    all_to_all x1, waiting for transfers between devices: 16.9 us -> 13.6 us  [local(): lax.all_to_all(v_local, 'seq', split_axis=1, concat_axis=0, tiled=True)]
    concatenate x0 -> x1, other arithmetic: none -> 3.11 us  [local(): all_vals = jnp.concatenate([prev_vh, v_heads], axis=0)]
    unnamed x15 -> x17, local copies, waits for them, and re-layouts: 7.23 us -> 6.26 us
  transfers between devices with their start and end apart: 8 -> 6, of which waited for: 5 -> 4; matrix products, arithmetic and copies ran while one was open for 5% -> 4% of each run, Pallas kernels for 0% -> 0%
where the time goes in v1:
time: 274 us; the launch traced here: 273 us
  waiting for transfers between devices  92.1 us (34%)
  matrix products  58.6 us (21%)
  other arithmetic  34.7 us (13%)
  local copies, waits for them, and re-layouts  26.6 us (10%)
  starting transfers between devices  22.6 us (8%)
  blocking collectives  21.3 us (8%)
  between operations  14.2 us (5%)
  loops' own time  2.92 us (1%)
    all_to_all x1, waiting for transfers between devices, local(): lax.all_to_all(k_local, 'seq', split_axis=1, concat_axis=0, tiled=True)  60.5 us
    dot_general x8, matrix products, attend(): jnp.einsum('hqk,khd->qhd', weights.astype(jnp.bfloat16), value_rows, pref...  30.1 us
    dot_general x8, matrix products, attend(): jnp.einsum('qhd,khd->hqk', query, key_rows, preferred_element_type=jnp.fl...  25.6 us
    reduce_sum x8, other arithmetic, attend(): den = jnp.sum(weights, axis=-1, keepdims=True)  23.5 us
    all_to_all x1, blocking collectives, local(): back = lax.all_to_all(mixed, 'seq', split_axis=0, concat_axis=1, tiled=True)  21.3 us
    all_to_all x1, waiting for transfers between devices, local(): lax.all_to_all(v_local, 'seq', split_axis=1, concat_axis=0, tiled=True)  13.6 us
    all_to_all x1, waiting for transfers between devices, local(): lax.all_to_all(q_local, 'seq', split_axis=1, concat_axis=0, tiled=True)  11.3 us
    reshape x1, local copies, waits for them, and re-layouts, local(): mixed = blocks.reshape(span_rows, head_count, HD)  8.9 us
  transfers between devices with their start and end apart: 6, of which 4 were waited for; matrix products, arithmetic and copies ran while one was open for 4% of the time, Pallas kernels for 0%

profile of v1, /device:TPU:1, one launch (start us, length us, event | category | flops | bytes accessed | tf_op | source)
XLA Modules:
  0.0 272.9 jit_solution(15263762931029204514)
XLA Ops:
  6.5 2.3 copy.51
  8.9 7.0 %all-to-all-start.2 = ((bf16[128,32,128]{0,2,1:T(8,128)(2,1)}), bf16[128,32,128]{0,2,1:T(8,128)(2,1)S(1)}, u32[]{:S(2)}, u32[]{:S(2)}) async-start(bf16[128,32,128]{0,2,1:T(8,128)(2,1)} %bitcast.12), calls=%async_computation.2 | async-start | bytes 2097152 | tf_op jit(solution)/shard_map/all_to_all | solution.py:36
  16.0 0.7 all-gather.2.cloned.1.call-update
  16.7 1.3 copy.48
  18.0 13.6 %all-to-all-done.2 = bf16[128,32,128]{0,2,1:T(8,128)(2,1)S(1)} async-done(((bf16[128,32,128]{0,2,1:T(8,128)(2,1)}), bf16[128,32,128]{0,2,1:T(8,128)(2,1)S(1)}, u32[]{:S(2)}, u32[]{:S(2)}) %all-to-all-start.2) | async-done | bytes 1048608 | tf_op jit(solution)/shard_map/all_to_all | solution.py:36
  31.6 4.4 %all-to-all-start.1 = ((bf16[128,32,128]{0,2,1:T(8,128)(2,1)}), bf16[128,32,128]{0,2,1:T(8,128)(2,1)S(1)}, u32[]{:S(2)}, u32[]{:S(2)}) async-start(bf16[128,32,128]{0,2,1:T(8,128)(2,1)} %bitcast.7), calls=%async_computation.1 | async-start | bytes 2097152 | tf_op jit(solution)/shard_map/all_to_all | solution.py:35
  36.0 1.3 copy.53
  37.3 4.5 %collective-permute-start.1 = (bf16[2048,2,128]{2,0,1:T(8,128)(2,1)}, bf16[2048,2,128]{2,0,1:T(8,128)(2,1)}, u32[]{:S(2)}, u32[]{:S(2)}) collective-permute-start(bf16[2048,2,128]{2,0,1:T(8,128)(2,1)} %bitcast.16), channel_id=1, source_target_pairs={{0,16},{16,32},{32,48},{48,64},{64,80},{80,96},{96,112},{112,128},... | collective-permute-start | bytes 3145736 | tf_op jit(solution)/shard_map/ppermute | solution.py:13
  41.9 1.3 copy.45
  43.2 60.5 %all-to-all-done.1 = bf16[128,32,128]{0,2,1:T(8,128)(2,1)S(1)} async-done(((bf16[128,32,128]{0,2,1:T(8,128)(2,1)}), bf16[128,32,128]{0,2,1:T(8,128)(2,1)S(1)}, u32[]{:S(2)}, u32[]{:S(2)}) %all-to-all-start.1) | async-done | bytes 1048608 | tf_op jit(solution)/shard_map/all_to_all | solution.py:35
  103.7 4.3 %all-to-all-start = ((bf16[128,32,128]{0,2,1:T(8,128)(2,1)}), bf16[128,32,128]{0,2,1:T(8,128)(2,1)S(1)}, u32[]{:S(2)}, u32[]{:S(2)}) async-start(bf16[128,32,128]{0,2,1:T(8,128)(2,1)} %bitcast.2), calls=%async_computation | async-start | bytes 2097152 | tf_op jit(solution)/shard_map/all_to_all | solution.py:37
  108.0 1.3 copy.50
  109.3 2.3 collective-permute-start
  112.4 11.3 %all-to-all-done = bf16[128,32,128]{0,2,1:T(8,128)(2,1)S(1)} async-done(((bf16[128,32,128]{0,2,1:T(8,128)(2,1)}), bf16[128,32,128]{0,2,1:T(8,128)(2,1)S(1)}, u32[]{:S(2)}, u32[]{:S(2)}) %all-to-all-start) | async-done | bytes 1048608 | tf_op jit(solution)/shard_map/all_to_all | solution.py:37
  124.5 3.1 %pad_maximum_fusion.1 = bf16[4096,2,128]{2,0,1:T(8,128)(2,1)} fusion(bf16[2048,2,128]{2,0,1:T(8,128)(2,1)} %bitcast.16, bf16[2048,2,128]{2,0,1:T(8,128)(2,1)} %collective-permute-done.1), kind=kLoop, calls=%fused_computation.38 | loop fusion | flops 4194304 | bytes 4194304 | tf_op jit(solution)/shard_map/concatenate | solution.py:58
  127.6 5.9 %collective-permute-done = bf16[2048,2,128]{2,0,1:T(8,128)(2,1)} collective-permute-done((bf16[2048,2,128]{2,0,1:T(8,128)(2,1)}, bf16[2048,2,128]{2,0,1:T(8,128)(2,1)}, u32[]{:S(2)}, u32[]{:S(2)}) %collective-permute-start) | collective-permute-done | bytes 1048608 | tf_op jit(solution)/shard_map/ppermute | solution.py:13
  133.5 3.0 %pad_maximum_fusion = bf16[4096,2,128]{2,0,1:T(8,128)(2,1)} fusion(bf16[2048,2,128]{2,0,1:T(8,128)(2,1)} %bitcast.11, bf16[2048,2,128]{2,0,1:T(8,128)(2,1)} %collective-permute-done), kind=kLoop, calls=%fused_computation.37 | loop fusion | flops 4194304 | bytes 4194304 | tf_op jit(solution)/shard_map/concatenate | solution.py:57
  136.5 2.9 %fusion.54 = bf16[1024,512]{0,1:T(8,128)(2,1)S(1)} fusion(bf16[1,1024,1024]{2,1,0:T(8,128)(2,1)} %all-gather.2.cloned.1.call-done, bf16[1024,256]{1,0:T(8,128)(2,1)S(1)} %copy-done.6, bf16[1024,256]{1,0:T(8,128)(2,1)S(1)} %copy-done.7), kind=kOutput, calls=%fused_computation.42 | convolution fusion | flops 1076363264 | bytes 4194304 | tf_op jit(solution)/shard_map/dot_general | solution.py:43
  139.4 1.0 copy.55
  140.7 93.0 %while.12 = (s32[]{:T(128)}, bf16[4,512,2,128]{3,1,0,2:T(8,128)(2,1)S(1)}, s32[1,2048]{1,0:T(1,128)S(1)}, s32[4]{0:T(128)S(1)}, s32[2048]{0:T(1024)S(1)}, /*inde...) while((s32[]{:T(128)}, ...), condition=%wide.region_7.8_spmd.clone.clone, body=%wide.region_2.7_spmd.clone.clone.sunk | while | flops 2745167872 | bytes 95226192 | solution.py:78
  144.1 1.1 fusion.86
  145.2 1.2 fusion.87
  146.4 1.9 fusion.88
  148.4 5.3 %fusion.89 = (f32[2,512]{1,0:T(2,128)S(1)}, f32[2,512,4096]{2,1,0:T(8,128)S(1)}) fusion(pred[512,4096]{1,0:T(8,128)(4,1)S(1)} %concatenate.18, bf16[4096,2,128]{2,0,1:T(8,128)(2,1)} %get-tuple-element.370, bf16[2048,2,128]{2,0,1:T(8,128)(2,1)S(1)} %get-tuple-element.369, s32[]{:T(128)S(6)} %select_n.80), kind=kOutput, calls=%fused_computation.3.clone.1 | convolution fusion | flops 1086323712 | bytes 21237764 | tf_op jit(solution)/shard_map/while/body/eval_jaxpr/qhd,khd->hqk/dot_general | solution.py:17
  153.7 4.6 %fusion.90 = f32[2,512]{1,0:T(2,128)S(1)} fusion(f32[2,512,4096]{2,1,0:T(8,128)S(1)} %get-tuple-element.327, f32[2,512]{1,0:T(2,128)S(1)} %get-tuple-element.328, pred[512,4096]{1,0:T(8,128)(4,1)S(1)} %concatenate.18), kind=kLoop, calls=%fused_computation.4.clone.1 | loop fusion | flops 16776192 | bytes 18882560 | tf_op jit(solution)/shard_map/while/body/eval_jaxpr/reduce_sum | solution.py:21
  158.4 5.6 %fusion.91 = bf16[4,512,2,128]{3,1,0,2:T(8,128)(2,1)S(1)} fusion(bf16[4,512,2,128]{3,1,0,2:T(8,128)(2,1)S(1)} %get-tuple-element.347, s32[]{:T(128)S(6)} %copy.69, f32[512,2,128]{2,0,1:T(8,128)S(1)} %copy-done.8, bf16[4096,2,128]{2,0,1:T(8,128)(2,1)S(1)} %copy-done, f32[2,512,4096]{2,1,0:T(8,128)S(1)} %get-tuple-element.327, ...), kind=kOutput, calls=%fused_computation.25.clone.1 | convolution fusion | flops 1090912256 | bytes 21766148 | tf_op jit(solution)/shard_map/while/body/eval_jaxpr/hqk,khd->qhd/dot_general | solution.py:22
  167.4 1.1 fusion.86
  168.5 1.2 fusion.87
  169.7 1.9 fusion.88
  171.6 5.3 %fusion.89 = (f32[2,512]{1,0:T(2,128)S(1)}, f32[2,512,4096]{2,1,0:T(8,128)S(1)}) fusion(pred[512,4096]{1,0:T(8,128)(4,1)S(1)} %concatenate.18, bf16[4096,2,128]{2,0,1:T(8,128)(2,1)} %get-tuple-element.370, bf16[2048,2,128]{2,0,1:T(8,128)(2,1)S(1)} %get-tuple-element.369, s32[]{:T(128)S(6)} %select_n.80), kind=kOutput, calls=%fused_computation.3.clone.1 | convolution fusion | flops 1086323712 | bytes 21237764 | tf_op jit(solution)/shard_map/while/body/eval_jaxpr/qhd,khd->hqk/dot_general | solution.py:17
  177.0 4.6 %fusion.90 = f32[2,512]{1,0:T(2,128)S(1)} fusion(f32[2,512,4096]{2,1,0:T(8,128)S(1)} %get-tuple-element.327, f32[2,512]{1,0:T(2,128)S(1)} %get-tuple-element.328, pred[512,4096]{1,0:T(8,128)(4,1)S(1)} %concatenate.18), kind=kLoop, calls=%fused_computation.4.clone.1 | loop fusion | flops 16776192 | bytes 18882560 | tf_op jit(solution)/shard_map/while/body/eval_jaxpr/reduce_sum | solution.py:21
  181.7 5.6 %fusion.91 = bf16[4,512,2,128]{3,1,0,2:T(8,128)(2,1)S(1)} fusion(bf16[4,512,2,128]{3,1,0,2:T(8,128)(2,1)S(1)} %get-tuple-element.347, s32[]{:T(128)S(6)} %copy.69, f32[512,2,128]{2,0,1:T(8,128)S(1)} %copy-done.8, bf16[4096,2,128]{2,0,1:T(8,128)(2,1)S(1)} %copy-done, f32[2,512,4096]{2,1,0:T(8,128)S(1)} %get-tuple-element.327, ...), kind=kOutput, calls=%fused_computation.25.clone.1 | convolution fusion | flops 1090912256 | bytes 21766148 | tf_op jit(solution)/shard_map/while/body/eval_jaxpr/hqk,khd->qhd/dot_general | solution.py:22
  190.6 1.1 fusion.86
  191.7 1.2 fusion.87
  193.0 1.9 fusion.88
  194.9 5.3 %fusion.89 = (f32[2,512]{1,0:T(2,128)S(1)}, f32[2,512,4096]{2,1,0:T(8,128)S(1)}) fusion(pred[512,4096]{1,0:T(8,128)(4,1)S(1)} %concatenate.18, bf16[4096,2,128]{2,0,1:T(8,128)(2,1)} %get-tuple-element.370, bf16[2048,2,128]{2,0,1:T(8,128)(2,1)S(1)} %get-tuple-element.369, s32[]{:T(128)S(6)} %select_n.80), kind=kOutput, calls=%fused_computation.3.clone.1 | convolution fusion | flops 1086323712 | bytes 21237764 | tf_op jit(solution)/shard_map/while/body/eval_jaxpr/qhd,khd->hqk/dot_general | solution.py:17
  200.3 4.6 %fusion.90 = f32[2,512]{1,0:T(2,128)S(1)} fusion(f32[2,512,4096]{2,1,0:T(8,128)S(1)} %get-tuple-element.327, f32[2,512]{1,0:T(2,128)S(1)} %get-tuple-element.328, pred[512,4096]{1,0:T(8,128)(4,1)S(1)} %concatenate.18), kind=kLoop, calls=%fused_computation.4.clone.1 | loop fusion | flops 16776192 | bytes 18882560 | tf_op jit(solution)/shard_map/while/body/eval_jaxpr/reduce_sum | solution.py:21
  204.9 5.6 %fusion.91 = bf16[4,512,2,128]{3,1,0,2:T(8,128)(2,1)S(1)} fusion(bf16[4,512,2,128]{3,1,0,2:T(8,128)(2,1)S(1)} %get-tuple-element.347, s32[]{:T(128)S(6)} %copy.69, f32[512,2,128]{2,0,1:T(8,128)S(1)} %copy-done.8, bf16[4096,2,128]{2,0,1:T(8,128)(2,1)S(1)} %copy-done, f32[2,512,4096]{2,1,0:T(8,128)S(1)} %get-tuple-element.327, ...), kind=kOutput, calls=%fused_computation.25.clone.1 | convolution fusion | flops 1090912256 | bytes 21766148 | tf_op jit(solution)/shard_map/while/body/eval_jaxpr/hqk,khd->qhd/dot_general | solution.py:22
  213.9 1.1 fusion.86
  215.0 1.2 fusion.87
  216.2 1.9 fusion.88
  218.2 5.3 %fusion.89 = (f32[2,512]{1,0:T(2,128)S(1)}, f32[2,512,4096]{2,1,0:T(8,128)S(1)}) fusion(pred[512,4096]{1,0:T(8,128)(4,1)S(1)} %concatenate.18, bf16[4096,2,128]{2,0,1:T(8,128)(2,1)} %get-tuple-element.370, bf16[2048,2,128]{2,0,1:T(8,128)(2,1)S(1)} %get-tuple-element.369, s32[]{:T(128)S(6)} %select_n.80), kind=kOutput, calls=%fused_computation.3.clone.1 | convolution fusion | flops 1086323712 | bytes 21237764 | tf_op jit(solution)/shard_map/while/body/eval_jaxpr/qhd,khd->hqk/dot_general | solution.py:17
  223.5 4.6 %fusion.90 = f32[2,512]{1,0:T(2,128)S(1)} fusion(f32[2,512,4096]{2,1,0:T(8,128)S(1)} %get-tuple-element.327, f32[2,512]{1,0:T(2,128)S(1)} %get-tuple-element.328, pred[512,4096]{1,0:T(8,128)(4,1)S(1)} %concatenate.18), kind=kLoop, calls=%fused_computation.4.clone.1 | loop fusion | flops 16776192 | bytes 18882560 | tf_op jit(solution)/shard_map/while/body/eval_jaxpr/reduce_sum | solution.py:21
  228.2 5.6 %fusion.91 = bf16[4,512,2,128]{3,1,0,2:T(8,128)(2,1)S(1)} fusion(bf16[4,512,2,128]{3,1,0,2:T(8,128)(2,1)S(1)} %get-tuple-element.347, s32[]{:T(128)S(6)} %copy.69, f32[512,2,128]{2,0,1:T(8,128)S(1)} %copy-done.8, bf16[4096,2,128]{2,0,1:T(8,128)(2,1)S(1)} %copy-done, f32[2,512,4096]{2,1,0:T(8,128)S(1)} %get-tuple-element.327, ...), kind=kOutput, calls=%fused_computation.25.clone.1 | convolution fusion | flops 1090912256 | bytes 21766148 | tf_op jit(solution)/shard_map/while/body/eval_jaxpr/hqk,khd->qhd/dot_general | solution.py:22
  233.8 8.9 %copy.57 = bf16[2048,2,128]{2,1,0:T(2,128)(2,1)S(1)} copy(bf16[2048,2,128]{2,0,1:T(8,128)(2,1)S(1)} %bitcast.106) | data formatting | bytes 2097152 | tf_op jit(solution)/shard_map/reshape | solution.py:79
  242.7 21.3 %all_to_all.69 = bf16[2048,2,128]{2,1,0:T(2,128)(2,1)S(1)} all-to-all(bf16[2048,2,128]{2,1,0:T(2,128)(2,1)S(1)} %copy.57), channel_id=1, replica_groups=mesh['span'=16,'seq'=16] {'seq'}, dimensions={0} | all-to-all | bytes 2097152 | tf_op jit(solution)/shard_map/all_to_all | solution.py:80
  264.1 0.7 copy.59
  264.8 1.3 copy.60
  (75 shorter events, 12.3 us)
Async XLA Ops:
  6.5 10.1 %copy-start.1 = (bf16[1,128,4096]{2,1,0:T(8,128)(2,1)S(1)}, bf16[1,128,4096]{2,1,0:T(8,128)(2,1)}, u32[]{:S(2)}) copy-start(bf16[1,128,4096]{2,1,0:T(8,128)(2,1)} %param.12) | copy-start | bytes 3145732
  8.9 33.0 %copy-start.2 = (bf16[1,128,4096]{2,1,0:T(8,128)(2,1)S(1)}, bf16[1,128,4096]{2,1,0:T(8,128)(2,1)}, u32[]{:S(2)}) copy-start(bf16[1,128,4096]{2,1,0:T(8,128)(2,1)} %param.11) | copy-start | bytes 3145732
  8.9 22.7 %all-to-all-start.2 = ((bf16[128,32,128]{0,2,1:T(8,128)(2,1)}), bf16[128,32,128]{0,2,1:T(8,128)(2,1)S(1)}, u32[]{:S(2)}, u32[]{:S(2)}) async-start(bf16[128,32,128]{0,2,1:T(8,128)(2,1)} %bitcast.12), calls=%async_computation.2 | async-start | bytes 2097152 | tf_op jit(solution)/shard_map/all_to_all | solution.py:36
  15.9 120.5 %all-gather.2.cloned.1.call-start = ((), (), s32[]{:S(2)}) async-start(), calls=%async_computation.4 | async-start | bytes 2228224 | tf_op jit(solution)/shard_map/all_gather | solution.py:44
  31.6 72.1 %all-to-all-start.1 = ((bf16[128,32,128]{0,2,1:T(8,128)(2,1)}), bf16[128,32,128]{0,2,1:T(8,128)(2,1)S(1)}, u32[]{:S(2)}, u32[]{:S(2)}) async-start(bf16[128,32,128]{0,2,1:T(8,128)(2,1)} %bitcast.7), calls=%async_computation.1 | async-start | bytes 2097152 | tf_op jit(solution)/shard_map/all_to_all | solution.py:35
  36.0 76.3 %copy-start.5 = (s32[1,16,2]{1,2,0:T(2,128)S(1)}, s32[1,16,2]{1,2,0:T(2,128)}, u32[]{:S(2)}) copy-start(s32[1,16,2]{1,2,0:T(2,128)} %param.18) | copy-start | bytes 388
  36.0 76.3 %copy-start.4 = (s32[1,2048]{1,0:T(1,128)S(1)}, s32[1,2048]{1,0:T(1,128)}, u32[]{:S(2)}) copy-start(s32[1,2048]{1,0:T(1,128)} %param.17) | copy-start | bytes 24580
  37.3 87.1 %collective-permute-start.1 = (bf16[2048,2,128]{2,0,1:T(8,128)(2,1)}, bf16[2048,2,128]{2,0,1:T(8,128)(2,1)}, u32[]{:S(2)}, u32[]{:S(2)}) collective-permute-start(bf16[2048,2,128]{2,0,1:T(8,128)(2,1)} %bitcast.16), channel_id=1, source_target_pairs={{0,16},{16,32},{32,48},{48,64},{64,80},{80,96},{96,112},{112,128},... | collective-permute-start | bytes 3145736 | tf_op jit(solution)/shard_map/ppermute | solution.py:13
  103.7 20.1 %all-to-all-start = ((bf16[128,32,128]{0,2,1:T(8,128)(2,1)}), bf16[128,32,128]{0,2,1:T(8,128)(2,1)S(1)}, u32[]{:S(2)}, u32[]{:S(2)}) async-start(bf16[128,32,128]{0,2,1:T(8,128)(2,1)} %bitcast.2), calls=%async_computation | async-start | bytes 2097152 | tf_op jit(solution)/shard_map/all_to_all | solution.py:37
  109.3 24.2 %collective-permute-start = (bf16[2048,2,128]{2,0,1:T(8,128)(2,1)}, bf16[2048,2,128]{2,0,1:T(8,128)(2,1)}, u32[]{:S(2)}, u32[]{:S(2)}) collective-permute-start(bf16[2048,2,128]{2,0,1:T(8,128)(2,1)} %bitcast.11), channel_id=1, source_target_pairs={{0,16},{16,32},{32,48},{48,64},{64,80},{80,96},{96,112},{112,128},... | collective-permute-start | bytes 3145736 | tf_op jit(solution)/shard_map/ppermute | solution.py:13
  124.4 12.0 %copy-start.6 = (bf16[1024,256]{1,0:T(8,128)(2,1)S(1)}, bf16[1024,256]{1,0:T(8,128)(2,1)}, u32[]{:S(2)}) copy-start(bf16[1024,256]{1,0:T(8,128)(2,1)} %param.16) | copy-start | bytes 1572868
  124.4 12.0 %copy-start.7 = (bf16[1024,256]{1,0:T(8,128)(2,1)S(1)}, bf16[1024,256]{1,0:T(8,128)(2,1)}, u32[]{:S(2)}) copy-start(bf16[1024,256]{1,0:T(8,128)(2,1)} %param.15) | copy-start | bytes 1572868
  144.1 2.3 copy-start.3
  153.7 4.7 %copy-start = (bf16[4096,2,128]{2,0,1:T(8,128)(2,1)S(1)}, bf16[4096,2,128]{2,0,1:T(8,128)(2,1)}, u32[]{:S(2)}) copy-start(bf16[4096,2,128]{2,0,1:T(8,128)(2,1)} %get-tuple-element.371) | copy-start | bytes 6291460 | tf_op jit(solution)/shard_map/while
  153.7 4.7 %copy-start.8 = (f32[512,2,128]{2,0,1:T(8,128)S(1)}, f32[512,2,128]{2,0,1:T(8,128)}, u32[]{:S(2)}) copy-start(f32[512,2,128]{2,0,1:T(8,128)} %fusion.88) | copy-start | bytes 1572868 | tf_op jit(solution)/shard_map/while
  167.4 2.3 copy-start.3
  177.0 4.7 %copy-start = (bf16[4096,2,128]{2,0,1:T(8,128)(2,1)S(1)}, bf16[4096,2,128]{2,0,1:T(8,128)(2,1)}, u32[]{:S(2)}) copy-start(bf16[4096,2,128]{2,0,1:T(8,128)(2,1)} %get-tuple-element.371) | copy-start | bytes 6291460 | tf_op jit(solution)/shard_map/while
  177.0 4.7 %copy-start.8 = (f32[512,2,128]{2,0,1:T(8,128)S(1)}, f32[512,2,128]{2,0,1:T(8,128)}, u32[]{:S(2)}) copy-start(f32[512,2,128]{2,0,1:T(8,128)} %fusion.88) | copy-start | bytes 1572868 | tf_op jit(solution)/shard_map/while
  190.6 2.3 copy-start.3
  200.2 4.7 %copy-start = (bf16[4096,2,128]{2,0,1:T(8,128)(2,1)S(1)}, bf16[4096,2,128]{2,0,1:T(8,128)(2,1)}, u32[]{:S(2)}) copy-start(bf16[4096,2,128]{2,0,1:T(8,128)(2,1)} %get-tuple-element.371) | copy-start | bytes 6291460 | tf_op jit(solution)/shard_map/while
  200.3 4.7 %copy-start.8 = (f32[512,2,128]{2,0,1:T(8,128)S(1)}, f32[512,2,128]{2,0,1:T(8,128)}, u32[]{:S(2)}) copy-start(f32[512,2,128]{2,0,1:T(8,128)} %fusion.88) | copy-start | bytes 1572868 | tf_op jit(solution)/shard_map/while
  213.9 2.3 copy-start.3
  223.5 4.7 %copy-start = (bf16[4096,2,128]{2,0,1:T(8,128)(2,1)S(1)}, bf16[4096,2,128]{2,0,1:T(8,128)(2,1)}, u32[]{:S(2)}) copy-start(bf16[4096,2,128]{2,0,1:T(8,128)(2,1)} %get-tuple-element.371) | copy-start | bytes 6291460 | tf_op jit(solution)/shard_map/while
  223.5 4.7 %copy-start.8 = (f32[512,2,128]{2,0,1:T(8,128)S(1)}, f32[512,2,128]{2,0,1:T(8,128)}, u32[]{:S(2)}) copy-start(f32[512,2,128]{2,0,1:T(8,128)} %fusion.88) | copy-start | bytes 1572868 | tf_op jit(solution)/shard_map/while
Sparse Core Ops, SparseCore 0:
  18.6 87.0 all-gather.1

commit v2 on v1

v2 whole, which is shorter than its diff:
```python
import functools

import jax
import jax.numpy as jnp
from jax import lax
from jax.experimental import pallas as pl
from jax.experimental.pallas import tpu as pltpu
from jax.sharding import PartitionSpec as P

HEADS = 32
HD = 128
TQ = 256
TK = 256
TA = 128
NEG = -1e30


def _attn_kernel(hp_ref, ncur_ref, alo_ref, ahi_ref,
                 q_ref, kc_ref, vc_ref, kp_ref, vp_ref, ka_ref, va_ref, meta_ref,
                 o_ref, sp_ref, sc_ref, sa_ref, *, scale):
    i = pl.program_id(1)
    has_prev = hp_ref[0] > 0
    ncur = ncur_ref[i]
    alo = alo_ref[i]
    ahi = ahi_ref[i]
    q = q_ref[...]
    kend = meta_ref[:, 0:1]
    lower = meta_ref[:, 1:2]
    upper = meta_ref[:, 2:3]
    tq = q.shape[0]
    nprev = kp_ref.shape[0] // TK
    dims = (((1,), (1,)), ((), ()))

    def scores(k):
        return lax.dot_general(q, k, dims, preferred_element_type=jnp.float32) * scale

    m0 = jnp.full((tq, 1), NEG, jnp.float32)

    def prev_max(c, m):
        at = pl.multiple_of(c * TK, TK)
        s = scores(kp_ref[pl.ds(at, TK), :])
        sp_ref[:, pl.ds(at, TK)] = s
        return jnp.maximum(m, jnp.max(s, axis=1, keepdims=True))

    m = lax.cond(has_prev, lambda mm: lax.fori_loop(0, nprev, prev_max, mm), lambda mm: mm, m0)

    def cur_max(c, m):
        at = pl.multiple_of(c * TK, TK)
        s = scores(kc_ref[pl.ds(at, TK), :])
        col = at + lax.broadcasted_iota(jnp.int32, s.shape, 1)
        s = jnp.where(col < kend, s, NEG)
        sc_ref[:, pl.ds(at, TK)] = s
        return jnp.maximum(m, jnp.max(s, axis=1, keepdims=True))

    m = lax.fori_loop(0, ncur, cur_max, m)

    l0 = jnp.zeros((tq, 1), jnp.float32)
    a0 = jnp.zeros((tq, HD), jnp.float32)

    def prev_sum(c, carry):
        l, acc = carry
        at = pl.multiple_of(c * TK, TK)
        p = jnp.exp(sp_ref[:, pl.ds(at, TK)] - m)
        l = l + jnp.sum(p, axis=1, keepdims=True)
        acc = acc + jnp.dot(p.astype(jnp.bfloat16), vp_ref[pl.ds(at, TK), :],
                            preferred_element_type=jnp.float32)
        return l, acc

    carry = lax.cond(has_prev, lambda cr: lax.fori_loop(0, nprev, prev_sum, cr), lambda cr: cr, (l0, a0))

    def cur_sum(c, carry):
        l, acc = carry
        at = pl.multiple_of(c * TK, TK)
        p = jnp.exp(sc_ref[:, pl.ds(at, TK)] - m)
        l = l + jnp.sum(p, axis=1, keepdims=True)
        acc = acc + jnp.dot(p.astype(jnp.bfloat16), vc_ref[pl.ds(at, TK), :],
                            preferred_element_type=jnp.float32)
        return l, acc

    l, acc = lax.fori_loop(0, ncur, cur_sum, carry)
    self_out = acc / l

    def aud_max(c, m):
        at = pl.multiple_of(c * TA, TA)
        s = scores(ka_ref[pl.ds(at, TA), :])
        pos = at + lax.broadcasted_iota(jnp.int32, s.shape, 1)
        s = jnp.where(jnp.logical_and(pos >= lower, pos < upper), s, NEG)
        sa_ref[:, pl.ds(at, TA)] = s
        return jnp.maximum(m, jnp.max(s, axis=1, keepdims=True))

    ma = lax.fori_loop(alo, ahi, aud_max, m0)

    def aud_sum(c, carry):
        l, acc = carry
        at = pl.multiple_of(c * TA, TA)
        p = jnp.exp(sa_ref[:, pl.ds(at, TA)] - ma)
        l = l + jnp.sum(p, axis=1, keepdims=True)
        acc = acc + jnp.dot(p.astype(jnp.bfloat16), va_ref[pl.ds(at, TA), :],
                            preferred_element_type=jnp.float32)
        return l, acc

    la, acca = lax.fori_loop(alo, ahi, aud_sum, (l0, a0))
    aud_out = acca / la
    o_ref[...] = (self_out + aud_out).astype(o_ref.dtype)


def fused_attention(q2, kc2, vc2, kp2, vp2, aud2, frames, table, has_prev):
    tokens, width = q2.shape
    heads = width // HD
    aud_rows = aud2.shape[0]
    nq = tokens // TQ
    scale = HD ** (-0.5)
    nf = table.shape[0]
    onehot = frames[:, None] == jnp.arange(nf, dtype=jnp.int32)[None, :]
    counts = jnp.sum(onehot.astype(jnp.int32), axis=0)
    cum = jnp.cumsum(counts)
    kend = jnp.sum(jnp.where(onehot, cum[None, :], 0), axis=1)
    lower = jnp.sum(jnp.where(onehot, table[None, :, 0], 0), axis=1)
    upper = jnp.sum(jnp.where(onehot, table[None, :, 1], 0), axis=1)
    meta = jnp.stack([kend, lower, upper], axis=1).astype(jnp.int32)
    ncur = (kend.reshape(nq, TQ)[:, -1] + TK - 1) // TK
    alo = jnp.min(lower.reshape(nq, TQ), axis=1) // TA
    ahi = (jnp.max(upper.reshape(nq, TQ), axis=1) + TA - 1) // TA
    hp = has_prev.astype(jnp.int32).reshape(1)

    full_k = pl.BlockSpec((tokens, HD), lambda h, i, *_: (0, h))
    full_a_k = pl.BlockSpec((aud_rows, HD), lambda h, i, *_: (0, h))
    full_a_v = pl.BlockSpec((aud_rows, HD), lambda h, i, *_: (0, heads + h))
    grid_spec = pltpu.PrefetchScalarGridSpec(
        num_scalar_prefetch=4,
        grid=(heads, nq),
        in_specs=[
            pl.BlockSpec((TQ, HD), lambda h, i, *_: (i, h)),
            full_k, full_k, full_k, full_k,
            full_a_k, full_a_v,
            pl.BlockSpec((TQ, 3), lambda h, i, *_: (i, 0)),
        ],
        out_specs=pl.BlockSpec((TQ, HD), lambda h, i, *_: (i, h)),
        scratch_shapes=[
            pltpu.VMEM((TQ, kp2.shape[0]), jnp.float32),
            pltpu.VMEM((TQ, tokens), jnp.float32),
            pltpu.VMEM((TQ, aud_rows), jnp.float32),
        ],
    )
    kv_rows = tokens + kp2.shape[0]
    flops = 4 * heads * tokens * HD * (kv_rows + aud_rows)
    cost = pl.CostEstimate(flops=flops, transcendentals=heads * tokens * (kv_rows + aud_rows),
                           bytes_accessed=2 * (5 * tokens * width + aud2.size))
    return pl.pallas_call(
        functools.partial(_attn_kernel, scale=scale),
        grid_spec=grid_spec,
        out_shape=jax.ShapeDtypeStruct((tokens, width), jnp.bfloat16),
        compiler_params=pltpu.CompilerParams(dimension_semantics=("arbitrary", "arbitrary")),
        cost_estimate=cost,
    )(hp, ncur, alo, ahi, q2, kc2, vc2, kp2, vp2, aud2, aud2, meta)


def shifted(value, axis, steps):
    count = lax.axis_size(axis)
    leading, last = (max(0, -steps), min(count, count - steps))
    return lax.ppermute(value, axis, [(source, source + steps) for source in range(leading, last)])


def local(queries, keys, values, audio, audio_wk, audio_wv, frame_ids, windows, video_start):
    tok_rows = queries.shape[1]
    groups = lax.axis_size("seq")
    width = HEADS * HD // groups

    def to_heads(x):
        x = x.reshape(tok_rows, groups, width)
        x = lax.all_to_all(x, "seq", split_axis=1, concat_axis=0, tiled=True)
        return x.reshape(tok_rows * groups, width)

    k2 = to_heads(keys)
    v2 = to_heads(values)
    q2 = to_heads(queries)
    kp2, vp2 = shifted((k2, v2), "span", 1)
    joint_w = jnp.concatenate([audio_wk, audio_wv], axis=1)
    aud2 = jnp.dot(
        lax.all_gather(audio, "seq", axis=1, tiled=True)[0],
        joint_w,
        preferred_element_type=jnp.float32,
    ).astype(jnp.bfloat16)
    has_prev = jnp.logical_and(lax.axis_index("span") > 0, video_start[0] == 0)
    out2 = fused_attention(q2, k2, v2, kp2, vp2, aud2, frame_ids[0], windows[0], has_prev)
    out3 = out2.reshape(tok_rows * groups, 1, width)
    back = lax.all_to_all(out3, "seq", split_axis=0, concat_axis=1, tiled=True)
    return back.reshape(1, tok_rows, HEADS * HD)


def solution(mesh):
    placed = (
        P("span", "seq", None),
        P("span", "seq", None),
        P("span", "seq", None),
        P("span", "seq", None),
        P(None, "seq"),
        P(None, "seq"),
        P("span", None),
        P("span", None, None),
        P("span"),
    )
    return jax.shard_map(
        local, mesh=mesh, in_specs=placed, out_specs=P("span", "seq", None), check_vma=False
    )
```

time: 274 us -> 276 us (level)
  the two profiles are of different devices: /device:TPU:1 before, /device:TPU:64 now
where the time goes in v2:
time: 276 us
  Pallas kernels  150 us (54%)
  waiting for transfers between devices  49.3 us (18%)
  blocking collectives  21.7 us (8%)
  starting transfers between devices  20.4 us (7%)
  between operations  14.3 us (5%)
  local copies, waits for them, and re-layouts  11.4 us (4%)
  other arithmetic  4.61 us (2%)
  matrix products  4.08 us (1%)
    pallas_call x1, Pallas kernels, fused_attention(): pl.pallas_call(functools.partial(_attn_kernel, scale=scale), grid_spec=gr...  150 us
    all_to_all x3, waiting for transfers between devices, to_heads(): x = lax.all_to_all(x, 'seq', split_axis=1, concat_axis=0, tiled=True)  36 us
    all_to_all x1, blocking collectives, local(): back = lax.all_to_all(out3, 'seq', split_axis=0, concat_axis=1, tiled=True)  21.7 us
    all_to_all x3, starting transfers between devices, to_heads(): x = lax.all_to_all(x, 'seq', split_axis=1, concat_axis=0, tiled=True)  12.8 us
    ppermute x2, waiting for transfers between devices, shifted(): lax.ppermute(value, axis, [(source, source + steps) for source in range(l...  12.6 us
    ppermute x2, starting transfers between devices, shifted(): lax.ppermute(value, axis, [(source, source + steps) for source in range(l...  7.59 us
  transfers between devices with their start and end apart: 6, of which 4 were waited for; matrix products, arithmetic and copies ran while one was open for 5% of the time, Pallas kernels for 0%

profile of v2, /device:TPU:64, one launch (start us, length us, event | category | flops | bytes accessed | tf_op | source)
XLA Modules:
  0.0 275.6 jit_solution(10514854481094660476)
XLA Ops:
  6.5 0.0 all-gather.2.cloned.1.call-start
  6.5 0.7 all-gather.2.cloned.1.call-update
  7.3 1.5 copy.71
  8.7 0.0 copy-start
  8.7 1.3 copy.61
  10.1 5.5 %all-to-all-start.2 = ((bf16[128,16,256]{2,0,1:T(8,128)(2,1)}), bf16[128,16,256]{2,0,1:T(8,128)(2,1)S(1)}, u32[]{:S(2)}, u32[]{:S(2)}) async-start(bf16[128,16,256]{2,0,1:T(8,128)(2,1)} %copy.61), calls=%async_computation.2 | async-start | bytes 2097152 | tf_op jit(solution)/shard_map/all_to_all | solution.py:171
  15.6 0.0 copy-done
  15.6 0.2 copy.70
  15.8 0.0 copy-start.5
  15.8 0.0 copy-start.1
  15.9 1.3 copy.60
  17.2 17.7 %all-to-all-done.2 = bf16[128,16,256]{2,0,1:T(8,128)(2,1)S(1)} async-done(((bf16[128,16,256]{2,0,1:T(8,128)(2,1)}), bf16[128,16,256]{2,0,1:T(8,128)(2,1)S(1)}, u32[]{:S(2)}, u32[]{:S(2)}) %all-to-all-start.2) | async-done | bytes 1048608 | tf_op jit(solution)/shard_map/all_to_all | solution.py:171
  34.9 3.7 %all-to-all-start.1 = ((bf16[128,16,256]{2,0,1:T(8,128)(2,1)}), bf16[128,16,256]{2,0,1:T(8,128)(2,1)S(1)}, u32[]{:S(2)}, u32[]{:S(2)}) async-start(bf16[128,16,256]{2,0,1:T(8,128)(2,1)} %copy.60), calls=%async_computation.1 | async-start | bytes 2097152 | tf_op jit(solution)/shard_map/all_to_all | solution.py:171
  38.5 0.0 copy-done.5
  38.5 0.1 convert_reduce_fusion
  38.7 0.1 copy.58
  38.8 0.1 reduce
  38.9 0.0 copy-done.1
  38.9 0.0 copy-start.6
  38.9 0.2 copy.69
  39.2 1.3 copy.59
  40.5 0.0 copy-done.6
  40.5 0.1 select_reduce_fusion
  40.7 0.0 copy-done.2
  40.7 3.8 %collective-permute-start.1 = (bf16[2048,256]{1,0:T(8,128)(2,1)S(1)}, bf16[2048,256]{1,0:T(8,128)(2,1)}, u32[]{:S(2)}, u32[]{:S(2)}) collective-permute-start(bf16[2048,256]{1,0:T(8,128)(2,1)S(1)} %bitcast.59), channel_id=1, source_target_pairs={{0,16},{16,32},{32,48},{48,64},{64,80},{80,96},{96,112},{112,128},... | collective-permute-start | bytes 3145736 | tf_op jit(solution)/shard_map/ppermute | solution.py:161
  44.5 13.2 %all-to-all-done.1 = bf16[128,16,256]{2,0,1:T(8,128)(2,1)S(1)} async-done(((bf16[128,16,256]{2,0,1:T(8,128)(2,1)}), bf16[128,16,256]{2,0,1:T(8,128)(2,1)S(1)}, u32[]{:S(2)}, u32[]{:S(2)}) %all-to-all-start.1) | async-done | bytes 1048608 | tf_op jit(solution)/shard_map/all_to_all | solution.py:171
  57.7 3.7 %all-to-all-start = ((bf16[128,16,256]{2,0,1:T(8,128)(2,1)}), bf16[128,16,256]{2,0,1:T(8,128)(2,1)S(1)}, u32[]{:S(2)}, u32[]{:S(2)}) async-start(bf16[128,16,256]{2,0,1:T(8,128)(2,1)} %copy.59), calls=%async_computation | async-start | bytes 2097152 | tf_op jit(solution)/shard_map/all_to_all | solution.py:171
  61.4 3.8 %collective-permute-start = (bf16[2048,256]{1,0:T(8,128)(2,1)S(1)}, bf16[2048,256]{1,0:T(8,128)(2,1)}, u32[]{:S(2)}, u32[]{:S(2)}) collective-permute-start(bf16[2048,256]{1,0:T(8,128)(2,1)S(1)} %bitcast.61), channel_id=1, source_target_pairs={{0,16},{16,32},{32,48},{48,64},{64,80},{80,96},{96,112},{112,128},... | collective-permute-start | bytes 3145736 | tf_op jit(solution)/shard_map/ppermute | solution.py:161
  65.9 1.3 copy.63.meta_ref
  67.2 0.1 reduce_max.9
  67.4 0.1 reduce_min.9
  67.5 0.2 fusion.11
  67.7 0.5 and_select_fusion.2.ncur_ref
  68.2 0.5 and_select_fusion
  68.7 4.1 %fusion.5.ka_ref.va_ref = bf16[1024,512]{1,0:T(8,128)(2,1)} fusion(bf16[1,1024,1024]{2,1,0:T(8,128)(2,1)} %all-gather.2.cloned.1.call-done, bf16[1024,256]{1,0:T(8,128)(2,1)} %param.14, bf16[1024,256]{1,0:T(8,128)(2,1)} %param.13), kind=kOutput, calls=%fused_computation.3 | convolution fusion | flops 1076363264 | bytes 4194304 | tf_op jit(solution)/shard_map/dot_general | solution.py:179
  72.8 0.0 copy-done.3
  72.8 5.1 %all-to-all-done = bf16[128,16,256]{2,0,1:T(8,128)(2,1)S(1)} async-done(((bf16[128,16,256]{2,0,1:T(8,128)(2,1)}), bf16[128,16,256]{2,0,1:T(8,128)(2,1)S(1)}, u32[]{:S(2)}, u32[]{:S(2)}) %all-to-all-start) | async-done | bytes 1048608 | tf_op jit(solution)/shard_map/all_to_all | solution.py:171
  77.9 0.0 collective-permute-done.1.vp_ref
  77.9 12.6 %collective-permute-done.kp_ref = bf16[2048,256]{1,0:T(8,128)(2,1)} collective-permute-done((bf16[2048,256]{1,0:T(8,128)(2,1)S(1)}, bf16[2048,256]{1,0:T(8,128)(2,1)}, u32[]{:S(2)}, u32[]{:S(2)}) %collective-permute-start) | collective-permute-done | bytes 1048608 | tf_op jit(solution)/shard_map/ppermute | solution.py:161
  90.5 149.8 %shard_map.91 = bf16[2048,256]{1,0:T(8,128)(2,1)} custom-call(s32[1]{0:T(128)} %bitcast.1.hp_ref, s32[8]{0:T(128)} %and_select_fusion.2.ncur_ref, s32[8]{0:T(128)} %get-tuple-element.11.alo_ref, s32[8]{0:T(128)} %get-tuple-element.10.ahi_ref, bf16[2048,256]{1,0:T(8,128)(2,1)} %bitcast.63, bf16[2048,256]{1,0:T(8,128)(2,1)} %bitcast.62, ...), custom_call_target="tpu_custom_call" | custom-call | flops 10737418240 | bytes 6291456 | tf_op jit(solution)/shard_map/pallas_call | solution.py:149
  240.3 0.5 broadcast.46
  240.8 2.7 reduce.3
  243.5 0.3 reshape.92
  243.8 21.7 %all_to_all.60 = bf16[16,2,16384]{2,1,0:T(2,128)(2,1)S(1)} all-to-all(bf16[16,2,16384]{2,1,0:T(2,128)(2,1)S(1)} %reshape.92), channel_id=1, replica_groups=mesh['span'=16,'seq'=16] {'seq'}, dimensions={0} | all-to-all | bytes 2097152 | tf_op jit(solution)/shard_map/all_to_all | solution.py:187
  265.5 1.0 reshape.93
  266.6 0.2 copy.68
  266.7 0.7 copy.65
  267.4 1.3 copy.66
  (11 shorter events, 0.1 us)
Async XLA Ops:
  6.5 62.2 %all-gather.2.cloned.1.call-start = ((), (), s32[]{:S(2)}) async-start(), calls=%async_computation.4 | async-start | bytes 2228224 | tf_op jit(solution)/shard_map/all_gather | solution.py:180
  8.7 6.8 %copy-start = (bf16[1,128,4096]{2,1,0:T(8,128)(2,1)S(1)}, bf16[1,128,4096]{2,1,0:T(8,128)(2,1)}, u32[]{:S(2)}) copy-start(bf16[1,128,4096]{2,1,0:T(8,128)(2,1)} %param.10) | copy-start | bytes 3145732
  10.1 24.8 %all-to-all-start.2 = ((bf16[128,16,256]{2,0,1:T(8,128)(2,1)}), bf16[128,16,256]{2,0,1:T(8,128)(2,1)S(1)}, u32[]{:S(2)}, u32[]{:S(2)}) async-start(bf16[128,16,256]{2,0,1:T(8,128)(2,1)} %copy.61), calls=%async_computation.2 | async-start | bytes 2097152 | tf_op jit(solution)/shard_map/all_to_all | solution.py:171
  15.8 22.7 %copy-start.5 = (s32[1,2048]{1,0:T(1,128)S(1)}, s32[1,2048]{1,0:T(1,128)}, u32[]{:S(2)}) copy-start(s32[1,2048]{1,0:T(1,128)} %param.15) | copy-start | bytes 24580
  15.8 23.1 %copy-start.1 = (bf16[1,128,4096]{2,1,0:T(8,128)(2,1)S(1)}, bf16[1,128,4096]{2,1,0:T(8,128)(2,1)}, u32[]{:S(2)}) copy-start(bf16[1,128,4096]{2,1,0:T(8,128)(2,1)} %param.9) | copy-start | bytes 3145732
  34.9 5.8 %copy-start.2 = (bf16[128,16,256]{2,0,1:T(8,128)(2,1)}, bf16[128,16,256]{2,0,1:T(8,128)(2,1)S(1)}, u32[]{:S(2)}) copy-start(bf16[128,16,256]{2,0,1:T(8,128)(2,1)S(1)} %all-to-all-done.2) | copy-start | bytes 3145732
  34.9 22.9 %all-to-all-start.1 = ((bf16[128,16,256]{2,0,1:T(8,128)(2,1)}), bf16[128,16,256]{2,0,1:T(8,128)(2,1)S(1)}, u32[]{:S(2)}, u32[]{:S(2)}) async-start(bf16[128,16,256]{2,0,1:T(8,128)(2,1)} %copy.60), calls=%async_computation.1 | async-start | bytes 2097152 | tf_op jit(solution)/shard_map/all_to_all | solution.py:171
  38.9 1.6 copy-start.6
  40.7 37.2 %collective-permute-start.1 = (bf16[2048,256]{1,0:T(8,128)(2,1)S(1)}, bf16[2048,256]{1,0:T(8,128)(2,1)}, u32[]{:S(2)}, u32[]{:S(2)}) collective-permute-start(bf16[2048,256]{1,0:T(8,128)(2,1)S(1)} %bitcast.59), channel_id=1, source_target_pairs={{0,16},{16,32},{32,48},{48,64},{64,80},{80,96},{96,112},{112,128},... | collective-permute-start | bytes 3145736 | tf_op jit(solution)/shard_map/ppermute | solution.py:161
  57.7 15.1 %copy-start.3 = (bf16[128,16,256]{2,0,1:T(8,128)(2,1)}, bf16[128,16,256]{2,0,1:T(8,128)(2,1)S(1)}, u32[]{:S(2)}) copy-start(bf16[128,16,256]{2,0,1:T(8,128)(2,1)S(1)} %all-to-all-done.1) | copy-start | bytes 3145732
  57.7 20.2 %all-to-all-start = ((bf16[128,16,256]{2,0,1:T(8,128)(2,1)}), bf16[128,16,256]{2,0,1:T(8,128)(2,1)S(1)}, u32[]{:S(2)}, u32[]{:S(2)}) async-start(bf16[128,16,256]{2,0,1:T(8,128)(2,1)} %copy.59), calls=%async_computation | async-start | bytes 2097152 | tf_op jit(solution)/shard_map/all_to_all | solution.py:171
  61.4 29.1 %collective-permute-start = (bf16[2048,256]{1,0:T(8,128)(2,1)S(1)}, bf16[2048,256]{1,0:T(8,128)(2,1)}, u32[]{:S(2)}, u32[]{:S(2)}) collective-permute-start(bf16[2048,256]{1,0:T(8,128)(2,1)S(1)} %bitcast.61), channel_id=1, source_target_pairs={{0,16},{16,32},{32,48},{48,64},{64,80},{80,96},{96,112},{112,128},... | collective-permute-start | bytes 3145736 | tf_op jit(solution)/shard_map/ppermute | solution.py:161
  77.9 12.6 %copy-start.4 = (bf16[128,16,256]{2,0,1:T(8,128)(2,1)}, bf16[128,16,256]{2,0,1:T(8,128)(2,1)S(1)}, u32[]{:S(2)}) copy-start(bf16[128,16,256]{2,0,1:T(8,128)(2,1)S(1)} %all-to-all-done) | copy-start | bytes 3145732
Sparse Core Ops, SparseCore 0:
  9.2 50.6 all-gather.1

commit v3 on v1

--- a/solution.py
+++ b/solution.py
@@ -4,6 +4,7 @@
 from jax.sharding import PartitionSpec as P
 
 HEADS = 32
+SEQ = ("chip", "core")
 HD = 128
 
 
@@ -32,16 +33,18 @@
     k_local = keys.reshape(tok_rows, HEADS, HD)
     v_local = values.reshape(tok_rows, HEADS, HD)
     k_heads, v_heads, q_heads = (
-        lax.all_to_all(k_local, "seq", split_axis=1, concat_axis=0, tiled=True),
-        lax.all_to_all(v_local, "seq", split_axis=1, concat_axis=0, tiled=True),
-        lax.all_to_all(q_local, "seq", split_axis=1, concat_axis=0, tiled=True),
+        lax.all_to_all(k_local, SEQ, split_axis=1, concat_axis=0, tiled=True),
+        lax.all_to_all(v_local, SEQ, split_axis=1, concat_axis=0, tiled=True),
+        lax.all_to_all(q_local, SEQ, split_axis=1, concat_axis=0, tiled=True),
     )
     prev_kh, prev_vh = shifted((k_heads, v_heads), "span", 1)
     span_rows = q_heads.shape[0]
     head_count = q_heads.shape[1]
     joint_w = jnp.concatenate([audio_wk, audio_wv], axis=1)
+    own = lax.all_gather(audio[0], "chip", axis=0, tiled=True)
+    gathered = lax.all_gather(own, "core", axis=0, tiled=True)
     projected = jnp.dot(
-        lax.all_gather(audio, "seq", axis=1, tiled=True)[0],
+        gathered,
         joint_w,
         preferred_element_type=jnp.float32,
     ).astype(jnp.bfloat16)[None][0]
@@ -56,7 +59,12 @@
     upper = jnp.sum(jnp.where(onehot, table[None, :, 1], 0), axis=1)
     all_keys = jnp.concatenate([prev_kh, k_heads], axis=0)
     all_vals = jnp.concatenate([prev_vh, v_heads], axis=0)
-    positions = jnp.arange(aud_rows, dtype=jnp.int32)
+    cores = lax.axis_size("core")
+    chips = lax.axis_size("chip")
+    piece = aud_rows // (cores * chips)
+    order = jnp.arange(aud_rows, dtype=jnp.int32)
+    held_core, held_chip, row = order // (chips * piece), (order // piece) % chips, order % piece
+    positions = (held_chip * cores + held_core) * piece + row
     block = min(512, span_rows)
 
     def one_block(index):
@@ -77,22 +85,24 @@
 
     blocks = lax.map(one_block, jnp.arange(span_rows // block, dtype=jnp.int32))
     mixed = blocks.reshape(span_rows, head_count, HD)
-    back = lax.all_to_all(mixed, "seq", split_axis=0, concat_axis=1, tiled=True)
+    back = lax.all_to_all(mixed, SEQ, split_axis=0, concat_axis=1, tiled=True)
     return back.reshape(1, tok_rows, HEADS * HD)
 
 
 def solution(mesh):
     placed = (
-        P("span", "seq", None),
-        P("span", "seq", None),
-        P("span", "seq", None),
-        P("span", "seq", None),
-        P(None, "seq"),
-        P(None, "seq"),
+        P("span", SEQ, None),
+        P("span", SEQ, None),
+        P("span", SEQ, None),
+        P("span", SEQ, None),
+        P(None, SEQ),
+        P(None, SEQ),
         P("span", None),
         P("span", None, None),
         P("span"),
     )
+    span, seq = mesh.devices.shape
+    split = jax.sharding.Mesh(mesh.devices.reshape(span, seq // 2, 2), ("span", "chip", "core"))
     return jax.shard_map(
-        local, mesh=mesh, in_specs=placed, out_specs=P("span", "seq", None), check_vma=False
+        local, mesh=split, in_specs=placed, out_specs=P("span", SEQ, None), check_vma=False
     )

time: 274 us -> 272 us (level)
  waiting for transfers between devices: 92.1 us -> 84.7 us
  starting transfers between devices: 22.6 us -> 27.6 us
    all_to_all x3, waiting for transfers between devices: 85.5 us -> 58 us  [the longest x1 44.4 us: local(): lax.all_to_all(q_local, SEQ, split_axis=1, concat_axis=0, tiled=True)]
    all_gather x1 -> x2, waiting for transfers between devices: 0.01 us -> 26 us  [the longest x1 26 us: local(): own = lax.all_gather(audio[0], 'chip', axis=0, tiled=True)]
    ppermute x2, waiting for transfers between devices: 5.92 us -> 0.01 us  [shifted(): lax.ppermute(value, axis, [(source, source + steps) for source in range(l...]
    all_to_all x3, starting transfers between devices: 15.8 us -> 19.5 us  [the longest x1 8.18 us: local(): lax.all_to_all(q_local, SEQ, split_axis=1, concat_axis=0, tiled=True)]
    unnamed x17 -> x15, local copies, waits for them, and re-layouts: 6.26 us -> 7.2 us
  transfers between devices with their start and end apart: 6 -> 7, of which waited for: 4 -> 3; matrix products, arithmetic and copies ran while one was open for 4% -> 5% of each run, Pallas kernels for 0% -> 0%
where the time goes in v3:
time: 272 us; the launch traced here: 271 us
  waiting for transfers between devices  84.7 us (31%)
  matrix products  58.5 us (22%)
  other arithmetic  34.3 us (13%)
  local copies, waits for them, and re-layouts  27.8 us (10%)
  starting transfers between devices  27.6 us (10%)
  blocking collectives  20.6 us (8%)
  between operations  14.2 us (5%)
  loops' own time  3.14 us (1%)
    all_to_all x1, waiting for transfers between devices, local(): lax.all_to_all(q_local, SEQ, split_axis=1, concat_axis=0, tiled=True)  44.4 us
    dot_general x8, matrix products, attend(): jnp.einsum('hqk,khd->qhd', weights.astype(jnp.bfloat16), value_rows, pref...  30 us
    all_gather x1, waiting for transfers between devices, local(): own = lax.all_gather(audio[0], 'chip', axis=0, tiled=True)  26 us
    dot_general x8, matrix products, attend(): jnp.einsum('qhd,khd->hqk', query, key_rows, preferred_element_type=jnp.fl...  25.6 us
    reduce_sum x8, other arithmetic, attend(): den = jnp.sum(weights, axis=-1, keepdims=True)  23.5 us
    all_to_all x1, blocking collectives, local(): back = lax.all_to_all(mixed, SEQ, split_axis=0, concat_axis=1, tiled=True)  20.6 us
    all_to_all x1, waiting for transfers between devices, local(): lax.all_to_all(v_local, SEQ, split_axis=1, concat_axis=0, tiled=True)  13.6 us
    reshape x1, local copies, waits for them, and re-layouts, local(): mixed = blocks.reshape(span_rows, head_count, HD)  8.9 us
  transfers between devices with their start and end apart: 7, of which 3 were waited for; matrix products, arithmetic and copies ran while one was open for 5% of the time, Pallas kernels for 0%

profile of v3, /device:TPU:1, one launch (start us, length us, event | category | flops | bytes accessed | tf_op | source)
XLA Modules:
  0.0 270.8 jit_solution(11181862202261994674)
XLA Ops:
  6.5 2.3 copy.51
  8.9 6.9 %all-to-all-start.2 = ((bf16[128,32,128]{0,2,1:T(8,128)(2,1)}), bf16[128,32,128]{0,2,1:T(8,128)(2,1)S(1)}, u32[]{:S(2)}, u32[]{:S(2)}) async-start(bf16[128,32,128]{0,2,1:T(8,128)(2,1)} %bitcast.12), calls=%async_computation.2 | async-start | bytes 2097152 | tf_op jit(solution)/shard_map/all_to_all | solution.py:37
  15.8 0.7 all-gather.5.cloned.1.call-update
  16.5 1.3 copy.48
  17.8 13.6 %all-to-all-done.2 = bf16[128,32,128]{0,2,1:T(8,128)(2,1)S(1)} async-done(((bf16[128,32,128]{0,2,1:T(8,128)(2,1)}), bf16[128,32,128]{0,2,1:T(8,128)(2,1)S(1)}, u32[]{:S(2)}, u32[]{:S(2)}) %all-to-all-start.2) | async-done | bytes 1048608 | tf_op jit(solution)/shard_map/all_to_all | solution.py:37
  31.5 4.4 %all-to-all-start.1 = ((bf16[128,32,128]{0,2,1:T(8,128)(2,1)}), bf16[128,32,128]{0,2,1:T(8,128)(2,1)S(1)}, u32[]{:S(2)}, u32[]{:S(2)}) async-start(bf16[128,32,128]{0,2,1:T(8,128)(2,1)} %bitcast.7), calls=%async_computation.1 | async-start | bytes 2097152 | tf_op jit(solution)/shard_map/all_to_all | solution.py:36
  35.9 26.0 %all-gather.5.cloned.1.call-done = bf16[1,512,1024]{2,1,0:T(8,128)(2,1)} async-done(((bf16[1,64,1024]{2,1,0:T(8,128)(2,1)}), bf16[1,512,1024]{2,1,0:T(8,128)(2,1)}) %all-gather.5.cloned.1.call-update) | async-done | bytes 1048592 | tf_op jit(solution)/shard_map/all_gather | solution.py:44
  61.9 1.3 copy.53
  63.2 4.5 %collective-permute-start.1 = (bf16[2048,2,128]{2,0,1:T(8,128)(2,1)}, bf16[2048,2,128]{2,0,1:T(8,128)(2,1)}, u32[]{:S(2)}, u32[]{:S(2)}) collective-permute-start(bf16[2048,2,128]{2,0,1:T(8,128)(2,1)} %bitcast.16), channel_id=1, source_target_pairs={{0,16},{16,32},{32,48},{48,64},{64,80},{80,96},{96,112},{112,128},... | collective-permute-start | bytes 3145736 | tf_op jit(solution)/shard_map/ppermute | solution.py:14
  67.8 2.3 copy.45
  70.0 8.2 %all-to-all-start = ((bf16[128,32,128]{0,2,1:T(8,128)(2,1)}), bf16[128,32,128]{0,2,1:T(8,128)(2,1)S(1)}, u32[]{:S(2)}, u32[]{:S(2)}) async-start(bf16[128,32,128]{0,2,1:T(8,128)(2,1)} %bitcast.2), calls=%async_computation | async-start | bytes 2097152 | tf_op jit(solution)/shard_map/all_to_all | solution.py:38
  78.2 1.4 copy.50
  79.6 3.5 %collective-permute-start = (bf16[2048,2,128]{2,0,1:T(8,128)(2,1)}, bf16[2048,2,128]{2,0,1:T(8,128)(2,1)}, u32[]{:S(2)}, u32[]{:S(2)}) collective-permute-start(bf16[2048,2,128]{2,0,1:T(8,128)(2,1)} %bitcast.11), channel_id=1, source_target_pairs={{0,16},{16,32},{32,48},{48,64},{64,80},{80,96},{96,112},{112,128},... | collective-permute-start | bytes 3145736 | tf_op jit(solution)/shard_map/ppermute | solution.py:14
  83.9 44.4 %all-to-all-done = bf16[128,32,128]{0,2,1:T(8,128)(2,1)S(1)} async-done(((bf16[128,32,128]{0,2,1:T(8,128)(2,1)}), bf16[128,32,128]{0,2,1:T(8,128)(2,1)S(1)}, u32[]{:S(2)}, u32[]{:S(2)}) %all-to-all-start) | async-done | bytes 1048608 | tf_op jit(solution)/shard_map/all_to_all | solution.py:38
  128.3 0.7 copy.47
  129.0 3.1 %pad_maximum_fusion.1 = bf16[4096,2,128]{2,0,1:T(8,128)(2,1)} fusion(bf16[2048,2,128]{2,0,1:T(8,128)(2,1)} %bitcast.16, bf16[2048,2,128]{2,0,1:T(8,128)(2,1)} %collective-permute-done.1), kind=kLoop, calls=%fused_computation.60 | loop fusion | flops 4194304 | bytes 4194304 | tf_op jit(solution)/shard_map/concatenate | solution.py:61
  132.1 3.0 %pad_maximum_fusion = bf16[4096,2,128]{2,0,1:T(8,128)(2,1)} fusion(bf16[2048,2,128]{2,0,1:T(8,128)(2,1)} %bitcast.11, bf16[2048,2,128]{2,0,1:T(8,128)(2,1)} %collective-permute-done), kind=kLoop, calls=%fused_computation.59 | loop fusion | flops 4194304 | bytes 4194304 | tf_op jit(solution)/shard_map/concatenate | solution.py:60
  135.1 2.9 %fusion.67 = bf16[1024,512]{0,1:T(8,128)(2,1)S(1)} fusion(bf16[1,1024,1024]{2,1,0:T(8,128)(2,1)} %all-gather.7.cloned.1.call-done, bf16[1024,256]{1,0:T(8,128)(2,1)S(1)} %copy-done.5, bf16[1024,256]{1,0:T(8,128)(2,1)S(1)} %copy-done.6), kind=kOutput, calls=%fused_computation.64 | convolution fusion | flops 1076363264 | bytes 4194304 | tf_op jit(solution)/shard_map/dot_general | solution.py:46
  138.1 1.0 copy.55
  139.4 93.0 %while.12 = (s32[]{:T(128)}, bf16[4,512,2,128]{3,1,0,2:T(8,128)(2,1)S(1)}, s32[1,2048]{1,0:T(1,128)S(1)}, s32[4]{0:T(128)S(1)}, s32[2048]{0:T(1024)S(1)}, /*inde...) while((s32[]{:T(128)}, ...), condition=%wide.region_7.8_spmd.clone.clone, body=%wide.region_2.7_spmd.clone.clone.sunk | while | flops 2745201664 | bytes 95234384 | solution.py:86
  142.8 1.1 fusion.99
  143.8 1.2 fusion.100
  145.1 1.9 fusion.101
  147.0 5.3 %fusion.102 = (f32[2,512]{1,0:T(2,128)S(1)}, f32[2,512,4096]{2,1,0:T(8,128)S(1)}) fusion(pred[512,4096]{1,0:T(8,128)(4,1)S(1)} %concatenate.18, bf16[4096,2,128]{2,0,1:T(8,128)(2,1)} %get-tuple-element.370, bf16[2048,2,128]{2,0,1:T(8,128)(2,1)S(1)} %get-tuple-element.369, s32[]{:T(128)S(6)} %select_n.231), kind=kOutput, calls=%fused_computation.3.clone.1 | convolution fusion | flops 1086323712 | bytes 21237764 | tf_op jit(solution)/shard_map/while/body/eval_jaxpr/qhd,khd->hqk/dot_general | solution.py:18
  152.4 4.6 %fusion.103 = f32[2,512]{1,0:T(2,128)S(1)} fusion(f32[2,512,4096]{2,1,0:T(8,128)S(1)} %get-tuple-element.327, f32[2,512]{1,0:T(2,128)S(1)} %get-tuple-element.328, pred[512,4096]{1,0:T(8,128)(4,1)S(1)} %concatenate.18), kind=kLoop, calls=%fused_computation.4.clone.1 | loop fusion | flops 16776192 | bytes 18882560 | tf_op jit(solution)/shard_map/while/body/eval_jaxpr/reduce_sum | solution.py:22
  157.0 5.6 %fusion.104 = bf16[4,512,2,128]{3,1,0,2:T(8,128)(2,1)S(1)} fusion(bf16[4,512,2,128]{3,1,0,2:T(8,128)(2,1)S(1)} %get-tuple-element.347, s32[]{:T(128)S(6)} %copy.69, f32[512,2,128]{2,0,1:T(8,128)S(1)} %copy-done.7, bf16[4096,2,128]{2,0,1:T(8,128)(2,1)S(1)} %copy-done, f32[2,512,4096]{2,1,0:T(8,128)S(1)} %get-tuple-element.327, ...), kind=kOutput, calls=%fused_computation.23.clone.1 | convolution fusion | flops 1090912256 | bytes 21766148 | tf_op jit(solution)/shard_map/while/body/eval_jaxpr/hqk,khd->qhd/dot_general | solution.py:23
  166.0 1.1 fusion.99
  167.1 1.2 fusion.100
  168.3 1.9 fusion.101
  170.3 5.3 %fusion.102 = (f32[2,512]{1,0:T(2,128)S(1)}, f32[2,512,4096]{2,1,0:T(8,128)S(1)}) fusion(pred[512,4096]{1,0:T(8,128)(4,1)S(1)} %concatenate.18, bf16[4096,2,128]{2,0,1:T(8,128)(2,1)} %get-tuple-element.370, bf16[2048,2,128]{2,0,1:T(8,128)(2,1)S(1)} %get-tuple-element.369, s32[]{:T(128)S(6)} %select_n.231), kind=kOutput, calls=%fused_computation.3.clone.1 | convolution fusion | flops 1086323712 | bytes 21237764 | tf_op jit(solution)/shard_map/while/body/eval_jaxpr/qhd,khd->hqk/dot_general | solution.py:18
  175.6 4.6 %fusion.103 = f32[2,512]{1,0:T(2,128)S(1)} fusion(f32[2,512,4096]{2,1,0:T(8,128)S(1)} %get-tuple-element.327, f32[2,512]{1,0:T(2,128)S(1)} %get-tuple-element.328, pred[512,4096]{1,0:T(8,128)(4,1)S(1)} %concatenate.18), kind=kLoop, calls=%fused_computation.4.clone.1 | loop fusion | flops 16776192 | bytes 18882560 | tf_op jit(solution)/shard_map/while/body/eval_jaxpr/reduce_sum | solution.py:22
  180.3 5.6 %fusion.104 = bf16[4,512,2,128]{3,1,0,2:T(8,128)(2,1)S(1)} fusion(bf16[4,512,2,128]{3,1,0,2:T(8,128)(2,1)S(1)} %get-tuple-element.347, s32[]{:T(128)S(6)} %copy.69, f32[512,2,128]{2,0,1:T(8,128)S(1)} %copy-done.7, bf16[4096,2,128]{2,0,1:T(8,128)(2,1)S(1)} %copy-done, f32[2,512,4096]{2,1,0:T(8,128)S(1)} %get-tuple-element.327, ...), kind=kOutput, calls=%fused_computation.23.clone.1 | convolution fusion | flops 1090912256 | bytes 21766148 | tf_op jit(solution)/shard_map/while/body/eval_jaxpr/hqk,khd->qhd/dot_general | solution.py:23
  189.3 1.1 fusion.99
  190.4 1.2 fusion.100
  191.6 1.9 fusion.101
  193.5 5.3 %fusion.102 = (f32[2,512]{1,0:T(2,128)S(1)}, f32[2,512,4096]{2,1,0:T(8,128)S(1)}) fusion(pred[512,4096]{1,0:T(8,128)(4,1)S(1)} %concatenate.18, bf16[4096,2,128]{2,0,1:T(8,128)(2,1)} %get-tuple-element.370, bf16[2048,2,128]{2,0,1:T(8,128)(2,1)S(1)} %get-tuple-element.369, s32[]{:T(128)S(6)} %select_n.231), kind=kOutput, calls=%fused_computation.3.clone.1 | convolution fusion | flops 1086323712 | bytes 21237764 | tf_op jit(solution)/shard_map/while/body/eval_jaxpr/qhd,khd->hqk/dot_general | solution.py:18
  198.9 4.6 %fusion.103 = f32[2,512]{1,0:T(2,128)S(1)} fusion(f32[2,512,4096]{2,1,0:T(8,128)S(1)} %get-tuple-element.327, f32[2,512]{1,0:T(2,128)S(1)} %get-tuple-element.328, pred[512,4096]{1,0:T(8,128)(4,1)S(1)} %concatenate.18), kind=kLoop, calls=%fused_computation.4.clone.1 | loop fusion | flops 16776192 | bytes 18882560 | tf_op jit(solution)/shard_map/while/body/eval_jaxpr/reduce_sum | solution.py:22
  203.6 5.6 %fusion.104 = bf16[4,512,2,128]{3,1,0,2:T(8,128)(2,1)S(1)} fusion(bf16[4,512,2,128]{3,1,0,2:T(8,128)(2,1)S(1)} %get-tuple-element.347, s32[]{:T(128)S(6)} %copy.69, f32[512,2,128]{2,0,1:T(8,128)S(1)} %copy-done.7, bf16[4096,2,128]{2,0,1:T(8,128)(2,1)S(1)} %copy-done, f32[2,512,4096]{2,1,0:T(8,128)S(1)} %get-tuple-element.327, ...), kind=kOutput, calls=%fused_computation.23.clone.1 | convolution fusion | flops 1090912256 | bytes 21766148 | tf_op jit(solution)/shard_map/while/body/eval_jaxpr/hqk,khd->qhd/dot_general | solution.py:23
  212.6 1.1 fusion.99
  213.6 1.2 fusion.100
  214.9 1.9 fusion.101
  216.8 5.3 %fusion.102 = (f32[2,512]{1,0:T(2,128)S(1)}, f32[2,512,4096]{2,1,0:T(8,128)S(1)}) fusion(pred[512,4096]{1,0:T(8,128)(4,1)S(1)} %concatenate.18, bf16[4096,2,128]{2,0,1:T(8,128)(2,1)} %get-tuple-element.370, bf16[2048,2,128]{2,0,1:T(8,128)(2,1)S(1)} %get-tuple-element.369, s32[]{:T(128)S(6)} %select_n.231), kind=kOutput, calls=%fused_computation.3.clone.1 | convolution fusion | flops 1086323712 | bytes 21237764 | tf_op jit(solution)/shard_map/while/body/eval_jaxpr/qhd,khd->hqk/dot_general | solution.py:18
  222.2 4.6 %fusion.103 = f32[2,512]{1,0:T(2,128)S(1)} fusion(f32[2,512,4096]{2,1,0:T(8,128)S(1)} %get-tuple-element.327, f32[2,512]{1,0:T(2,128)S(1)} %get-tuple-element.328, pred[512,4096]{1,0:T(8,128)(4,1)S(1)} %concatenate.18), kind=kLoop, calls=%fused_computation.4.clone.1 | loop fusion | flops 16776192 | bytes 18882560 | tf_op jit(solution)/shard_map/while/body/eval_jaxpr/reduce_sum | solution.py:22
  226.8 5.6 %fusion.104 = bf16[4,512,2,128]{3,1,0,2:T(8,128)(2,1)S(1)} fusion(bf16[4,512,2,128]{3,1,0,2:T(8,128)(2,1)S(1)} %get-tuple-element.347, s32[]{:T(128)S(6)} %copy.69, f32[512,2,128]{2,0,1:T(8,128)S(1)} %copy-done.7, bf16[4096,2,128]{2,0,1:T(8,128)(2,1)S(1)} %copy-done, f32[2,512,4096]{2,1,0:T(8,128)S(1)} %get-tuple-element.327, ...), kind=kOutput, calls=%fused_computation.23.clone.1 | convolution fusion | flops 1090912256 | bytes 21766148 | tf_op jit(solution)/shard_map/while/body/eval_jaxpr/hqk,khd->qhd/dot_general | solution.py:23
  232.4 8.9 %copy.57 = bf16[2048,2,128]{2,1,0:T(2,128)(2,1)S(1)} copy(bf16[2048,2,128]{2,0,1:T(8,128)(2,1)S(1)} %bitcast.106) | data formatting | bytes 2097152 | tf_op jit(solution)/shard_map/reshape | solution.py:87
  241.3 20.6 %all_to_all.69 = bf16[2048,2,128]{2,1,0:T(2,128)(2,1)S(1)} all-to-all(bf16[2048,2,128]{2,1,0:T(2,128)(2,1)S(1)} %copy.57), channel_id=1, replica_groups=mesh['span'=16,'chip'=8,'core'=2] {'chip','core'}, dimensions={0} | all-to-all | bytes 2097152 | tf_op jit(solution)/shard_map/all_to_all | solution.py:88
  262.0 0.7 copy.59
  262.7 1.3 copy.60
  (80 shorter events, 11.5 us)
Async XLA Ops:
  6.5 10.0 %copy-start.1 = (bf16[1,128,4096]{2,1,0:T(8,128)(2,1)S(1)}, bf16[1,128,4096]{2,1,0:T(8,128)(2,1)}, u32[]{:S(2)}) copy-start(bf16[1,128,4096]{2,1,0:T(8,128)(2,1)} %param.12) | copy-start | bytes 3145732
  8.9 22.6 %all-to-all-start.2 = ((bf16[128,32,128]{0,2,1:T(8,128)(2,1)}), bf16[128,32,128]{0,2,1:T(8,128)(2,1)S(1)}, u32[]{:S(2)}, u32[]{:S(2)}) async-start(bf16[128,32,128]{0,2,1:T(8,128)(2,1)} %bitcast.12), calls=%async_computation.2 | async-start | bytes 2097152 | tf_op jit(solution)/shard_map/all_to_all | solution.py:37
  15.8 46.1 %all-gather.5.cloned.1.call-start = ((), (), s32[]{:S(2)}) async-start(), calls=%async_computation.4 | async-start | bytes 1179648 | tf_op jit(solution)/shard_map/all_gather | solution.py:44
  31.5 38.6 %all-to-all-start.1 = ((bf16[128,32,128]{0,2,1:T(8,128)(2,1)}), bf16[128,32,128]{0,2,1:T(8,128)(2,1)S(1)}, u32[]{:S(2)}, u32[]{:S(2)}) async-start(bf16[128,32,128]{0,2,1:T(8,128)(2,1)} %bitcast.7), calls=%async_computation.1 | async-start | bytes 2097152 | tf_op jit(solution)/shard_map/all_to_all | solution.py:36
  35.9 99.2 %all-gather.7.cloned.1.call-start = ((), (), s32[]{:S(2)}) async-start(), calls=%async_computation.5 | async-start | bytes 3145728 | tf_op jit(solution)/shard_map/all_gather | solution.py:45
  61.9 21.9 %copy-start.4 = (s32[1,16,2]{1,2,0:T(2,128)S(1)}, s32[1,16,2]{1,2,0:T(2,128)}, u32[]{:S(2)}) copy-start(s32[1,16,2]{1,2,0:T(2,128)} %param.18) | copy-start | bytes 388
  61.9 21.9 %copy-start.3 = (s32[1,2048]{1,0:T(1,128)S(1)}, s32[1,2048]{1,0:T(1,128)}, u32[]{:S(2)}) copy-start(s32[1,2048]{1,0:T(1,128)} %param.17) | copy-start | bytes 24580
  63.2 65.7 %collective-permute-start.1 = (bf16[2048,2,128]{2,0,1:T(8,128)(2,1)}, bf16[2048,2,128]{2,0,1:T(8,128)(2,1)}, u32[]{:S(2)}, u32[]{:S(2)}) collective-permute-start(bf16[2048,2,128]{2,0,1:T(8,128)(2,1)} %bitcast.16), channel_id=1, source_target_pairs={{0,16},{16,32},{32,48},{48,64},{64,80},{80,96},{96,112},{112,128},... | collective-permute-start | bytes 3145736 | tf_op jit(solution)/shard_map/ppermute | solution.py:14
  70.0 58.3 %all-to-all-start = ((bf16[128,32,128]{0,2,1:T(8,128)(2,1)}), bf16[128,32,128]{0,2,1:T(8,128)(2,1)S(1)}, u32[]{:S(2)}, u32[]{:S(2)}) async-start(bf16[128,32,128]{0,2,1:T(8,128)(2,1)} %bitcast.2), calls=%async_computation | async-start | bytes 2097152 | tf_op jit(solution)/shard_map/all_to_all | solution.py:38
  79.6 52.5 %collective-permute-start = (bf16[2048,2,128]{2,0,1:T(8,128)(2,1)}, bf16[2048,2,128]{2,0,1:T(8,128)(2,1)}, u32[]{:S(2)}, u32[]{:S(2)}) collective-permute-start(bf16[2048,2,128]{2,0,1:T(8,128)(2,1)} %bitcast.11), channel_id=1, source_target_pairs={{0,16},{16,32},{32,48},{48,64},{64,80},{80,96},{96,112},{112,128},... | collective-permute-start | bytes 3145736 | tf_op jit(solution)/shard_map/ppermute | solution.py:14
  129.0 6.1 %copy-start.5 = (bf16[1024,256]{1,0:T(8,128)(2,1)S(1)}, bf16[1024,256]{1,0:T(8,128)(2,1)}, u32[]{:S(2)}) copy-start(bf16[1024,256]{1,0:T(8,128)(2,1)} %param.16) | copy-start | bytes 1572868
  129.0 6.1 %copy-start.6 = (bf16[1024,256]{1,0:T(8,128)(2,1)S(1)}, bf16[1024,256]{1,0:T(8,128)(2,1)}, u32[]{:S(2)}) copy-start(bf16[1024,256]{1,0:T(8,128)(2,1)} %param.15) | copy-start | bytes 1572868
  142.8 2.3 copy-start.2
  152.4 4.7 %copy-start = (bf16[4096,2,128]{2,0,1:T(8,128)(2,1)S(1)}, bf16[4096,2,128]{2,0,1:T(8,128)(2,1)}, u32[]{:S(2)}) copy-start(bf16[4096,2,128]{2,0,1:T(8,128)(2,1)} %get-tuple-element.371) | copy-start | bytes 6291460 | tf_op jit(solution)/shard_map/while
  152.4 4.7 %copy-start.7 = (f32[512,2,128]{2,0,1:T(8,128)S(1)}, f32[512,2,128]{2,0,1:T(8,128)}, u32[]{:S(2)}) copy-start(f32[512,2,128]{2,0,1:T(8,128)} %fusion.101) | copy-start | bytes 1572868 | tf_op jit(solution)/shard_map/while
  166.0 2.3 copy-start.2
  175.6 4.7 %copy-start = (bf16[4096,2,128]{2,0,1:T(8,128)(2,1)S(1)}, bf16[4096,2,128]{2,0,1:T(8,128)(2,1)}, u32[]{:S(2)}) copy-start(bf16[4096,2,128]{2,0,1:T(8,128)(2,1)} %get-tuple-element.371) | copy-start | bytes 6291460 | tf_op jit(solution)/shard_map/while
  175.6 4.7 %copy-start.7 = (f32[512,2,128]{2,0,1:T(8,128)S(1)}, f32[512,2,128]{2,0,1:T(8,128)}, u32[]{:S(2)}) copy-start(f32[512,2,128]{2,0,1:T(8,128)} %fusion.101) | copy-start | bytes 1572868 | tf_op jit(solution)/shard_map/while
  189.3 2.3 copy-start.2
  198.9 4.7 %copy-start = (bf16[4096,2,128]{2,0,1:T(8,128)(2,1)S(1)}, bf16[4096,2,128]{2,0,1:T(8,128)(2,1)}, u32[]{:S(2)}) copy-start(bf16[4096,2,128]{2,0,1:T(8,128)(2,1)} %get-tuple-element.371) | copy-start | bytes 6291460 | tf_op jit(solution)/shard_map/while
  198.9 4.7 %copy-start.7 = (f32[512,2,128]{2,0,1:T(8,128)S(1)}, f32[512,2,128]{2,0,1:T(8,128)}, u32[]{:S(2)}) copy-start(f32[512,2,128]{2,0,1:T(8,128)} %fusion.101) | copy-start | bytes 1572868 | tf_op jit(solution)/shard_map/while
  212.5 2.3 copy-start.2
  222.1 4.7 %copy-start = (bf16[4096,2,128]{2,0,1:T(8,128)(2,1)S(1)}, bf16[4096,2,128]{2,0,1:T(8,128)(2,1)}, u32[]{:S(2)}) copy-start(bf16[4096,2,128]{2,0,1:T(8,128)(2,1)} %get-tuple-element.371) | copy-start | bytes 6291460 | tf_op jit(solution)/shard_map/while
  222.1 4.7 %copy-start.7 = (f32[512,2,128]{2,0,1:T(8,128)S(1)}, f32[512,2,128]{2,0,1:T(8,128)}, u32[]{:S(2)}) copy-start(f32[512,2,128]{2,0,1:T(8,128)} %fusion.101) | copy-start | bytes 1572868 | tf_op jit(solution)/shard_map/while
Sparse Core Ops, SparseCore 0:
  18.4 43.4 all-gather.4
  63.7 21.1 all-gather.6

commit v4 on v3

--- a/solution.py
+++ b/solution.py
@@ -40,17 +40,6 @@
     prev_kh, prev_vh = shifted((k_heads, v_heads), "span", 1)
     span_rows = q_heads.shape[0]
     head_count = q_heads.shape[1]
-    joint_w = jnp.concatenate([audio_wk, audio_wv], axis=1)
-    own = lax.all_gather(audio[0], "chip", axis=0, tiled=True)
-    gathered = lax.all_gather(own, "core", axis=0, tiled=True)
-    projected = jnp.dot(
-        gathered,
-        joint_w,
-        preferred_element_type=jnp.float32,
-    ).astype(jnp.bfloat16)[None][0]
-    aud_rows = projected.shape[0]
-    audio_keys = projected[:, : head_count * HD].reshape(aud_rows, head_count, HD)
-    audio_vals = projected[:, head_count * HD :].reshape(aud_rows, head_count, HD)
     has_prev = jnp.logical_and(lax.axis_index("span") > 0, video_start[0] == 0)
     frames = frame_ids[0]
     table = windows[0]
@@ -59,31 +48,44 @@
     upper = jnp.sum(jnp.where(onehot, table[None, :, 1], 0), axis=1)
     all_keys = jnp.concatenate([prev_kh, k_heads], axis=0)
     all_vals = jnp.concatenate([prev_vh, v_heads], axis=0)
-    cores = lax.axis_size("core")
-    chips = lax.axis_size("chip")
-    piece = aud_rows // (cores * chips)
-    order = jnp.arange(aud_rows, dtype=jnp.int32)
-    held_core, held_chip, row = order // (chips * piece), (order // piece) % chips, order % piece
-    positions = (held_chip * cores + held_core) * piece + row
     block = min(512, span_rows)
 
-    def one_block(index):
+    def self_block(index):
         begin = index * block
         q_block = lax.dynamic_slice_in_dim(q_heads, begin, block, 0)
         f_block = lax.dynamic_slice_in_dim(frames, begin, block, 0)
-        lo_block = lax.dynamic_slice_in_dim(lower, begin, block, 0)
-        hi_block = lax.dynamic_slice_in_dim(upper, begin, block, 0)
         own = frames[None, :] <= f_block[:, None]
         before = jnp.broadcast_to(has_prev, (block, span_rows))
         self_mask = jnp.concatenate([before, own], axis=1)
+        return attend(q_block, all_keys, all_vals, self_mask, scale)
+
+    self_out = lax.map(self_block, jnp.arange(span_rows // block, dtype=jnp.int32))
+
+    audio_late = lax.optimization_barrier((audio, q_heads, k_heads, v_heads))[0]
+    joint_w = jnp.concatenate([audio_wk, audio_wv], axis=1)
+    gathered = lax.all_gather(audio_late[0], SEQ, axis=0, tiled=True)
+    projected = jnp.dot(
+        gathered,
+        joint_w,
+        preferred_element_type=jnp.float32,
+    ).astype(jnp.bfloat16)
+    aud_rows = projected.shape[0]
+    audio_keys = projected[:, : head_count * HD].reshape(aud_rows, head_count, HD)
+    audio_vals = projected[:, head_count * HD :].reshape(aud_rows, head_count, HD)
+    positions = jnp.arange(aud_rows, dtype=jnp.int32)
+
+    def audio_block(index):
+        begin = index * block
+        q_block = lax.dynamic_slice_in_dim(q_heads, begin, block, 0)
+        lo_block = lax.dynamic_slice_in_dim(lower, begin, block, 0)
+        hi_block = lax.dynamic_slice_in_dim(upper, begin, block, 0)
         audio_mask = jnp.logical_and(
             positions[None, :] >= lo_block[:, None], positions[None, :] < hi_block[:, None]
         )
-        self_out = attend(q_block, all_keys, all_vals, self_mask, scale)
         audio_out = attend(q_block, audio_keys, audio_vals, audio_mask, scale)
-        return (self_out + audio_out).astype(jnp.bfloat16)
+        return (self_out[index] + audio_out).astype(jnp.bfloat16)
 
-    blocks = lax.map(one_block, jnp.arange(span_rows // block, dtype=jnp.int32))
+    blocks = lax.map(audio_block, jnp.arange(span_rows // block, dtype=jnp.int32))
     mixed = blocks.reshape(span_rows, head_count, HD)
     back = lax.all_to_all(mixed, SEQ, split_axis=0, concat_axis=1, tiled=True)
     return back.reshape(1, tok_rows, HEADS * HD)

time: 272 us -> 287 us (1.055)
  loops' own time: 3.14 us -> 13.9 us
  matrix products: 58.5 us -> 64.1 us
  starting transfers between devices: 27.6 us -> 22.6 us
  local copies, waits for them, and re-layouts: 27.8 us -> 30.7 us
    all_to_all x1, waiting for transfers between devices: 13.6 us -> 53.2 us  [local(): lax.all_to_all(v_local, SEQ, split_axis=1, concat_axis=0, tiled=True)]
    all_to_all x1, waiting for transfers between devices: 44.4 us -> 11.3 us  [local(): lax.all_to_all(q_local, SEQ, split_axis=1, concat_axis=0, tiled=True)]
    all_gather x2 -> x1, waiting for transfers between devices: 26 us -> 0.01 us  [local(): gathered = lax.all_gather(audio_late[0], SEQ, axis=0, tiled=True)]
    all_to_all x1, waiting for transfers between devices: 0.01 us -> 14.3 us  [local(): lax.all_to_all(k_local, SEQ, split_axis=1, concat_axis=0, tiled=True)]
    another operation x1 -> x2, loops' own time: 3.14 us -> 13.9 us  [the longest x1 10.9 us: local(): lax.map(audio_block, jnp.arange(span_rows // block, dtype=jnp.int32))]
    dot_general x8, matrix products: 30 us -> 40.6 us  [attend(): jnp.einsum('hqk,khd->qhd', weights.astype(jnp.bfloat16), value_rows, pref...]
    while x24, local copies, waits for them, and re-layouts: 0.06 us -> 7.8 us
    ppermute x2, waiting for transfers between devices: 0.01 us -> 6.3 us  [shifted(): lax.ppermute(value, axis, [(source, source + steps) for source in range(l...]
  transfers between devices with their start and end apart: 7 -> 6, of which waited for: 3 -> 4; matrix products, arithmetic and copies ran while one was open for 5% -> 28% of each run, Pallas kernels for 0% -> 0%
where the time goes in v4:
time: 287 us; the launch traced here: 286 us
  waiting for transfers between devices  85.1 us (30%)
  matrix products  64.1 us (22%)
  other arithmetic  33.9 us (12%)
  local copies, waits for them, and re-layouts  30.7 us (11%)
  starting transfers between devices  22.6 us (8%)
  blocking collectives  21.2 us (7%)
  between operations  14.2 us (5%)
  loops' own time  13.9 us (5%)
    all_to_all x1, waiting for transfers between devices, local(): lax.all_to_all(v_local, SEQ, split_axis=1, concat_axis=0, tiled=True)  53.2 us
    dot_general x8, matrix products, attend(): jnp.einsum('hqk,khd->qhd', weights.astype(jnp.bfloat16), value_rows, pref...  40.6 us
    reduce_sum x8, other arithmetic, attend(): den = jnp.sum(weights, axis=-1, keepdims=True)  23.3 us
    all_to_all x1, blocking collectives, local(): back = lax.all_to_all(mixed, SEQ, split_axis=0, concat_axis=1, tiled=True)  21.2 us
    dot_general x8, matrix products, attend(): jnp.einsum('qhd,khd->hqk', query, key_rows, preferred_element_type=jnp.fl...  20.4 us
    all_to_all x1, waiting for transfers between devices, local(): lax.all_to_all(k_local, SEQ, split_axis=1, concat_axis=0, tiled=True)  14.3 us
    all_to_all x1, waiting for transfers between devices, local(): lax.all_to_all(q_local, SEQ, split_axis=1, concat_axis=0, tiled=True)  11.3 us
    another operation x1, loops' own time, local(): lax.map(audio_block, jnp.arange(span_rows // block, dtype=jnp.int32))  10.9 us
  transfers between devices with their start and end apart: 6, of which 4 were waited for; matrix products, arithmetic and copies ran while one was open for 28% of the time, Pallas kernels for 0%

profile of v4, /device:TPU:1, one launch (start us, length us, event | category | flops | bytes accessed | tf_op | source)
XLA Modules:
  0.0 285.7 jit_solution(13055591604796634604)
XLA Ops:
  6.5 2.3 copy.48
  8.9 6.9 %all-to-all-start.1 = ((bf16[128,32,128]{0,2,1:T(8,128)(2,1)}), bf16[128,32,128]{0,2,1:T(8,128)(2,1)S(1)}, u32[]{:S(2)}, u32[]{:S(2)}) async-start(bf16[128,32,128]{0,2,1:T(8,128)(2,1)} %bitcast.14), calls=%async_computation.1 | async-start | bytes 2097152 | tf_op jit(solution)/shard_map/all_to_all | solution.py:36
  15.8 1.3 copy.51
  17.1 14.3 %all-to-all-done.1 = bf16[128,32,128]{0,2,1:T(8,128)(2,1)S(1)} async-done(((bf16[128,32,128]{0,2,1:T(8,128)(2,1)}), bf16[128,32,128]{0,2,1:T(8,128)(2,1)S(1)}, u32[]{:S(2)}, u32[]{:S(2)}) %all-to-all-start.1) | async-done | bytes 1048608 | tf_op jit(solution)/shard_map/all_to_all | solution.py:36
  31.5 4.4 %all-to-all-start.2 = ((bf16[128,32,128]{0,2,1:T(8,128)(2,1)}), bf16[128,32,128]{0,2,1:T(8,128)(2,1)S(1)}, u32[]{:S(2)}, u32[]{:S(2)}) async-start(bf16[128,32,128]{0,2,1:T(8,128)(2,1)} %bitcast.19), calls=%async_computation.2 | async-start | bytes 2097152 | tf_op jit(solution)/shard_map/all_to_all | solution.py:37
  36.6 4.5 %collective-permute-start = (bf16[2048,2,128]{2,0,1:T(8,128)(2,1)S(1)}, bf16[2048,2,128]{2,0,1:T(8,128)(2,1)}, u32[]{:S(2)}, u32[]{:S(2)}) collective-permute-start(bf16[2048,2,128]{2,0,1:T(8,128)(2,1)S(1)} %bitcast.117), channel_id=1, source_target_pairs={{0,16},{16,32},{32,48},{48,64},{64,80},{80,96},{96,112},{112,128},... | collective-permute-start | bytes 3145736 | tf_op jit(solution)/shard_map/ppermute | solution.py:14
  41.1 2.3 copy.45
  43.3 53.2 %all-to-all-done.2 = bf16[128,32,128]{0,2,1:T(8,128)(2,1)S(1)} async-done(((bf16[128,32,128]{0,2,1:T(8,128)(2,1)}), bf16[128,32,128]{0,2,1:T(8,128)(2,1)S(1)}, u32[]{:S(2)}, u32[]{:S(2)}) %all-to-all-start.2) | async-done | bytes 1048608 | tf_op jit(solution)/shard_map/all_to_all | solution.py:37
  96.6 4.4 %all-to-all-start = ((bf16[128,32,128]{0,2,1:T(8,128)(2,1)}), bf16[128,32,128]{0,2,1:T(8,128)(2,1)S(1)}, u32[]{:S(2)}, u32[]{:S(2)}) async-start(bf16[128,32,128]{0,2,1:T(8,128)(2,1)} %bitcast.9), calls=%async_computation | async-start | bytes 2097152 | tf_op jit(solution)/shard_map/all_to_all | solution.py:38
  101.0 1.3 copy.53
  102.3 2.3 collective-permute-start.1
  105.5 11.3 %all-to-all-done = bf16[128,32,128]{0,2,1:T(8,128)(2,1)S(1)} async-done(((bf16[128,32,128]{0,2,1:T(8,128)(2,1)}), bf16[128,32,128]{0,2,1:T(8,128)(2,1)S(1)}, u32[]{:S(2)}, u32[]{:S(2)}) %all-to-all-start) | async-done | bytes 1048608 | tf_op jit(solution)/shard_map/all_to_all | solution.py:38
  117.4 2.8 pad_maximum_fusion
  120.2 6.3 %collective-permute-done.1 = bf16[2048,2,128]{2,0,1:T(8,128)(2,1)} collective-permute-done((bf16[2048,2,128]{2,0,1:T(8,128)(2,1)}, bf16[2048,2,128]{2,0,1:T(8,128)(2,1)}, u32[]{:S(2)}, u32[]{:S(2)}) %collective-permute-start.1) | collective-permute-done | bytes 1048608 | tf_op jit(solution)/shard_map/ppermute | solution.py:14
  126.5 2.7 pad_maximum_fusion.1
  129.2 70.0 %while.22 = (s32[]{:T(128)}, f32[4,512,2,128]{3,1,2,0:T(8,128)}, s32[1,2048]{1,0:T(1,128)S(1)}, s32[4]{0:T(128)S(1)}, s32[2048]{0:T(1024)S(1)}, /*index=5*/pred[...) while((s32[]{:T(128)}, f32[4,512,2,128]{3,1,2,0:T(8,128)}, ...), condition=%wide.region_5.6_spmd, body=%wide.region_2.5_spmd.sunk | while | flops 2194798592 | bytes 82610936 | solution.py:62
  132.0 4.0 %fusion.85 = (f32[2,512]{1,0:T(2,128)S(1)}, f32[2,512,4096]{2,1,0:T(8,128)S(1)}) fusion(pred[512,4096]{1,0:T(8,128)(4,1)S(1)} %concatenate.16, bf16[4096,2,128]{2,0,1:T(8,128)(2,1)S(1)} %copy-done.2, bf16[2048,2,128]{2,0,1:T(8,128)(2,1)S(1)} %get-tuple-element.396, s32[]{:T(128)S(6)} %select_n.89), kind=kOutput, calls=%fused_computation.3.clone.1 | convolution fusion | flops 1086323712 | bytes 21237764 | tf_op jit(solution)/shard_map/while/body/eval_jaxpr/qhd,khd->hqk/dot_general | solution.py:18
  136.0 4.6 %fusion.86 = f32[2,512]{1,0:T(2,128)S(1)} fusion(f32[2,512,4096]{2,1,0:T(8,128)S(1)} %get-tuple-element.351, f32[2,512]{1,0:T(2,128)S(1)} %get-tuple-element.352, pred[512,4096]{1,0:T(8,128)(4,1)S(1)} %concatenate.16), kind=kLoop, calls=%fused_computation.4.clone.1 | loop fusion | flops 16776192 | bytes 18882560 | tf_op jit(solution)/shard_map/while/body/eval_jaxpr/reduce_sum | solution.py:22
  140.7 6.0 %fusion.87 = f32[4,512,2,128]{3,1,2,0:T(8,128)} fusion(f32[4,512,2,128]{3,1,2,0:T(8,128)} %get-tuple-element.378, s32[]{:T(128)} %get-tuple-element.377, bf16[4096,2,128]{2,0,1:T(8,128)(2,1)S(1)} %copy-done.3, f32[2,512,4096]{2,1,0:T(8,128)S(1)} %get-tuple-element.351, f32[2,512]{1,0:T(2,128)S(1)} %get-tuple-element.352, ...), kind=kOutput, calls=%fused_computation.12.clone.1 | convolution fusion | flops 1090650112 | bytes 21504512 | tf_op jit(solution)/shard_map/while/body/eval_jaxpr/hqk,khd->qhd/dot_general | solution.py:23
  149.4 4.0 %fusion.85 = (f32[2,512]{1,0:T(2,128)S(1)}, f32[2,512,4096]{2,1,0:T(8,128)S(1)}) fusion(pred[512,4096]{1,0:T(8,128)(4,1)S(1)} %concatenate.16, bf16[4096,2,128]{2,0,1:T(8,128)(2,1)S(1)} %copy-done.2, bf16[2048,2,128]{2,0,1:T(8,128)(2,1)S(1)} %get-tuple-element.396, s32[]{:T(128)S(6)} %select_n.89), kind=kOutput, calls=%fused_computation.3.clone.1 | convolution fusion | flops 1086323712 | bytes 21237764 | tf_op jit(solution)/shard_map/while/body/eval_jaxpr/qhd,khd->hqk/dot_general | solution.py:18
  153.5 4.6 %fusion.86 = f32[2,512]{1,0:T(2,128)S(1)} fusion(f32[2,512,4096]{2,1,0:T(8,128)S(1)} %get-tuple-element.351, f32[2,512]{1,0:T(2,128)S(1)} %get-tuple-element.352, pred[512,4096]{1,0:T(8,128)(4,1)S(1)} %concatenate.16), kind=kLoop, calls=%fused_computation.4.clone.1 | loop fusion | flops 16776192 | bytes 18882560 | tf_op jit(solution)/shard_map/while/body/eval_jaxpr/reduce_sum | solution.py:22
  158.1 6.0 %fusion.87 = f32[4,512,2,128]{3,1,2,0:T(8,128)} fusion(f32[4,512,2,128]{3,1,2,0:T(8,128)} %get-tuple-element.378, s32[]{:T(128)} %get-tuple-element.377, bf16[4096,2,128]{2,0,1:T(8,128)(2,1)S(1)} %copy-done.3, f32[2,512,4096]{2,1,0:T(8,128)S(1)} %get-tuple-element.351, f32[2,512]{1,0:T(2,128)S(1)} %get-tuple-element.352, ...), kind=kOutput, calls=%fused_computation.12.clone.1 | convolution fusion | flops 1090650112 | bytes 21504512 | tf_op jit(solution)/shard_map/while/body/eval_jaxpr/hqk,khd->qhd/dot_general | solution.py:23
  166.9 4.0 %fusion.85 = (f32[2,512]{1,0:T(2,128)S(1)}, f32[2,512,4096]{2,1,0:T(8,128)S(1)}) fusion(pred[512,4096]{1,0:T(8,128)(4,1)S(1)} %concatenate.16, bf16[4096,2,128]{2,0,1:T(8,128)(2,1)S(1)} %copy-done.2, bf16[2048,2,128]{2,0,1:T(8,128)(2,1)S(1)} %get-tuple-element.396, s32[]{:T(128)S(6)} %select_n.89), kind=kOutput, calls=%fused_computation.3.clone.1 | convolution fusion | flops 1086323712 | bytes 21237764 | tf_op jit(solution)/shard_map/while/body/eval_jaxpr/qhd,khd->hqk/dot_general | solution.py:18
  171.0 4.6 %fusion.86 = f32[2,512]{1,0:T(2,128)S(1)} fusion(f32[2,512,4096]{2,1,0:T(8,128)S(1)} %get-tuple-element.351, f32[2,512]{1,0:T(2,128)S(1)} %get-tuple-element.352, pred[512,4096]{1,0:T(8,128)(4,1)S(1)} %concatenate.16), kind=kLoop, calls=%fused_computation.4.clone.1 | loop fusion | flops 16776192 | bytes 18882560 | tf_op jit(solution)/shard_map/while/body/eval_jaxpr/reduce_sum | solution.py:22
  175.6 6.0 %fusion.87 = f32[4,512,2,128]{3,1,2,0:T(8,128)} fusion(f32[4,512,2,128]{3,1,2,0:T(8,128)} %get-tuple-element.378, s32[]{:T(128)} %get-tuple-element.377, bf16[4096,2,128]{2,0,1:T(8,128)(2,1)S(1)} %copy-done.3, f32[2,512,4096]{2,1,0:T(8,128)S(1)} %get-tuple-element.351, f32[2,512]{1,0:T(2,128)S(1)} %get-tuple-element.352, ...), kind=kOutput, calls=%fused_computation.12.clone.1 | convolution fusion | flops 1090650112 | bytes 21504512 | tf_op jit(solution)/shard_map/while/body/eval_jaxpr/hqk,khd->qhd/dot_general | solution.py:23
  184.4 4.0 %fusion.85 = (f32[2,512]{1,0:T(2,128)S(1)}, f32[2,512,4096]{2,1,0:T(8,128)S(1)}) fusion(pred[512,4096]{1,0:T(8,128)(4,1)S(1)} %concatenate.16, bf16[4096,2,128]{2,0,1:T(8,128)(2,1)S(1)} %copy-done.2, bf16[2048,2,128]{2,0,1:T(8,128)(2,1)S(1)} %get-tuple-element.396, s32[]{:T(128)S(6)} %select_n.89), kind=kOutput, calls=%fused_computation.3.clone.1 | convolution fusion | flops 1086323712 | bytes 21237764 | tf_op jit(solution)/shard_map/while/body/eval_jaxpr/qhd,khd->hqk/dot_general | solution.py:18
  188.5 4.6 %fusion.86 = f32[2,512]{1,0:T(2,128)S(1)} fusion(f32[2,512,4096]{2,1,0:T(8,128)S(1)} %get-tuple-element.351, f32[2,512]{1,0:T(2,128)S(1)} %get-tuple-element.352, pred[512,4096]{1,0:T(8,128)(4,1)S(1)} %concatenate.16), kind=kLoop, calls=%fused_computation.4.clone.1 | loop fusion | flops 16776192 | bytes 18882560 | tf_op jit(solution)/shard_map/while/body/eval_jaxpr/reduce_sum | solution.py:22
  193.1 6.0 %fusion.87 = f32[4,512,2,128]{3,1,2,0:T(8,128)} fusion(f32[4,512,2,128]{3,1,2,0:T(8,128)} %get-tuple-element.378, s32[]{:T(128)} %get-tuple-element.377, bf16[4096,2,128]{2,0,1:T(8,128)(2,1)S(1)} %copy-done.3, f32[2,512,4096]{2,1,0:T(8,128)S(1)} %get-tuple-element.351, f32[2,512]{1,0:T(2,128)S(1)} %get-tuple-element.352, ...), kind=kOutput, calls=%fused_computation.12.clone.1 | convolution fusion | flops 1090650112 | bytes 21504512 | tf_op jit(solution)/shard_map/while/body/eval_jaxpr/hqk,khd->qhd/dot_general | solution.py:23
  199.2 3.1 %fusion.57 = bf16[1024,512]{0,1:T(8,128)(2,1)S(1)} fusion(bf16[1,1024,1024]{2,1,0:T(8,128)(2,1)} %all-gather.3.cloned.1.call-done, bf16[1024,256]{1,0:T(8,128)(2,1)} %param.18, bf16[1024,256]{1,0:T(8,128)(2,1)} %param.17), kind=kOutput, calls=%fused_computation.43 | convolution fusion | flops 1076363264 | bytes 4194304 | tf_op jit(solution)/shard_map/dot_general | solution.py:67
  202.9 49.7 %while.23 = (s32[]{:T(128)}, bf16[4,512,2,128]{3,1,0,2:T(8,128)(2,1)}, s32[4]{0:T(128)S(1)}, f32[4,512,2,128]{3,1,2,0:T(8,128)}, s32[2048]{0:T(1024)S(1)}, /*ind...) while((s32[]{:T(128)}, ...), condition=%wide.region_9.10_spmd.clone.clone, body=%wide.region_6.9_spmd.clone.clone.sunk | while | flops 550369280 | bytes 33587980 | solution.py:88
  206.1 1.9 copy-done
  208.0 1.2 fusion.93
  211.2 4.1 %fusion.94 = bf16[4,512,2,128]{3,1,0,2:T(8,128)(2,1)} fusion(bf16[4,512,2,128]{3,1,0,2:T(8,128)(2,1)} %get-tuple-element.418, s32[]{:T(128)} %get-tuple-element.417, bf16[1024,2,128]{2,0,1:T(8,128)(2,1)S(1)} %get-tuple-element.439, f32[2,512,1024]{2,1,0:T(8,128)} %copy-done, f32[2,512]{1,0:T(2,128)S(1)} %get-tuple-element.363, ...), kind=kOutput, calls=%fused_computation.33.clone.1 | convolution fusion | flops 273022976 | bytes 6038020 | tf_op jit(solution)/shard_map/while/body/eval_jaxpr/hqk,khd->qhd/dot_general | solution.py:23
  217.4 1.1 fusion.92
  218.5 1.9 copy-done
  220.4 1.2 fusion.93
  223.7 4.1 %fusion.94 = bf16[4,512,2,128]{3,1,0,2:T(8,128)(2,1)} fusion(bf16[4,512,2,128]{3,1,0,2:T(8,128)(2,1)} %get-tuple-element.418, s32[]{:T(128)} %get-tuple-element.417, bf16[1024,2,128]{2,0,1:T(8,128)(2,1)S(1)} %get-tuple-element.439, f32[2,512,1024]{2,1,0:T(8,128)} %copy-done, f32[2,512]{1,0:T(2,128)S(1)} %get-tuple-element.363, ...), kind=kOutput, calls=%fused_computation.33.clone.1 | convolution fusion | flops 273022976 | bytes 6038020 | tf_op jit(solution)/shard_map/while/body/eval_jaxpr/hqk,khd->qhd/dot_general | solution.py:23
  229.8 1.1 fusion.92
  230.9 1.9 copy-done
  232.9 1.2 fusion.93
  236.1 4.1 %fusion.94 = bf16[4,512,2,128]{3,1,0,2:T(8,128)(2,1)} fusion(bf16[4,512,2,128]{3,1,0,2:T(8,128)(2,1)} %get-tuple-element.418, s32[]{:T(128)} %get-tuple-element.417, bf16[1024,2,128]{2,0,1:T(8,128)(2,1)S(1)} %get-tuple-element.439, f32[2,512,1024]{2,1,0:T(8,128)} %copy-done, f32[2,512]{1,0:T(2,128)S(1)} %get-tuple-element.363, ...), kind=kOutput, calls=%fused_computation.33.clone.1 | convolution fusion | flops 273022976 | bytes 6038020 | tf_op jit(solution)/shard_map/while/body/eval_jaxpr/hqk,khd->qhd/dot_general | solution.py:23
  242.3 1.1 fusion.92
  243.3 1.9 copy-done
  245.3 1.2 fusion.93
  248.5 4.1 %fusion.94 = bf16[4,512,2,128]{3,1,0,2:T(8,128)(2,1)} fusion(bf16[4,512,2,128]{3,1,0,2:T(8,128)(2,1)} %get-tuple-element.418, s32[]{:T(128)} %get-tuple-element.417, bf16[1024,2,128]{2,0,1:T(8,128)(2,1)S(1)} %get-tuple-element.439, f32[2,512,1024]{2,1,0:T(8,128)} %copy-done, f32[2,512]{1,0:T(2,128)S(1)} %get-tuple-element.363, ...), kind=kOutput, calls=%fused_computation.33.clone.1 | convolution fusion | flops 273022976 | bytes 6038020 | tf_op jit(solution)/shard_map/while/body/eval_jaxpr/hqk,khd->qhd/dot_general | solution.py:23
  252.6 2.8 copy.57
  255.4 21.2 %all_to_all.69 = bf16[2048,2,128]{2,1,0:T(2,128)(2,1)S(1)} all-to-all(bf16[2048,2,128]{2,1,0:T(2,128)(2,1)S(1)} %copy.57), channel_id=1, replica_groups=mesh['span'=16,'chip'=8,'core'=2] {'chip','core'}, dimensions={0} | all-to-all | bytes 2097152 | tf_op jit(solution)/shard_map/all_to_all | solution.py:90
  277.5 1.3 copy.60
  (78 shorter events, 17.7 us)
Async XLA Ops:
  6.5 9.3 %copy-start.4 = (bf16[1,128,4096]{2,1,0:T(8,128)(2,1)S(1)}, bf16[1,128,4096]{2,1,0:T(8,128)(2,1)}, u32[]{:S(2)}) copy-start(bf16[1,128,4096]{2,1,0:T(8,128)(2,1)} %param.15) | copy-start | bytes 3145732
  8.9 22.6 %all-to-all-start.1 = ((bf16[128,32,128]{0,2,1:T(8,128)(2,1)}), bf16[128,32,128]{0,2,1:T(8,128)(2,1)S(1)}, u32[]{:S(2)}, u32[]{:S(2)}) async-start(bf16[128,32,128]{0,2,1:T(8,128)(2,1)} %bitcast.14), calls=%async_computation.1 | async-start | bytes 2097152 | tf_op jit(solution)/shard_map/all_to_all | solution.py:36
  31.5 65.1 %all-to-all-start.2 = ((bf16[128,32,128]{0,2,1:T(8,128)(2,1)}), bf16[128,32,128]{0,2,1:T(8,128)(2,1)S(1)}, u32[]{:S(2)}, u32[]{:S(2)}) async-start(bf16[128,32,128]{0,2,1:T(8,128)(2,1)} %bitcast.19), calls=%async_computation.2 | async-start | bytes 2097152 | tf_op jit(solution)/shard_map/all_to_all | solution.py:37
  35.9 69.5 %copy-start.6 = (s32[1,16,2]{1,2,0:T(2,128)S(1)}, s32[1,16,2]{1,2,0:T(2,128)}, u32[]{:S(2)}) copy-start(s32[1,16,2]{1,2,0:T(2,128)} %param.20) | copy-start | bytes 388
  35.9 69.5 %copy-start.5 = (s32[1,2048]{1,0:T(1,128)S(1)}, s32[1,2048]{1,0:T(1,128)}, u32[]{:S(2)}) copy-start(s32[1,2048]{1,0:T(1,128)} %param.19) | copy-start | bytes 24580
  36.6 80.9 %collective-permute-start = (bf16[2048,2,128]{2,0,1:T(8,128)(2,1)S(1)}, bf16[2048,2,128]{2,0,1:T(8,128)(2,1)}, u32[]{:S(2)}, u32[]{:S(2)}) collective-permute-start(bf16[2048,2,128]{2,0,1:T(8,128)(2,1)S(1)} %bitcast.117), channel_id=1, source_target_pairs={{0,16},{16,32},{32,48},{48,64},{64,80},{80,96},{96,112},{112,128},... | collective-permute-start | bytes 3145736 | tf_op jit(solution)/shard_map/ppermute | solution.py:14
  96.6 20.2 %all-to-all-start = ((bf16[128,32,128]{0,2,1:T(8,128)(2,1)}), bf16[128,32,128]{0,2,1:T(8,128)(2,1)S(1)}, u32[]{:S(2)}, u32[]{:S(2)}) async-start(bf16[128,32,128]{0,2,1:T(8,128)(2,1)} %bitcast.9), calls=%async_computation | async-start | bytes 2097152 | tf_op jit(solution)/shard_map/all_to_all | solution.py:38
  101.0 98.2 %all-gather.3.cloned.1.call-start = ((), (), s32[]{:S(2)}) async-start(), calls=%async_computation.4 | async-start | bytes 2228224 | tf_op jit(solution)/shard_map/all_gather | solution.py:66
  102.3 24.2 %collective-permute-start.1 = (bf16[2048,2,128]{2,0,1:T(8,128)(2,1)}, bf16[2048,2,128]{2,0,1:T(8,128)(2,1)}, u32[]{:S(2)}, u32[]{:S(2)}) collective-permute-start(bf16[2048,2,128]{2,0,1:T(8,128)(2,1)} %bitcast.119), channel_id=1, source_target_pairs={{0,16},{16,32},{32,48},{48,64},{64,80},{80,96},{96,112},{112,128},... | collective-permute-start | bytes 3145736 | tf_op jit(solution)/shard_map/ppermute | solution.py:14
  117.4 9.1 %copy-start.1 = (bf16[16,128,2,128]{3,1,0,2:T(8,128)(2,1)S(1)}, bf16[16,128,2,128]{3,1,0,2:T(8,128)(2,1)}, u32[]{:S(2)}) copy-start(bf16[16,128,2,128]{3,1,0,2:T(8,128)(2,1)} %copy.53) | copy-start | bytes 3145732
  129.2 2.8 copy-start.2
  136.0 4.7 %copy-start.3 = (bf16[4096,2,128]{2,0,1:T(8,128)(2,1)S(1)}, bf16[4096,2,128]{2,0,1:T(8,128)(2,1)}, u32[]{:S(2)}) copy-start(bf16[4096,2,128]{2,0,1:T(8,128)(2,1)} %get-tuple-element.398) | copy-start | bytes 6291460 | tf_op jit(solution)/shard_map/while
  146.7 2.7 copy-start.2
  153.5 4.7 %copy-start.3 = (bf16[4096,2,128]{2,0,1:T(8,128)(2,1)S(1)}, bf16[4096,2,128]{2,0,1:T(8,128)(2,1)}, u32[]{:S(2)}) copy-start(bf16[4096,2,128]{2,0,1:T(8,128)(2,1)} %get-tuple-element.398) | copy-start | bytes 6291460 | tf_op jit(solution)/shard_map/while
  164.2 2.7 copy-start.2
  171.0 4.7 %copy-start.3 = (bf16[4096,2,128]{2,0,1:T(8,128)(2,1)S(1)}, bf16[4096,2,128]{2,0,1:T(8,128)(2,1)}, u32[]{:S(2)}) copy-start(bf16[4096,2,128]{2,0,1:T(8,128)(2,1)} %get-tuple-element.398) | copy-start | bytes 6291460 | tf_op jit(solution)/shard_map/while
  181.7 2.7 copy-start.2
  188.5 4.7 %copy-start.3 = (bf16[4096,2,128]{2,0,1:T(8,128)(2,1)S(1)}, bf16[4096,2,128]{2,0,1:T(8,128)(2,1)}, u32[]{:S(2)}) copy-start(bf16[4096,2,128]{2,0,1:T(8,128)(2,1)} %get-tuple-element.398) | copy-start | bytes 6291460 | tf_op jit(solution)/shard_map/while
  206.1 1.9 copy-start
  218.5 1.9 copy-start
  230.9 1.9 copy-start
  243.3 1.9 copy-start
Sparse Core Ops, SparseCore 0:
  117.5 29.0 all-gather.2

commit v5 on v3

--- a/solution.py
+++ b/solution.py
@@ -37,7 +37,8 @@
         lax.all_to_all(v_local, SEQ, split_axis=1, concat_axis=0, tiled=True),
         lax.all_to_all(q_local, SEQ, split_axis=1, concat_axis=0, tiled=True),
     )
-    prev_kh, prev_vh = shifted((k_heads, v_heads), "span", 1)
+    k_late, v_late = lax.optimization_barrier((k_heads, v_heads, q_heads))[:2]
+    prev_kh, prev_vh = shifted((k_late, v_late), "span", 1)
     span_rows = q_heads.shape[0]
     head_count = q_heads.shape[1]
     joint_w = jnp.concatenate([audio_wk, audio_wv], axis=1)

time: 272 us -> 275 us (1.011); the launches traced: 271 us -> 270 us
  starting transfers between devices: 27.6 us -> 23.9 us
  blocking collectives: 20.6 us -> 23.8 us
    ppermute x2, waiting for transfers between devices: 0.01 us -> 33.2 us  [shifted(): lax.ppermute(value, axis, [(source, source + steps) for source in range(l...]
    all_to_all x1, waiting for transfers between devices: 44.4 us -> 14.4 us  [local(): lax.all_to_all(q_local, SEQ, split_axis=1, concat_axis=0, tiled=True)]
    all_to_all x1, waiting for transfers between devices: 13.6 us -> 0.01 us  [local(): lax.all_to_all(v_local, SEQ, split_axis=1, concat_axis=0, tiled=True)]
    all_to_all x1, waiting for transfers between devices: 0.01 us -> 12.8 us  [local(): lax.all_to_all(k_local, SEQ, split_axis=1, concat_axis=0, tiled=True)]
    all_to_all x1, blocking collectives: 20.6 us -> 23.8 us  [local(): back = lax.all_to_all(mixed, SEQ, split_axis=0, concat_axis=1, tiled=True)]
    unnamed x15 -> x13, local copies, waits for them, and re-layouts: 7.2 us -> 7.21 us
  transfers between devices with their start and end apart: 7 -> 7, of which waited for: 3 -> 5; matrix products, arithmetic and copies ran while one was open for 5% -> 4% of each run, Pallas kernels for 0% -> 0%
where the time goes in v5:
time: 275 us; the launch traced here: 270 us
  waiting for transfers between devices  86 us (31%)
  matrix products  58.8 us (21%)
  other arithmetic  33.6 us (12%)
  local copies, waits for them, and re-layouts  27.2 us (10%)
  starting transfers between devices  23.9 us (9%)
  blocking collectives  23.8 us (9%)
  between operations  14.2 us (5%)
  loops' own time  3.03 us (1%)
    ppermute x2, waiting for transfers between devices, shifted(): lax.ppermute(value, axis, [(source, source + steps) for source in range(l...  33.2 us
    dot_general x8, matrix products, attend(): jnp.einsum('hqk,khd->qhd', weights.astype(jnp.bfloat16), value_rows, pref...  30 us
    dot_general x8, matrix products, attend(): jnp.einsum('qhd,khd->hqk', query, key_rows, preferred_element_type=jnp.fl...  25.6 us
    all_gather x1, waiting for transfers between devices, local(): own = lax.all_gather(audio[0], 'chip', axis=0, tiled=True)  25 us
    all_to_all x1, blocking collectives, local(): back = lax.all_to_all(mixed, SEQ, split_axis=0, concat_axis=1, tiled=True)  23.8 us
    reduce_sum x8, other arithmetic, attend(): den = jnp.sum(weights, axis=-1, keepdims=True)  23.5 us
    all_to_all x1, waiting for transfers between devices, local(): lax.all_to_all(q_local, SEQ, split_axis=1, concat_axis=0, tiled=True)  14.4 us
    all_to_all x1, waiting for transfers between devices, local(): lax.all_to_all(k_local, SEQ, split_axis=1, concat_axis=0, tiled=True)  12.8 us
  transfers between devices with their start and end apart: 7, of which 5 were waited for; matrix products, arithmetic and copies ran while one was open for 4% of the time, Pallas kernels for 0%

profile of v5, /device:TPU:1, one launch (start us, length us, event | category | flops | bytes accessed | tf_op | source)
XLA Modules:
  0.0 270.5 jit_solution(6960782530148173843)
XLA Ops:
  6.5 2.3 copy.45
  8.9 6.9 %all-to-all-start = ((bf16[128,32,128]{0,2,1:T(8,128)(2,1)}), bf16[128,32,128]{0,2,1:T(8,128)(2,1)S(1)}, u32[]{:S(2)}, u32[]{:S(2)}) async-start(bf16[128,32,128]{0,2,1:T(8,128)(2,1)} %bitcast.2), calls=%async_computation | async-start | bytes 2097152 | tf_op jit(solution)/shard_map/all_to_all | solution.py:38
  15.8 1.3 copy.48
  17.1 14.4 %all-to-all-done = bf16[128,32,128]{0,2,1:T(8,128)(2,1)S(1)} async-done(((bf16[128,32,128]{0,2,1:T(8,128)(2,1)}), bf16[128,32,128]{0,2,1:T(8,128)(2,1)S(1)}, u32[]{:S(2)}, u32[]{:S(2)}) %all-to-all-start) | async-done | bytes 1048608 | tf_op jit(solution)/shard_map/all_to_all | solution.py:38
  31.5 4.4 %all-to-all-start.1 = ((bf16[128,32,128]{0,2,1:T(8,128)(2,1)}), bf16[128,32,128]{0,2,1:T(8,128)(2,1)S(1)}, u32[]{:S(2)}, u32[]{:S(2)}) async-start(bf16[128,32,128]{0,2,1:T(8,128)(2,1)} %bitcast.7), calls=%async_computation.1 | async-start | bytes 2097152 | tf_op jit(solution)/shard_map/all_to_all | solution.py:36
  35.9 0.7 all-gather.5.cloned.1.call-update
  36.6 2.3 copy.51
  38.9 12.8 %all-to-all-done.1 = bf16[128,32,128]{0,2,1:T(8,128)(2,1)S(1)} async-done(((bf16[128,32,128]{0,2,1:T(8,128)(2,1)}), bf16[128,32,128]{0,2,1:T(8,128)(2,1)S(1)}, u32[]{:S(2)}, u32[]{:S(2)}) %all-to-all-start.1) | async-done | bytes 1048608 | tf_op jit(solution)/shard_map/all_to_all | solution.py:36
  51.6 5.0 %all-to-all-start.2 = ((bf16[128,32,128]{0,2,1:T(8,128)(2,1)}), bf16[128,32,128]{0,2,1:T(8,128)(2,1)}, u32[]{:S(2)}, u32[]{:S(2)}) async-start(bf16[128,32,128]{0,2,1:T(8,128)(2,1)} %bitcast.12), calls=%async_computation.2 | async-start | bytes 2097152 | tf_op jit(solution)/shard_map/all_to_all | solution.py:37
  56.7 25.0 %all-gather.5.cloned.1.call-done = bf16[1,512,1024]{2,1,0:T(8,128)(2,1)} async-done(((bf16[1,64,1024]{2,1,0:T(8,128)(2,1)}), bf16[1,512,1024]{2,1,0:T(8,128)(2,1)}) %all-gather.5.cloned.1.call-update) | async-done | bytes 1048592 | tf_op jit(solution)/shard_map/all_gather | solution.py:45
  81.7 0.7 copy.47
  83.1 1.6 copy.53
  84.7 4.3 %collective-permute-start = (bf16[2048,2,128]{2,0,1:T(8,128)(2,1)S(1)}, bf16[2048,2,128]{2,0,1:T(8,128)(2,1)}, u32[]{:S(2)}, u32[]{:S(2)}) collective-permute-start(bf16[2048,2,128]{2,0,1:T(8,128)(2,1)S(1)} %bitcast.103), channel_id=1, source_target_pairs={{0,16},{16,32},{32,48},{48,64},{64,80},{80,96},{96,112},{112,128},... | collective-permute-start | bytes 3145736 | tf_op jit(solution)/shard_map/ppermute | solution.py:14
  89.1 3.2 %collective-permute-start.1 = (bf16[2048,2,128]{2,0,1:T(8,128)(2,1)S(1)}, bf16[2048,2,128]{2,0,1:T(8,128)(2,1)}, u32[]{:S(2)}, u32[]{:S(2)}) collective-permute-start(bf16[2048,2,128]{2,0,1:T(8,128)(2,1)S(1)} %bitcast.105), channel_id=1, source_target_pairs={{0,16},{16,32},{32,48},{48,64},{64,80},{80,96},{96,112},{112,128},... | collective-permute-start | bytes 3145736 | tf_op jit(solution)/shard_map/ppermute | solution.py:14
  93.0 13.4 %collective-permute-done = bf16[2048,2,128]{2,0,1:T(8,128)(2,1)} collective-permute-done((bf16[2048,2,128]{2,0,1:T(8,128)(2,1)S(1)}, bf16[2048,2,128]{2,0,1:T(8,128)(2,1)}, u32[]{:S(2)}, u32[]{:S(2)}) %collective-permute-start) | collective-permute-done | bytes 1048608 | tf_op jit(solution)/shard_map/ppermute | solution.py:14
  106.4 2.7 pad_maximum_fusion
  109.1 19.8 %collective-permute-done.1 = bf16[2048,2,128]{2,0,1:T(8,128)(2,1)} collective-permute-done((bf16[2048,2,128]{2,0,1:T(8,128)(2,1)S(1)}, bf16[2048,2,128]{2,0,1:T(8,128)(2,1)}, u32[]{:S(2)}, u32[]{:S(2)}) %collective-permute-start.1) | collective-permute-done | bytes 1048608 | tf_op jit(solution)/shard_map/ppermute | solution.py:14
  128.9 2.7 pad_maximum_fusion.1
  131.6 3.2 %fusion.67 = bf16[1024,512]{0,1:T(8,128)(2,1)S(1)} fusion(bf16[1,1024,1024]{2,1,0:T(8,128)(2,1)} %all-gather.7.cloned.1.call-done, bf16[1024,256]{1,0:T(8,128)(2,1)} %param.16, bf16[1024,256]{1,0:T(8,128)(2,1)} %param.15), kind=kOutput, calls=%fused_computation.64 | convolution fusion | flops 1076363264 | bytes 4194304 | tf_op jit(solution)/shard_map/dot_general | solution.py:47
  134.9 1.0 copy.55
  136.2 92.6 %while.12 = (s32[]{:T(128)}, bf16[4,512,2,128]{3,1,0,2:T(8,128)(2,1)S(1)}, s32[1,2048]{1,0:T(1,128)S(1)}, s32[4]{0:T(128)S(1)}, s32[2048]{0:T(1024)S(1)}, /*inde...) while((s32[]{:T(128)}, ...), condition=%wide.region_7.8_spmd.clone.clone, body=%wide.region_2.7_spmd.clone.clone.sunk | while | flops 2745201664 | bytes 95234384 | solution.py:87
  139.5 1.1 fusion.99
  140.6 1.2 fusion.100
  141.8 1.9 fusion.101
  143.8 5.3 %fusion.102 = (f32[2,512]{1,0:T(2,128)S(1)}, f32[2,512,4096]{2,1,0:T(8,128)S(1)}) fusion(pred[512,4096]{1,0:T(8,128)(4,1)S(1)} %concatenate.18, bf16[4096,2,128]{2,0,1:T(8,128)(2,1)} %get-tuple-element.374, bf16[2048,2,128]{2,0,1:T(8,128)(2,1)S(1)} %get-tuple-element.373, s32[]{:T(128)S(6)} %select_n.231), kind=kOutput, calls=%fused_computation.3.clone.1 | convolution fusion | flops 1086323712 | bytes 21237764 | tf_op jit(solution)/shard_map/while/body/eval_jaxpr/qhd,khd->hqk/dot_general | solution.py:18
  149.1 4.6 %fusion.103 = f32[2,512]{1,0:T(2,128)S(1)} fusion(f32[2,512,4096]{2,1,0:T(8,128)S(1)} %get-tuple-element.331, f32[2,512]{1,0:T(2,128)S(1)} %get-tuple-element.332, pred[512,4096]{1,0:T(8,128)(4,1)S(1)} %concatenate.18), kind=kLoop, calls=%fused_computation.4.clone.1 | loop fusion | flops 16776192 | bytes 18882560 | tf_op jit(solution)/shard_map/while/body/eval_jaxpr/reduce_sum | solution.py:22
  153.8 5.6 %fusion.104 = bf16[4,512,2,128]{3,1,0,2:T(8,128)(2,1)S(1)} fusion(bf16[4,512,2,128]{3,1,0,2:T(8,128)(2,1)S(1)} %get-tuple-element.351, s32[]{:T(128)S(6)} %copy.69, f32[512,2,128]{2,0,1:T(8,128)S(1)} %copy-done.6, bf16[4096,2,128]{2,0,1:T(8,128)(2,1)S(1)} %copy-done, f32[2,512,4096]{2,1,0:T(8,128)S(1)} %get-tuple-element.331, ...), kind=kOutput, calls=%fused_computation.23.clone.1 | convolution fusion | flops 1090912256 | bytes 21766148 | tf_op jit(solution)/shard_map/while/body/eval_jaxpr/hqk,khd->qhd/dot_general | solution.py:23
  162.7 1.1 fusion.99
  163.8 1.2 fusion.100
  165.0 1.9 fusion.101
  166.9 5.3 %fusion.102 = (f32[2,512]{1,0:T(2,128)S(1)}, f32[2,512,4096]{2,1,0:T(8,128)S(1)}) fusion(pred[512,4096]{1,0:T(8,128)(4,1)S(1)} %concatenate.18, bf16[4096,2,128]{2,0,1:T(8,128)(2,1)} %get-tuple-element.374, bf16[2048,2,128]{2,0,1:T(8,128)(2,1)S(1)} %get-tuple-element.373, s32[]{:T(128)S(6)} %select_n.231), kind=kOutput, calls=%fused_computation.3.clone.1 | convolution fusion | flops 1086323712 | bytes 21237764 | tf_op jit(solution)/shard_map/while/body/eval_jaxpr/qhd,khd->hqk/dot_general | solution.py:18
  172.3 4.6 %fusion.103 = f32[2,512]{1,0:T(2,128)S(1)} fusion(f32[2,512,4096]{2,1,0:T(8,128)S(1)} %get-tuple-element.331, f32[2,512]{1,0:T(2,128)S(1)} %get-tuple-element.332, pred[512,4096]{1,0:T(8,128)(4,1)S(1)} %concatenate.18), kind=kLoop, calls=%fused_computation.4.clone.1 | loop fusion | flops 16776192 | bytes 18882560 | tf_op jit(solution)/shard_map/while/body/eval_jaxpr/reduce_sum | solution.py:22
  176.9 5.6 %fusion.104 = bf16[4,512,2,128]{3,1,0,2:T(8,128)(2,1)S(1)} fusion(bf16[4,512,2,128]{3,1,0,2:T(8,128)(2,1)S(1)} %get-tuple-element.351, s32[]{:T(128)S(6)} %copy.69, f32[512,2,128]{2,0,1:T(8,128)S(1)} %copy-done.6, bf16[4096,2,128]{2,0,1:T(8,128)(2,1)S(1)} %copy-done, f32[2,512,4096]{2,1,0:T(8,128)S(1)} %get-tuple-element.331, ...), kind=kOutput, calls=%fused_computation.23.clone.1 | convolution fusion | flops 1090912256 | bytes 21766148 | tf_op jit(solution)/shard_map/while/body/eval_jaxpr/hqk,khd->qhd/dot_general | solution.py:23
  185.9 1.1 fusion.99
  186.9 1.2 fusion.100
  188.2 1.9 fusion.101
  190.1 5.3 %fusion.102 = (f32[2,512]{1,0:T(2,128)S(1)}, f32[2,512,4096]{2,1,0:T(8,128)S(1)}) fusion(pred[512,4096]{1,0:T(8,128)(4,1)S(1)} %concatenate.18, bf16[4096,2,128]{2,0,1:T(8,128)(2,1)} %get-tuple-element.374, bf16[2048,2,128]{2,0,1:T(8,128)(2,1)S(1)} %get-tuple-element.373, s32[]{:T(128)S(6)} %select_n.231), kind=kOutput, calls=%fused_computation.3.clone.1 | convolution fusion | flops 1086323712 | bytes 21237764 | tf_op jit(solution)/shard_map/while/body/eval_jaxpr/qhd,khd->hqk/dot_general | solution.py:18
  195.4 4.6 %fusion.103 = f32[2,512]{1,0:T(2,128)S(1)} fusion(f32[2,512,4096]{2,1,0:T(8,128)S(1)} %get-tuple-element.331, f32[2,512]{1,0:T(2,128)S(1)} %get-tuple-element.332, pred[512,4096]{1,0:T(8,128)(4,1)S(1)} %concatenate.18), kind=kLoop, calls=%fused_computation.4.clone.1 | loop fusion | flops 16776192 | bytes 18882560 | tf_op jit(solution)/shard_map/while/body/eval_jaxpr/reduce_sum | solution.py:22
  200.1 5.6 %fusion.104 = bf16[4,512,2,128]{3,1,0,2:T(8,128)(2,1)S(1)} fusion(bf16[4,512,2,128]{3,1,0,2:T(8,128)(2,1)S(1)} %get-tuple-element.351, s32[]{:T(128)S(6)} %copy.69, f32[512,2,128]{2,0,1:T(8,128)S(1)} %copy-done.6, bf16[4096,2,128]{2,0,1:T(8,128)(2,1)S(1)} %copy-done, f32[2,512,4096]{2,1,0:T(8,128)S(1)} %get-tuple-element.331, ...), kind=kOutput, calls=%fused_computation.23.clone.1 | convolution fusion | flops 1090912256 | bytes 21766148 | tf_op jit(solution)/shard_map/while/body/eval_jaxpr/hqk,khd->qhd/dot_general | solution.py:23
  209.0 1.1 fusion.99
  210.1 1.2 fusion.100
  211.3 1.9 fusion.101
  213.2 5.3 %fusion.102 = (f32[2,512]{1,0:T(2,128)S(1)}, f32[2,512,4096]{2,1,0:T(8,128)S(1)}) fusion(pred[512,4096]{1,0:T(8,128)(4,1)S(1)} %concatenate.18, bf16[4096,2,128]{2,0,1:T(8,128)(2,1)} %get-tuple-element.374, bf16[2048,2,128]{2,0,1:T(8,128)(2,1)S(1)} %get-tuple-element.373, s32[]{:T(128)S(6)} %select_n.231), kind=kOutput, calls=%fused_computation.3.clone.1 | convolution fusion | flops 1086323712 | bytes 21237764 | tf_op jit(solution)/shard_map/while/body/eval_jaxpr/qhd,khd->hqk/dot_general | solution.py:18
  218.6 4.6 %fusion.103 = f32[2,512]{1,0:T(2,128)S(1)} fusion(f32[2,512,4096]{2,1,0:T(8,128)S(1)} %get-tuple-element.331, f32[2,512]{1,0:T(2,128)S(1)} %get-tuple-element.332, pred[512,4096]{1,0:T(8,128)(4,1)S(1)} %concatenate.18), kind=kLoop, calls=%fused_computation.4.clone.1 | loop fusion | flops 16776192 | bytes 18882560 | tf_op jit(solution)/shard_map/while/body/eval_jaxpr/reduce_sum | solution.py:22
  223.3 5.6 %fusion.104 = bf16[4,512,2,128]{3,1,0,2:T(8,128)(2,1)S(1)} fusion(bf16[4,512,2,128]{3,1,0,2:T(8,128)(2,1)S(1)} %get-tuple-element.351, s32[]{:T(128)S(6)} %copy.69, f32[512,2,128]{2,0,1:T(8,128)S(1)} %copy-done.6, bf16[4096,2,128]{2,0,1:T(8,128)(2,1)S(1)} %copy-done, f32[2,512,4096]{2,1,0:T(8,128)S(1)} %get-tuple-element.331, ...), kind=kOutput, calls=%fused_computation.23.clone.1 | convolution fusion | flops 1090912256 | bytes 21766148 | tf_op jit(solution)/shard_map/while/body/eval_jaxpr/hqk,khd->qhd/dot_general | solution.py:23
  228.9 8.9 %copy.57 = bf16[2048,2,128]{2,1,0:T(2,128)(2,1)S(1)} copy(bf16[2048,2,128]{2,0,1:T(8,128)(2,1)S(1)} %bitcast.109) | data formatting | bytes 2097152 | tf_op jit(solution)/shard_map/reshape | solution.py:88
  237.8 23.8 %all_to_all.69 = bf16[2048,2,128]{2,1,0:T(2,128)(2,1)S(1)} all-to-all(bf16[2048,2,128]{2,1,0:T(2,128)(2,1)S(1)} %copy.57), channel_id=1, replica_groups=mesh['span'=16,'chip'=8,'core'=2] {'chip','core'}, dimensions={0} | all-to-all | bytes 2097152 | tf_op jit(solution)/shard_map/all_to_all | solution.py:89
  262.3 1.3 copy.60
  (78 shorter events, 12.6 us)
Async XLA Ops:
  6.5 9.3 %copy-start.1 = (bf16[1,128,4096]{2,1,0:T(8,128)(2,1)S(1)}, bf16[1,128,4096]{2,1,0:T(8,128)(2,1)}, u32[]{:S(2)}) copy-start(bf16[1,128,4096]{2,1,0:T(8,128)(2,1)} %param.12) | copy-start | bytes 3145732
  8.9 22.6 %all-to-all-start = ((bf16[128,32,128]{0,2,1:T(8,128)(2,1)}), bf16[128,32,128]{0,2,1:T(8,128)(2,1)S(1)}, u32[]{:S(2)}, u32[]{:S(2)}) async-start(bf16[128,32,128]{0,2,1:T(8,128)(2,1)} %bitcast.2), calls=%async_computation | async-start | bytes 2097152 | tf_op jit(solution)/shard_map/all_to_all | solution.py:38
  31.5 20.2 %all-to-all-start.1 = ((bf16[128,32,128]{0,2,1:T(8,128)(2,1)}), bf16[128,32,128]{0,2,1:T(8,128)(2,1)S(1)}, u32[]{:S(2)}, u32[]{:S(2)}) async-start(bf16[128,32,128]{0,2,1:T(8,128)(2,1)} %bitcast.7), calls=%async_computation.1 | async-start | bytes 2097152 | tf_op jit(solution)/shard_map/all_to_all | solution.py:36
  35.9 45.8 %all-gather.5.cloned.1.call-start = ((), (), s32[]{:S(2)}) async-start(), calls=%async_computation.4 | async-start | bytes 1179648 | tf_op jit(solution)/shard_map/all_gather | solution.py:45
  51.6 31.4 %all-to-all-start.2 = ((bf16[128,32,128]{0,2,1:T(8,128)(2,1)}), bf16[128,32,128]{0,2,1:T(8,128)(2,1)}, u32[]{:S(2)}, u32[]{:S(2)}) async-start(bf16[128,32,128]{0,2,1:T(8,128)(2,1)} %bitcast.12), calls=%async_computation.2 | async-start | bytes 2097152 | tf_op jit(solution)/shard_map/all_to_all | solution.py:37
  56.7 36.2 %copy-start.5 = (s32[1,16,2]{1,2,0:T(2,128)S(1)}, s32[1,16,2]{1,2,0:T(2,128)}, u32[]{:S(2)}) copy-start(s32[1,16,2]{1,2,0:T(2,128)} %param.18) | copy-start | bytes 388
  56.7 36.2 %copy-start.4 = (s32[1,2048]{1,0:T(1,128)S(1)}, s32[1,2048]{1,0:T(1,128)}, u32[]{:S(2)}) copy-start(s32[1,2048]{1,0:T(1,128)} %param.17) | copy-start | bytes 24580
  56.7 74.9 %all-gather.7.cloned.1.call-start = ((), (), s32[]{:S(2)}) async-start(), calls=%async_computation.5 | async-start | bytes 3145728 | tf_op jit(solution)/shard_map/all_gather | solution.py:46
  84.7 21.7 %collective-permute-start = (bf16[2048,2,128]{2,0,1:T(8,128)(2,1)S(1)}, bf16[2048,2,128]{2,0,1:T(8,128)(2,1)}, u32[]{:S(2)}, u32[]{:S(2)}) collective-permute-start(bf16[2048,2,128]{2,0,1:T(8,128)(2,1)S(1)} %bitcast.103), channel_id=1, source_target_pairs={{0,16},{16,32},{32,48},{48,64},{64,80},{80,96},{96,112},{112,128},... | collective-permute-start | bytes 3145736 | tf_op jit(solution)/shard_map/ppermute | solution.py:14
  89.1 39.8 %collective-permute-start.1 = (bf16[2048,2,128]{2,0,1:T(8,128)(2,1)S(1)}, bf16[2048,2,128]{2,0,1:T(8,128)(2,1)}, u32[]{:S(2)}, u32[]{:S(2)}) collective-permute-start(bf16[2048,2,128]{2,0,1:T(8,128)(2,1)S(1)} %bitcast.105), channel_id=1, source_target_pairs={{0,16},{16,32},{32,48},{48,64},{64,80},{80,96},{96,112},{112,128},... | collective-permute-start | bytes 3145736 | tf_op jit(solution)/shard_map/ppermute | solution.py:14
  134.8 1.4 copy-start.2
  139.5 2.3 copy-start.3
  149.1 4.7 %copy-start = (bf16[4096,2,128]{2,0,1:T(8,128)(2,1)S(1)}, bf16[4096,2,128]{2,0,1:T(8,128)(2,1)}, u32[]{:S(2)}) copy-start(bf16[4096,2,128]{2,0,1:T(8,128)(2,1)} %get-tuple-element.375) | copy-start | bytes 6291460 | tf_op jit(solution)/shard_map/while
  149.1 4.7 %copy-start.6 = (f32[512,2,128]{2,0,1:T(8,128)S(1)}, f32[512,2,128]{2,0,1:T(8,128)}, u32[]{:S(2)}) copy-start(f32[512,2,128]{2,0,1:T(8,128)} %fusion.101) | copy-start | bytes 1572868 | tf_op jit(solution)/shard_map/while
  162.7 2.3 copy-start.3
  172.3 4.7 %copy-start = (bf16[4096,2,128]{2,0,1:T(8,128)(2,1)S(1)}, bf16[4096,2,128]{2,0,1:T(8,128)(2,1)}, u32[]{:S(2)}) copy-start(bf16[4096,2,128]{2,0,1:T(8,128)(2,1)} %get-tuple-element.375) | copy-start | bytes 6291460 | tf_op jit(solution)/shard_map/while
  172.3 4.7 %copy-start.6 = (f32[512,2,128]{2,0,1:T(8,128)S(1)}, f32[512,2,128]{2,0,1:T(8,128)}, u32[]{:S(2)}) copy-start(f32[512,2,128]{2,0,1:T(8,128)} %fusion.101) | copy-start | bytes 1572868 | tf_op jit(solution)/shard_map/while
  185.8 2.3 copy-start.3
  195.4 4.7 %copy-start = (bf16[4096,2,128]{2,0,1:T(8,128)(2,1)S(1)}, bf16[4096,2,128]{2,0,1:T(8,128)(2,1)}, u32[]{:S(2)}) copy-start(bf16[4096,2,128]{2,0,1:T(8,128)(2,1)} %get-tuple-element.375) | copy-start | bytes 6291460 | tf_op jit(solution)/shard_map/while
  195.4 4.7 %copy-start.6 = (f32[512,2,128]{2,0,1:T(8,128)S(1)}, f32[512,2,128]{2,0,1:T(8,128)}, u32[]{:S(2)}) copy-start(f32[512,2,128]{2,0,1:T(8,128)} %fusion.101) | copy-start | bytes 1572868 | tf_op jit(solution)/shard_map/while
  209.0 2.3 copy-start.3
  218.6 4.7 %copy-start = (bf16[4096,2,128]{2,0,1:T(8,128)(2,1)S(1)}, bf16[4096,2,128]{2,0,1:T(8,128)(2,1)}, u32[]{:S(2)}) copy-start(bf16[4096,2,128]{2,0,1:T(8,128)(2,1)} %get-tuple-element.375) | copy-start | bytes 6291460 | tf_op jit(solution)/shard_map/while
  218.6 4.7 %copy-start.6 = (f32[512,2,128]{2,0,1:T(8,128)S(1)}, f32[512,2,128]{2,0,1:T(8,128)}, u32[]{:S(2)}) copy-start(f32[512,2,128]{2,0,1:T(8,128)} %fusion.101) | copy-start | bytes 1572868 | tf_op jit(solution)/shard_map/while
Sparse Core Ops, SparseCore 0:
  38.5 43.1 all-gather.4
  83.5 20.2 all-gather.6

commit v6 on v5

--- a/solution.py
+++ b/solution.py
@@ -37,13 +37,12 @@
         lax.all_to_all(v_local, SEQ, split_axis=1, concat_axis=0, tiled=True),
         lax.all_to_all(q_local, SEQ, split_axis=1, concat_axis=0, tiled=True),
     )
-    k_late, v_late = lax.optimization_barrier((k_heads, v_heads, q_heads))[:2]
+    k_late, v_late, audio_late = lax.optimization_barrier((k_heads, v_heads, audio, q_heads))[:3]
     prev_kh, prev_vh = shifted((k_late, v_late), "span", 1)
     span_rows = q_heads.shape[0]
     head_count = q_heads.shape[1]
     joint_w = jnp.concatenate([audio_wk, audio_wv], axis=1)
-    own = lax.all_gather(audio[0], "chip", axis=0, tiled=True)
-    gathered = lax.all_gather(own, "core", axis=0, tiled=True)
+    gathered = lax.all_gather(audio_late[0], SEQ, axis=0, tiled=True)
     projected = jnp.dot(
         gathered,
         joint_w,
@@ -60,12 +59,7 @@
     upper = jnp.sum(jnp.where(onehot, table[None, :, 1], 0), axis=1)
     all_keys = jnp.concatenate([prev_kh, k_heads], axis=0)
     all_vals = jnp.concatenate([prev_vh, v_heads], axis=0)
-    cores = lax.axis_size("core")
-    chips = lax.axis_size("chip")
-    piece = aud_rows // (cores * chips)
-    order = jnp.arange(aud_rows, dtype=jnp.int32)
-    held_core, held_chip, row = order // (chips * piece), (order // piece) % chips, order % piece
-    positions = (held_chip * cores + held_core) * piece + row
+    positions = jnp.arange(aud_rows, dtype=jnp.int32)
     block = min(512, span_rows)
 
     def one_block(index):

time: 275 us -> 286 us (1.040); the launches traced: 270 us -> 285 us
  waiting for transfers between devices: 86 us -> 104 us
  blocking collectives: 23.8 us -> 18.8 us
    all_to_all x1, waiting for transfers between devices: 0.01 us -> 14.5 us  [local(): lax.all_to_all(v_local, SEQ, split_axis=1, concat_axis=0, tiled=True)]
    all_to_all x1, blocking collectives: 23.8 us -> 18.8 us  [local(): back = lax.all_to_all(mixed, SEQ, split_axis=0, concat_axis=1, tiled=True)]
    all_gather x2 -> x1, waiting for transfers between devices: 25 us -> 26 us  [local(): gathered = lax.all_gather(audio_late[0], SEQ, axis=0, tiled=True)]
  transfers between devices with their start and end apart: 7 -> 6, of which waited for: 5 -> 6; matrix products, arithmetic and copies ran while one was open for 4% -> 4% of each run, Pallas kernels for 0% -> 0%
where the time goes in v6:
time: 286 us; the launch traced here: 285 us
  waiting for transfers between devices  104 us (36%)
  matrix products  58.7 us (21%)
  other arithmetic  34 us (12%)
  local copies, waits for them, and re-layouts  27.2 us (10%)
  starting transfers between devices  24.6 us (9%)
  blocking collectives  18.8 us (7%)
  between operations  14.2 us (5%)
  loops' own time  3.02 us (1%)
    ppermute x2, waiting for transfers between devices, shifted(): lax.ppermute(value, axis, [(source, source + steps) for source in range(l...  35.9 us
    dot_general x8, matrix products, attend(): jnp.einsum('hqk,khd->qhd', weights.astype(jnp.bfloat16), value_rows, pref...  30 us
    all_gather x1, waiting for transfers between devices, local(): gathered = lax.all_gather(audio_late[0], SEQ, axis=0, tiled=True)  26 us
    dot_general x8, matrix products, attend(): jnp.einsum('qhd,khd->hqk', query, key_rows, preferred_element_type=jnp.fl...  25.6 us
    reduce_sum x8, other arithmetic, attend(): den = jnp.sum(weights, axis=-1, keepdims=True)  23.5 us
    all_to_all x1, blocking collectives, local(): back = lax.all_to_all(mixed, SEQ, split_axis=0, concat_axis=1, tiled=True)  18.8 us
    all_to_all x1, waiting for transfers between devices, local(): lax.all_to_all(v_local, SEQ, split_axis=1, concat_axis=0, tiled=True)  14.5 us
    all_to_all x1, waiting for transfers between devices, local(): lax.all_to_all(q_local, SEQ, split_axis=1, concat_axis=0, tiled=True)  14.3 us
  transfers between devices with their start and end apart: 6, of which 6 were waited for; matrix products, arithmetic and copies ran while one was open for 4% of the time, Pallas kernels for 0%

profile of v6, /device:TPU:1, one launch (start us, length us, event | category | flops | bytes accessed | tf_op | source)
XLA Modules:
  0.0 284.8 jit_solution(8586607202026289744)
XLA Ops:
  6.5 2.3 copy.45
  8.9 6.9 %all-to-all-start = ((bf16[128,32,128]{0,2,1:T(8,128)(2,1)}), bf16[128,32,128]{0,2,1:T(8,128)(2,1)S(1)}, u32[]{:S(2)}, u32[]{:S(2)}) async-start(bf16[128,32,128]{0,2,1:T(8,128)(2,1)} %bitcast.2), calls=%async_computation | async-start | bytes 2097152 | tf_op jit(solution)/shard_map/all_to_all | solution.py:38
  15.8 1.3 copy.48
  17.1 14.3 %all-to-all-done = bf16[128,32,128]{0,2,1:T(8,128)(2,1)S(1)} async-done(((bf16[128,32,128]{0,2,1:T(8,128)(2,1)}), bf16[128,32,128]{0,2,1:T(8,128)(2,1)S(1)}, u32[]{:S(2)}, u32[]{:S(2)}) %all-to-all-start) | async-done | bytes 1048608 | tf_op jit(solution)/shard_map/all_to_all | solution.py:38
  31.5 4.4 %all-to-all-start.1 = ((bf16[128,32,128]{0,2,1:T(8,128)(2,1)}), bf16[128,32,128]{0,2,1:T(8,128)(2,1)S(1)}, u32[]{:S(2)}, u32[]{:S(2)}) async-start(bf16[128,32,128]{0,2,1:T(8,128)(2,1)} %bitcast.7), calls=%async_computation.1 | async-start | bytes 2097152 | tf_op jit(solution)/shard_map/all_to_all | solution.py:36
  35.9 2.3 copy.51
  38.1 13.5 %all-to-all-done.1 = bf16[128,32,128]{0,2,1:T(8,128)(2,1)S(1)} async-done(((bf16[128,32,128]{0,2,1:T(8,128)(2,1)}), bf16[128,32,128]{0,2,1:T(8,128)(2,1)S(1)}, u32[]{:S(2)}, u32[]{:S(2)}) %all-to-all-start.1) | async-done | bytes 1048608 | tf_op jit(solution)/shard_map/all_to_all | solution.py:36
  51.6 5.2 %all-to-all-start.2 = ((bf16[128,32,128]{0,2,1:T(8,128)(2,1)}), bf16[128,32,128]{0,2,1:T(8,128)(2,1)}, u32[]{:S(2)}, u32[]{:S(2)}) async-start(bf16[128,32,128]{0,2,1:T(8,128)(2,1)} %bitcast.12), calls=%async_computation.2 | async-start | bytes 2097152 | tf_op jit(solution)/shard_map/all_to_all | solution.py:37
  56.8 0.7 copy.47
  58.2 14.5 %all-to-all-done.2 = bf16[128,32,128]{0,2,1:T(8,128)(2,1)} async-done(((bf16[128,32,128]{0,2,1:T(8,128)(2,1)}), bf16[128,32,128]{0,2,1:T(8,128)(2,1)}, u32[]{:S(2)}, u32[]{:S(2)}) %all-to-all-start.2) | async-done | bytes 1048608 | tf_op jit(solution)/shard_map/all_to_all | solution.py:37
  72.7 1.6 copy.53
  74.3 4.6 %collective-permute-start = (bf16[2048,2,128]{2,0,1:T(8,128)(2,1)S(1)}, bf16[2048,2,128]{2,0,1:T(8,128)(2,1)}, u32[]{:S(2)}, u32[]{:S(2)}) collective-permute-start(bf16[2048,2,128]{2,0,1:T(8,128)(2,1)S(1)} %bitcast.99), channel_id=1, source_target_pairs={{0,16},{16,32},{32,48},{48,64},{64,80},{80,96},{96,112},{112,128},... | collective-permute-start | bytes 3145736 | tf_op jit(solution)/shard_map/ppermute | solution.py:14
  78.9 3.6 %collective-permute-start.1 = (bf16[2048,2,128]{2,0,1:T(8,128)(2,1)S(1)}, bf16[2048,2,128]{2,0,1:T(8,128)(2,1)}, u32[]{:S(2)}, u32[]{:S(2)}) collective-permute-start(bf16[2048,2,128]{2,0,1:T(8,128)(2,1)S(1)} %bitcast.101), channel_id=1, source_target_pairs={{0,16},{16,32},{32,48},{48,64},{64,80},{80,96},{96,112},{112,128},... | collective-permute-start | bytes 3145736 | tf_op jit(solution)/shard_map/ppermute | solution.py:14
  83.2 16.2 %collective-permute-done = bf16[2048,2,128]{2,0,1:T(8,128)(2,1)} collective-permute-done((bf16[2048,2,128]{2,0,1:T(8,128)(2,1)S(1)}, bf16[2048,2,128]{2,0,1:T(8,128)(2,1)}, u32[]{:S(2)}, u32[]{:S(2)}) %collective-permute-start) | collective-permute-done | bytes 1048608 | tf_op jit(solution)/shard_map/ppermute | solution.py:14
  99.4 2.7 pad_maximum_fusion
  102.1 19.8 %collective-permute-done.1 = bf16[2048,2,128]{2,0,1:T(8,128)(2,1)} collective-permute-done((bf16[2048,2,128]{2,0,1:T(8,128)(2,1)S(1)}, bf16[2048,2,128]{2,0,1:T(8,128)(2,1)}, u32[]{:S(2)}, u32[]{:S(2)}) %collective-permute-start.1) | collective-permute-done | bytes 1048608 | tf_op jit(solution)/shard_map/ppermute | solution.py:14
  121.9 2.7 pad_maximum_fusion.1
  124.5 26.0 %all-gather.3.cloned.1.call-done = bf16[1,1024,1024]{2,1,0:T(8,128)(2,1)} async-done(((bf16[1,64,1024]{2,1,0:T(8,128)(2,1)}), bf16[1,1024,1024]{2,1,0:T(8,128)(2,1)}) %all-gather.3.cloned.1.call-update) | async-done | bytes 2097168 | tf_op jit(solution)/shard_map/all_gather | solution.py:45
  150.5 3.1 %fusion.51 = bf16[1024,512]{0,1:T(8,128)(2,1)S(1)} fusion(bf16[1,1024,1024]{2,1,0:T(8,128)(2,1)} %all-gather.3.cloned.1.call-done, bf16[1024,256]{1,0:T(8,128)(2,1)} %param.16, bf16[1024,256]{1,0:T(8,128)(2,1)} %param.15), kind=kOutput, calls=%fused_computation.41 | convolution fusion | flops 1076363264 | bytes 4194304 | tf_op jit(solution)/shard_map/dot_general | solution.py:46
  153.7 1.0 copy.55
  155.0 93.0 %while.12 = (s32[]{:T(128)}, bf16[4,512,2,128]{3,1,0,2:T(8,128)(2,1)S(1)}, s32[1,2048]{1,0:T(1,128)S(1)}, s32[4]{0:T(128)S(1)}, s32[2048]{0:T(1024)S(1)}, /*inde...) while((s32[]{:T(128)}, ...), condition=%wide.region_7.8_spmd.clone.clone, body=%wide.region_2.7_spmd.clone.clone.sunk | while | flops 2745167872 | bytes 95226192 | solution.py:81
  158.5 1.1 fusion.83
  159.5 1.2 fusion.84
  160.8 1.9 fusion.85
  162.7 5.3 %fusion.86 = (f32[2,512]{1,0:T(2,128)S(1)}, f32[2,512,4096]{2,1,0:T(8,128)S(1)}) fusion(pred[512,4096]{1,0:T(8,128)(4,1)S(1)} %concatenate.18, bf16[4096,2,128]{2,0,1:T(8,128)(2,1)} %get-tuple-element.376, bf16[2048,2,128]{2,0,1:T(8,128)(2,1)S(1)} %get-tuple-element.375, s32[]{:T(128)S(6)} %select_n.80), kind=kOutput, calls=%fused_computation.3.clone.1 | convolution fusion | flops 1086323712 | bytes 21237764 | tf_op jit(solution)/shard_map/while/body/eval_jaxpr/qhd,khd->hqk/dot_general | solution.py:18
  168.1 4.6 %fusion.87 = f32[2,512]{1,0:T(2,128)S(1)} fusion(f32[2,512,4096]{2,1,0:T(8,128)S(1)} %get-tuple-element.333, f32[2,512]{1,0:T(2,128)S(1)} %get-tuple-element.334, pred[512,4096]{1,0:T(8,128)(4,1)S(1)} %concatenate.18), kind=kLoop, calls=%fused_computation.4.clone.1 | loop fusion | flops 16776192 | bytes 18882560 | tf_op jit(solution)/shard_map/while/body/eval_jaxpr/reduce_sum | solution.py:22
  172.7 5.6 %fusion.88 = bf16[4,512,2,128]{3,1,0,2:T(8,128)(2,1)S(1)} fusion(bf16[4,512,2,128]{3,1,0,2:T(8,128)(2,1)S(1)} %get-tuple-element.353, s32[]{:T(128)S(6)} %copy.69, f32[512,2,128]{2,0,1:T(8,128)S(1)} %copy-done.6, bf16[4096,2,128]{2,0,1:T(8,128)(2,1)S(1)} %copy-done, f32[2,512,4096]{2,1,0:T(8,128)S(1)} %get-tuple-element.333, ...), kind=kOutput, calls=%fused_computation.25.clone.1 | convolution fusion | flops 1090912256 | bytes 21766148 | tf_op jit(solution)/shard_map/while/body/eval_jaxpr/hqk,khd->qhd/dot_general | solution.py:23
  181.7 1.1 fusion.83
  182.8 1.2 fusion.84
  184.0 1.9 fusion.85
  185.9 5.3 %fusion.86 = (f32[2,512]{1,0:T(2,128)S(1)}, f32[2,512,4096]{2,1,0:T(8,128)S(1)}) fusion(pred[512,4096]{1,0:T(8,128)(4,1)S(1)} %concatenate.18, bf16[4096,2,128]{2,0,1:T(8,128)(2,1)} %get-tuple-element.376, bf16[2048,2,128]{2,0,1:T(8,128)(2,1)S(1)} %get-tuple-element.375, s32[]{:T(128)S(6)} %select_n.80), kind=kOutput, calls=%fused_computation.3.clone.1 | convolution fusion | flops 1086323712 | bytes 21237764 | tf_op jit(solution)/shard_map/while/body/eval_jaxpr/qhd,khd->hqk/dot_general | solution.py:18
  191.3 4.6 %fusion.87 = f32[2,512]{1,0:T(2,128)S(1)} fusion(f32[2,512,4096]{2,1,0:T(8,128)S(1)} %get-tuple-element.333, f32[2,512]{1,0:T(2,128)S(1)} %get-tuple-element.334, pred[512,4096]{1,0:T(8,128)(4,1)S(1)} %concatenate.18), kind=kLoop, calls=%fused_computation.4.clone.1 | loop fusion | flops 16776192 | bytes 18882560 | tf_op jit(solution)/shard_map/while/body/eval_jaxpr/reduce_sum | solution.py:22
  196.0 5.6 %fusion.88 = bf16[4,512,2,128]{3,1,0,2:T(8,128)(2,1)S(1)} fusion(bf16[4,512,2,128]{3,1,0,2:T(8,128)(2,1)S(1)} %get-tuple-element.353, s32[]{:T(128)S(6)} %copy.69, f32[512,2,128]{2,0,1:T(8,128)S(1)} %copy-done.6, bf16[4096,2,128]{2,0,1:T(8,128)(2,1)S(1)} %copy-done, f32[2,512,4096]{2,1,0:T(8,128)S(1)} %get-tuple-element.333, ...), kind=kOutput, calls=%fused_computation.25.clone.1 | convolution fusion | flops 1090912256 | bytes 21766148 | tf_op jit(solution)/shard_map/while/body/eval_jaxpr/hqk,khd->qhd/dot_general | solution.py:23
  205.0 1.1 fusion.83
  206.0 1.2 fusion.84
  207.3 1.9 fusion.85
  209.2 5.3 %fusion.86 = (f32[2,512]{1,0:T(2,128)S(1)}, f32[2,512,4096]{2,1,0:T(8,128)S(1)}) fusion(pred[512,4096]{1,0:T(8,128)(4,1)S(1)} %concatenate.18, bf16[4096,2,128]{2,0,1:T(8,128)(2,1)} %get-tuple-element.376, bf16[2048,2,128]{2,0,1:T(8,128)(2,1)S(1)} %get-tuple-element.375, s32[]{:T(128)S(6)} %select_n.80), kind=kOutput, calls=%fused_computation.3.clone.1 | convolution fusion | flops 1086323712 | bytes 21237764 | tf_op jit(solution)/shard_map/while/body/eval_jaxpr/qhd,khd->hqk/dot_general | solution.py:18
  214.6 4.6 %fusion.87 = f32[2,512]{1,0:T(2,128)S(1)} fusion(f32[2,512,4096]{2,1,0:T(8,128)S(1)} %get-tuple-element.333, f32[2,512]{1,0:T(2,128)S(1)} %get-tuple-element.334, pred[512,4096]{1,0:T(8,128)(4,1)S(1)} %concatenate.18), kind=kLoop, calls=%fused_computation.4.clone.1 | loop fusion | flops 16776192 | bytes 18882560 | tf_op jit(solution)/shard_map/while/body/eval_jaxpr/reduce_sum | solution.py:22
  219.2 5.6 %fusion.88 = bf16[4,512,2,128]{3,1,0,2:T(8,128)(2,1)S(1)} fusion(bf16[4,512,2,128]{3,1,0,2:T(8,128)(2,1)S(1)} %get-tuple-element.353, s32[]{:T(128)S(6)} %copy.69, f32[512,2,128]{2,0,1:T(8,128)S(1)} %copy-done.6, bf16[4096,2,128]{2,0,1:T(8,128)(2,1)S(1)} %copy-done, f32[2,512,4096]{2,1,0:T(8,128)S(1)} %get-tuple-element.333, ...), kind=kOutput, calls=%fused_computation.25.clone.1 | convolution fusion | flops 1090912256 | bytes 21766148 | tf_op jit(solution)/shard_map/while/body/eval_jaxpr/hqk,khd->qhd/dot_general | solution.py:23
  228.2 1.1 fusion.83
  229.3 1.2 fusion.84
  230.5 1.9 fusion.85
  232.5 5.3 %fusion.86 = (f32[2,512]{1,0:T(2,128)S(1)}, f32[2,512,4096]{2,1,0:T(8,128)S(1)}) fusion(pred[512,4096]{1,0:T(8,128)(4,1)S(1)} %concatenate.18, bf16[4096,2,128]{2,0,1:T(8,128)(2,1)} %get-tuple-element.376, bf16[2048,2,128]{2,0,1:T(8,128)(2,1)S(1)} %get-tuple-element.375, s32[]{:T(128)S(6)} %select_n.80), kind=kOutput, calls=%fused_computation.3.clone.1 | convolution fusion | flops 1086323712 | bytes 21237764 | tf_op jit(solution)/shard_map/while/body/eval_jaxpr/qhd,khd->hqk/dot_general | solution.py:18
  237.8 4.6 %fusion.87 = f32[2,512]{1,0:T(2,128)S(1)} fusion(f32[2,512,4096]{2,1,0:T(8,128)S(1)} %get-tuple-element.333, f32[2,512]{1,0:T(2,128)S(1)} %get-tuple-element.334, pred[512,4096]{1,0:T(8,128)(4,1)S(1)} %concatenate.18), kind=kLoop, calls=%fused_computation.4.clone.1 | loop fusion | flops 16776192 | bytes 18882560 | tf_op jit(solution)/shard_map/while/body/eval_jaxpr/reduce_sum | solution.py:22
  242.5 5.6 %fusion.88 = bf16[4,512,2,128]{3,1,0,2:T(8,128)(2,1)S(1)} fusion(bf16[4,512,2,128]{3,1,0,2:T(8,128)(2,1)S(1)} %get-tuple-element.353, s32[]{:T(128)S(6)} %copy.69, f32[512,2,128]{2,0,1:T(8,128)S(1)} %copy-done.6, bf16[4096,2,128]{2,0,1:T(8,128)(2,1)S(1)} %copy-done, f32[2,512,4096]{2,1,0:T(8,128)S(1)} %get-tuple-element.333, ...), kind=kOutput, calls=%fused_computation.25.clone.1 | convolution fusion | flops 1090912256 | bytes 21766148 | tf_op jit(solution)/shard_map/while/body/eval_jaxpr/hqk,khd->qhd/dot_general | solution.py:23
  248.1 8.9 %copy.57 = bf16[2048,2,128]{2,1,0:T(2,128)(2,1)S(1)} copy(bf16[2048,2,128]{2,0,1:T(8,128)(2,1)S(1)} %bitcast.105) | data formatting | bytes 2097152 | tf_op jit(solution)/shard_map/reshape | solution.py:82
  257.0 18.8 %all_to_all.69 = bf16[2048,2,128]{2,1,0:T(2,128)(2,1)S(1)} all-to-all(bf16[2048,2,128]{2,1,0:T(2,128)(2,1)S(1)} %copy.57), channel_id=1, replica_groups=mesh['span'=16,'chip'=8,'core'=2] {'chip','core'}, dimensions={0} | all-to-all | bytes 2097152 | tf_op jit(solution)/shard_map/all_to_all | solution.py:83
  276.6 1.3 copy.60
  (71 shorter events, 12.9 us)
Async XLA Ops:
  6.5 9.3 %copy-start.1 = (bf16[1,128,4096]{2,1,0:T(8,128)(2,1)S(1)}, bf16[1,128,4096]{2,1,0:T(8,128)(2,1)}, u32[]{:S(2)}) copy-start(bf16[1,128,4096]{2,1,0:T(8,128)(2,1)} %param.12) | copy-start | bytes 3145732
  8.9 22.6 %all-to-all-start = ((bf16[128,32,128]{0,2,1:T(8,128)(2,1)}), bf16[128,32,128]{0,2,1:T(8,128)(2,1)S(1)}, u32[]{:S(2)}, u32[]{:S(2)}) async-start(bf16[128,32,128]{0,2,1:T(8,128)(2,1)} %bitcast.2), calls=%async_computation | async-start | bytes 2097152 | tf_op jit(solution)/shard_map/all_to_all | solution.py:38
  31.5 20.2 %all-to-all-start.1 = ((bf16[128,32,128]{0,2,1:T(8,128)(2,1)}), bf16[128,32,128]{0,2,1:T(8,128)(2,1)S(1)}, u32[]{:S(2)}, u32[]{:S(2)}) async-start(bf16[128,32,128]{0,2,1:T(8,128)(2,1)} %bitcast.7), calls=%async_computation.1 | async-start | bytes 2097152 | tf_op jit(solution)/shard_map/all_to_all | solution.py:36
  51.6 31.5 %copy-start.5 = (s32[1,16,2]{1,2,0:T(2,128)S(1)}, s32[1,16,2]{1,2,0:T(2,128)}, u32[]{:S(2)}) copy-start(s32[1,16,2]{1,2,0:T(2,128)} %param.18) | copy-start | bytes 388
  51.6 31.5 %copy-start.4 = (s32[1,2048]{1,0:T(1,128)S(1)}, s32[1,2048]{1,0:T(1,128)}, u32[]{:S(2)}) copy-start(s32[1,2048]{1,0:T(1,128)} %param.17) | copy-start | bytes 24580
  51.6 21.0 %all-to-all-start.2 = ((bf16[128,32,128]{0,2,1:T(8,128)(2,1)}), bf16[128,32,128]{0,2,1:T(8,128)(2,1)}, u32[]{:S(2)}, u32[]{:S(2)}) async-start(bf16[128,32,128]{0,2,1:T(8,128)(2,1)} %bitcast.12), calls=%async_computation.2 | async-start | bytes 2097152 | tf_op jit(solution)/shard_map/all_to_all | solution.py:37
  56.8 93.7 %all-gather.3.cloned.1.call-start = ((), (), s32[]{:S(2)}) async-start(), calls=%async_computation.4 | async-start | bytes 2228224 | tf_op jit(solution)/shard_map/all_gather | solution.py:45
  74.3 25.1 %collective-permute-start = (bf16[2048,2,128]{2,0,1:T(8,128)(2,1)S(1)}, bf16[2048,2,128]{2,0,1:T(8,128)(2,1)}, u32[]{:S(2)}, u32[]{:S(2)}) collective-permute-start(bf16[2048,2,128]{2,0,1:T(8,128)(2,1)S(1)} %bitcast.99), channel_id=1, source_target_pairs={{0,16},{16,32},{32,48},{48,64},{64,80},{80,96},{96,112},{112,128},... | collective-permute-start | bytes 3145736 | tf_op jit(solution)/shard_map/ppermute | solution.py:14
  78.9 43.0 %collective-permute-start.1 = (bf16[2048,2,128]{2,0,1:T(8,128)(2,1)S(1)}, bf16[2048,2,128]{2,0,1:T(8,128)(2,1)}, u32[]{:S(2)}, u32[]{:S(2)}) collective-permute-start(bf16[2048,2,128]{2,0,1:T(8,128)(2,1)S(1)} %bitcast.101), channel_id=1, source_target_pairs={{0,16},{16,32},{32,48},{48,64},{64,80},{80,96},{96,112},{112,128},... | collective-permute-start | bytes 3145736 | tf_op jit(solution)/shard_map/ppermute | solution.py:14
  153.6 1.4 copy-start.2
  158.4 2.3 copy-start.3
  168.0 4.7 %copy-start = (bf16[4096,2,128]{2,0,1:T(8,128)(2,1)S(1)}, bf16[4096,2,128]{2,0,1:T(8,128)(2,1)}, u32[]{:S(2)}) copy-start(bf16[4096,2,128]{2,0,1:T(8,128)(2,1)} %get-tuple-element.377) | copy-start | bytes 6291460 | tf_op jit(solution)/shard_map/while
  168.0 4.7 %copy-start.6 = (f32[512,2,128]{2,0,1:T(8,128)S(1)}, f32[512,2,128]{2,0,1:T(8,128)}, u32[]{:S(2)}) copy-start(f32[512,2,128]{2,0,1:T(8,128)} %fusion.85) | copy-start | bytes 1572868 | tf_op jit(solution)/shard_map/while
  181.7 2.3 copy-start.3
  191.3 4.7 %copy-start = (bf16[4096,2,128]{2,0,1:T(8,128)(2,1)S(1)}, bf16[4096,2,128]{2,0,1:T(8,128)(2,1)}, u32[]{:S(2)}) copy-start(bf16[4096,2,128]{2,0,1:T(8,128)(2,1)} %get-tuple-element.377) | copy-start | bytes 6291460 | tf_op jit(solution)/shard_map/while
  191.3 4.7 %copy-start.6 = (f32[512,2,128]{2,0,1:T(8,128)S(1)}, f32[512,2,128]{2,0,1:T(8,128)}, u32[]{:S(2)}) copy-start(f32[512,2,128]{2,0,1:T(8,128)} %fusion.85) | copy-start | bytes 1572868 | tf_op jit(solution)/shard_map/while
  205.0 2.3 copy-start.3
  214.6 4.7 %copy-start = (bf16[4096,2,128]{2,0,1:T(8,128)(2,1)S(1)}, bf16[4096,2,128]{2,0,1:T(8,128)(2,1)}, u32[]{:S(2)}) copy-start(bf16[4096,2,128]{2,0,1:T(8,128)(2,1)} %get-tuple-element.377) | copy-start | bytes 6291460 | tf_op jit(solution)/shard_map/while
  214.6 4.7 %copy-start.6 = (f32[512,2,128]{2,0,1:T(8,128)S(1)}, f32[512,2,128]{2,0,1:T(8,128)}, u32[]{:S(2)}) copy-start(f32[512,2,128]{2,0,1:T(8,128)} %fusion.85) | copy-start | bytes 1572868 | tf_op jit(solution)/shard_map/while
  228.2 2.3 copy-start.3
  237.8 4.7 %copy-start = (bf16[4096,2,128]{2,0,1:T(8,128)(2,1)S(1)}, bf16[4096,2,128]{2,0,1:T(8,128)(2,1)}, u32[]{:S(2)}) copy-start(bf16[4096,2,128]{2,0,1:T(8,128)(2,1)} %get-tuple-element.377) | copy-start | bytes 6291460 | tf_op jit(solution)/shard_map/while
  237.8 4.7 %copy-start.6 = (f32[512,2,128]{2,0,1:T(8,128)S(1)}, f32[512,2,128]{2,0,1:T(8,128)}, u32[]{:S(2)}) copy-start(f32[512,2,128]{2,0,1:T(8,128)} %fusion.85) | copy-start | bytes 1572868 | tf_op jit(solution)/shard_map/while
Sparse Core Ops, SparseCore 0:
  74.4 76.0 all-gather.2

commit v7 on v3

--- a/solution.py
+++ b/solution.py
@@ -81,10 +81,10 @@
         )
         self_out = attend(q_block, all_keys, all_vals, self_mask, scale)
         audio_out = attend(q_block, audio_keys, audio_vals, audio_mask, scale)
-        return (self_out + audio_out).astype(jnp.bfloat16)
+        return (self_out + audio_out).astype(jnp.bfloat16).reshape(block, head_count * HD)
 
     blocks = lax.map(one_block, jnp.arange(span_rows // block, dtype=jnp.int32))
-    mixed = blocks.reshape(span_rows, head_count, HD)
+    mixed = blocks.reshape(span_rows, head_count * HD)
     back = lax.all_to_all(mixed, SEQ, split_axis=0, concat_axis=1, tiled=True)
     return back.reshape(1, tok_rows, HEADS * HD)
 

time: 272 us -> 269 us (0.989)
  local copies, waits for them, and re-layouts: 27.8 us -> 23.3 us
  matrix products: 58.5 us -> 61.5 us
    reshape x1 -> x0, local copies, waits for them, and re-layouts: 8.9 us -> none  [local(): mixed = blocks.reshape(span_rows, head_count, HD)]
    dynamic_update_slice x0 -> x8, local copies, waits for them, and re-layouts: none -> 3.43 us  [local(): blocks = lax.map(one_block, jnp.arange(span_rows // block, dtype=jnp.int32))]
    dot_general x8, matrix products: 30 us -> 32.8 us  [attend(): jnp.einsum('hqk,khd->qhd', weights.astype(jnp.bfloat16), value_rows, pref...]
    unnamed x15 -> x17, local copies, waits for them, and re-layouts: 7.2 us -> 8.07 us
where the time goes in v7:
time: 269 us
  waiting for transfers between devices  85.6 us (32%)
  matrix products  61.5 us (23%)
  other arithmetic  32.8 us (12%)
  starting transfers between devices  27.6 us (10%)
  local copies, waits for them, and re-layouts  23.3 us (9%)
  blocking collectives  20.8 us (8%)
  between operations  14.2 us (5%)
    all_to_all x1, waiting for transfers between devices, local(): lax.all_to_all(q_local, SEQ, split_axis=1, concat_axis=0, tiled=True)  45.3 us
    dot_general x8, matrix products, attend(): jnp.einsum('hqk,khd->qhd', weights.astype(jnp.bfloat16), value_rows, pref...  32.8 us
    all_gather x1, waiting for transfers between devices, local(): own = lax.all_gather(audio[0], 'chip', axis=0, tiled=True)  26 us
    dot_general x8, matrix products, attend(): jnp.einsum('qhd,khd->hqk', query, key_rows, preferred_element_type=jnp.fl...  25.8 us
    reduce_sum x8, other arithmetic, attend(): den = jnp.sum(weights, axis=-1, keepdims=True)  23.3 us
    all_to_all x1, blocking collectives, local(): back = lax.all_to_all(mixed, SEQ, split_axis=0, concat_axis=1, tiled=True)  20.8 us
    all_to_all x1, waiting for transfers between devices, local(): lax.all_to_all(v_local, SEQ, split_axis=1, concat_axis=0, tiled=True)  13.6 us
    all_to_all x1, starting transfers between devices, local(): lax.all_to_all(q_local, SEQ, split_axis=1, concat_axis=0, tiled=True)  8.19 us
  transfers between devices with their start and end apart: 7, of which 3 were waited for; matrix products, arithmetic and copies ran while one was open for 5% of the time, Pallas kernels for 0%

profile of v7, /device:TPU:1, one launch (start us, length us, event | category | flops | bytes accessed | tf_op | source)
XLA Modules:
  0.0 268.5 jit_solution(8056571570001019599)
XLA Ops:
  6.5 2.3 copy.33
  8.9 6.9 %all-to-all-start.2 = ((bf16[128,32,128]{0,2,1:T(8,128)(2,1)}), bf16[128,32,128]{0,2,1:T(8,128)(2,1)S(1)}, u32[]{:S(2)}, u32[]{:S(2)}) async-start(bf16[128,32,128]{0,2,1:T(8,128)(2,1)} %bitcast.12), calls=%async_computation.2 | async-start | bytes 2097152 | tf_op jit(solution)/shard_map/all_to_all | solution.py:37
  16.5 1.3 copy.30
  17.8 13.6 %all-to-all-done.2 = bf16[128,32,128]{0,2,1:T(8,128)(2,1)S(1)} async-done(((bf16[128,32,128]{0,2,1:T(8,128)(2,1)}), bf16[128,32,128]{0,2,1:T(8,128)(2,1)S(1)}, u32[]{:S(2)}, u32[]{:S(2)}) %all-to-all-start.2) | async-done | bytes 1048608 | tf_op jit(solution)/shard_map/all_to_all | solution.py:37
  31.4 4.4 %all-to-all-start.1 = ((bf16[128,32,128]{0,2,1:T(8,128)(2,1)}), bf16[128,32,128]{0,2,1:T(8,128)(2,1)S(1)}, u32[]{:S(2)}, u32[]{:S(2)}) async-start(bf16[128,32,128]{0,2,1:T(8,128)(2,1)} %bitcast.7), calls=%async_computation.1 | async-start | bytes 2097152 | tf_op jit(solution)/shard_map/all_to_all | solution.py:36
  35.9 26.0 %all-gather.5.cloned.1.call-done = bf16[1,512,1024]{2,1,0:T(8,128)(2,1)} async-done(((bf16[1,64,1024]{2,1,0:T(8,128)(2,1)}), bf16[1,512,1024]{2,1,0:T(8,128)(2,1)}) %all-gather.5.cloned.1.call-update) | async-done | bytes 1048592 | tf_op jit(solution)/shard_map/all_gather | solution.py:44
  61.9 1.3 copy.35
  63.2 4.6 %collective-permute-start.1 = (bf16[2048,2,128]{2,0,1:T(8,128)(2,1)}, bf16[2048,2,128]{2,0,1:T(8,128)(2,1)}, u32[]{:S(2)}, u32[]{:S(2)}) collective-permute-start(bf16[2048,2,128]{2,0,1:T(8,128)(2,1)} %bitcast.16), channel_id=1, source_target_pairs={{0,16},{16,32},{32,48},{48,64},{64,80},{80,96},{96,112},{112,128},... | collective-permute-start | bytes 3145736 | tf_op jit(solution)/shard_map/ppermute | solution.py:14
  67.8 1.3 copy.27
  69.1 8.2 %all-to-all-start = ((bf16[128,32,128]{0,2,1:T(8,128)(2,1)}), bf16[128,32,128]{0,2,1:T(8,128)(2,1)S(1)}, u32[]{:S(2)}, u32[]{:S(2)}) async-start(bf16[128,32,128]{0,2,1:T(8,128)(2,1)} %bitcast.2), calls=%async_computation | async-start | bytes 2097152 | tf_op jit(solution)/shard_map/all_to_all | solution.py:38
  77.3 1.4 copy.32
  78.6 3.5 %collective-permute-start = (bf16[2048,2,128]{2,0,1:T(8,128)(2,1)}, bf16[2048,2,128]{2,0,1:T(8,128)(2,1)}, u32[]{:S(2)}, u32[]{:S(2)}) collective-permute-start(bf16[2048,2,128]{2,0,1:T(8,128)(2,1)} %bitcast.11), channel_id=1, source_target_pairs={{0,16},{16,32},{32,48},{48,64},{64,80},{80,96},{96,112},{112,128},... | collective-permute-start | bytes 3145736 | tf_op jit(solution)/shard_map/ppermute | solution.py:14
  83.0 45.3 %all-to-all-done = bf16[128,32,128]{0,2,1:T(8,128)(2,1)S(1)} async-done(((bf16[128,32,128]{0,2,1:T(8,128)(2,1)}), bf16[128,32,128]{0,2,1:T(8,128)(2,1)S(1)}, u32[]{:S(2)}, u32[]{:S(2)}) %all-to-all-start) | async-done | bytes 1048608 | tf_op jit(solution)/shard_map/all_to_all | solution.py:38
  128.9 1.7 pad_maximum_fusion.1
  130.6 2.8 %copy.36 = bf16[4096,2,128]{0,2,1:T(8,128)(2,1)} copy(bf16[4096,2,128]{2,0,1:T(8,128)(2,1)S(1)} %pad_maximum_fusion.1) | data formatting | bytes 4194304
  133.5 3.1 %pad_maximum_fusion = bf16[4096,2,128]{2,0,1:T(8,128)(2,1)} fusion(bf16[2048,2,128]{2,0,1:T(8,128)(2,1)} %bitcast.11, bf16[2048,2,128]{2,0,1:T(8,128)(2,1)} %collective-permute-done), kind=kLoop, calls=%fused_computation.58 | loop fusion | flops 4194304 | bytes 4194304 | tf_op jit(solution)/shard_map/concatenate | solution.py:60
  136.6 2.9 %fusion.61 = bf16[1024,512]{0,1:T(8,128)(2,1)S(1)} fusion(bf16[1,1024,1024]{2,1,0:T(8,128)(2,1)} %all-gather.7.cloned.1.call-done, bf16[1024,256]{1,0:T(8,128)(2,1)S(1)} %copy-done.5, bf16[1024,256]{1,0:T(8,128)(2,1)S(1)} %copy-done.6), kind=kOutput, calls=%fused_computation.63 | convolution fusion | flops 1076363264 | bytes 4194304 | tf_op jit(solution)/shard_map/dot_general | solution.py:46
  139.5 0.9 fusion.68
  140.6 98.3 %while.12 = (s32[]{:T(128)}, bf16[4,512,256]{2,1,0:T(8,128)(2,1)}, s32[1,2048]{1,0:T(1,128)S(1)}, s32[4]{0:T(128)S(1)}, s32[2048]{0:T(1024)S(1)}, /*index=5*/pre...) while((s32[]{:T(128)}, bf16[4,512,256]{2,1,0:T(8,128)(2,1)}, ...), condition=%wide.region_7.8_spmd.clone.clone, body=%wide.region_2.7_spmd.clone.clone.sunk | while | flops 2745201664 | bytes 85797136 | solution.py:86
  144.0 1.1 fusion.93
  145.0 1.2 fusion.94
  146.2 2.2 fusion.95
  148.4 5.4 %fusion.96 = (f32[2,512]{1,0:T(2,128)S(1)}, f32[2,512,4096]{2,1,0:T(8,128)S(1)}) fusion(pred[512,4096]{1,0:T(8,128)(4,1)S(1)} %concatenate.18, bf16[4096,2,128]{2,0,1:T(8,128)(2,1)} %get-tuple-element.357, bf16[2048,2,128]{2,0,1:T(8,128)(2,1)S(1)} %get-tuple-element.356, s32[]{:T(128)S(6)} %select_n.227), kind=kOutput, calls=%fused_computation.3.clone.1 | convolution fusion | flops 1086323712 | bytes 21237764 | tf_op jit(solution)/shard_map/while/body/eval_jaxpr/qhd,khd->hqk/dot_general | solution.py:18
  153.8 4.6 %fusion.97 = f32[2,512]{1,0:T(2,128)S(1)} fusion(f32[2,512,4096]{2,1,0:T(8,128)S(1)} %get-tuple-element.314, f32[2,512]{1,0:T(2,128)S(1)} %get-tuple-element.315, pred[512,4096]{1,0:T(8,128)(4,1)S(1)} %concatenate.18), kind=kLoop, calls=%fused_computation.4.clone.1 | loop fusion | flops 16776192 | bytes 18882560 | tf_op jit(solution)/shard_map/while/body/eval_jaxpr/reduce_sum | solution.py:22
  158.4 6.1 %fusion.98 = bf16[512,2,128]{0,2,1:T(8,128)(2,1)S(1)} fusion(f32[512,2,128]{0,2,1:T(8,128)} %fusion.95, bf16[4096,2,128]{0,2,1:T(8,128)(2,1)} %get-tuple-element.358, f32[2,512,4096]{2,1,0:T(8,128)S(1)} %get-tuple-element.314, f32[2,512]{1,0:T(2,128)S(1)} %get-tuple-element.315, pred[512,4096]{1,0:T(8,128)(4,1)S(1)} %concatenate.18, ...), kind=kOutput, calls=%fused_computation.21.clone.1 | convolution fusion | flops 1090912256 | bytes 21766144 | tf_op jit(solution)/shard_map/while/body/eval_jaxpr/hqk,khd->qhd/dot_general | solution.py:23
  164.6 0.7 constant_dynamic-update-slice_fusion.2
  168.5 1.1 fusion.93
  169.6 1.2 fusion.94
  170.8 2.2 fusion.95
  172.9 5.4 %fusion.96 = (f32[2,512]{1,0:T(2,128)S(1)}, f32[2,512,4096]{2,1,0:T(8,128)S(1)}) fusion(pred[512,4096]{1,0:T(8,128)(4,1)S(1)} %concatenate.18, bf16[4096,2,128]{2,0,1:T(8,128)(2,1)} %get-tuple-element.357, bf16[2048,2,128]{2,0,1:T(8,128)(2,1)S(1)} %get-tuple-element.356, s32[]{:T(128)S(6)} %select_n.227), kind=kOutput, calls=%fused_computation.3.clone.1 | convolution fusion | flops 1086323712 | bytes 21237764 | tf_op jit(solution)/shard_map/while/body/eval_jaxpr/qhd,khd->hqk/dot_general | solution.py:18
  178.3 4.6 %fusion.97 = f32[2,512]{1,0:T(2,128)S(1)} fusion(f32[2,512,4096]{2,1,0:T(8,128)S(1)} %get-tuple-element.314, f32[2,512]{1,0:T(2,128)S(1)} %get-tuple-element.315, pred[512,4096]{1,0:T(8,128)(4,1)S(1)} %concatenate.18), kind=kLoop, calls=%fused_computation.4.clone.1 | loop fusion | flops 16776192 | bytes 18882560 | tf_op jit(solution)/shard_map/while/body/eval_jaxpr/reduce_sum | solution.py:22
  183.0 6.1 %fusion.98 = bf16[512,2,128]{0,2,1:T(8,128)(2,1)S(1)} fusion(f32[512,2,128]{0,2,1:T(8,128)} %fusion.95, bf16[4096,2,128]{0,2,1:T(8,128)(2,1)} %get-tuple-element.358, f32[2,512,4096]{2,1,0:T(8,128)S(1)} %get-tuple-element.314, f32[2,512]{1,0:T(2,128)S(1)} %get-tuple-element.315, pred[512,4096]{1,0:T(8,128)(4,1)S(1)} %concatenate.18, ...), kind=kOutput, calls=%fused_computation.21.clone.1 | convolution fusion | flops 1090912256 | bytes 21766144 | tf_op jit(solution)/shard_map/while/body/eval_jaxpr/hqk,khd->qhd/dot_general | solution.py:23
  189.2 0.7 constant_dynamic-update-slice_fusion.2
  193.0 1.1 fusion.93
  194.1 1.2 fusion.94
  195.3 2.2 fusion.95
  197.5 5.4 %fusion.96 = (f32[2,512]{1,0:T(2,128)S(1)}, f32[2,512,4096]{2,1,0:T(8,128)S(1)}) fusion(pred[512,4096]{1,0:T(8,128)(4,1)S(1)} %concatenate.18, bf16[4096,2,128]{2,0,1:T(8,128)(2,1)} %get-tuple-element.357, bf16[2048,2,128]{2,0,1:T(8,128)(2,1)S(1)} %get-tuple-element.356, s32[]{:T(128)S(6)} %select_n.227), kind=kOutput, calls=%fused_computation.3.clone.1 | convolution fusion | flops 1086323712 | bytes 21237764 | tf_op jit(solution)/shard_map/while/body/eval_jaxpr/qhd,khd->hqk/dot_general | solution.py:18
  202.9 4.6 %fusion.97 = f32[2,512]{1,0:T(2,128)S(1)} fusion(f32[2,512,4096]{2,1,0:T(8,128)S(1)} %get-tuple-element.314, f32[2,512]{1,0:T(2,128)S(1)} %get-tuple-element.315, pred[512,4096]{1,0:T(8,128)(4,1)S(1)} %concatenate.18), kind=kLoop, calls=%fused_computation.4.clone.1 | loop fusion | flops 16776192 | bytes 18882560 | tf_op jit(solution)/shard_map/while/body/eval_jaxpr/reduce_sum | solution.py:22
  207.5 6.1 %fusion.98 = bf16[512,2,128]{0,2,1:T(8,128)(2,1)S(1)} fusion(f32[512,2,128]{0,2,1:T(8,128)} %fusion.95, bf16[4096,2,128]{0,2,1:T(8,128)(2,1)} %get-tuple-element.358, f32[2,512,4096]{2,1,0:T(8,128)S(1)} %get-tuple-element.314, f32[2,512]{1,0:T(2,128)S(1)} %get-tuple-element.315, pred[512,4096]{1,0:T(8,128)(4,1)S(1)} %concatenate.18, ...), kind=kOutput, calls=%fused_computation.21.clone.1 | convolution fusion | flops 1090912256 | bytes 21766144 | tf_op jit(solution)/shard_map/while/body/eval_jaxpr/hqk,khd->qhd/dot_general | solution.py:23
  213.7 0.7 constant_dynamic-update-slice_fusion.2
  217.6 1.1 fusion.93
  218.6 1.2 fusion.94
  219.8 2.2 fusion.95
  222.0 5.4 %fusion.96 = (f32[2,512]{1,0:T(2,128)S(1)}, f32[2,512,4096]{2,1,0:T(8,128)S(1)}) fusion(pred[512,4096]{1,0:T(8,128)(4,1)S(1)} %concatenate.18, bf16[4096,2,128]{2,0,1:T(8,128)(2,1)} %get-tuple-element.357, bf16[2048,2,128]{2,0,1:T(8,128)(2,1)S(1)} %get-tuple-element.356, s32[]{:T(128)S(6)} %select_n.227), kind=kOutput, calls=%fused_computation.3.clone.1 | convolution fusion | flops 1086323712 | bytes 21237764 | tf_op jit(solution)/shard_map/while/body/eval_jaxpr/qhd,khd->hqk/dot_general | solution.py:18
  227.4 4.6 %fusion.97 = f32[2,512]{1,0:T(2,128)S(1)} fusion(f32[2,512,4096]{2,1,0:T(8,128)S(1)} %get-tuple-element.314, f32[2,512]{1,0:T(2,128)S(1)} %get-tuple-element.315, pred[512,4096]{1,0:T(8,128)(4,1)S(1)} %concatenate.18), kind=kLoop, calls=%fused_computation.4.clone.1 | loop fusion | flops 16776192 | bytes 18882560 | tf_op jit(solution)/shard_map/while/body/eval_jaxpr/reduce_sum | solution.py:22
  232.0 6.1 %fusion.98 = bf16[512,2,128]{0,2,1:T(8,128)(2,1)S(1)} fusion(f32[512,2,128]{0,2,1:T(8,128)} %fusion.95, bf16[4096,2,128]{0,2,1:T(8,128)(2,1)} %get-tuple-element.358, f32[2,512,4096]{2,1,0:T(8,128)S(1)} %get-tuple-element.314, f32[2,512]{1,0:T(2,128)S(1)} %get-tuple-element.315, pred[512,4096]{1,0:T(8,128)(4,1)S(1)} %concatenate.18, ...), kind=kOutput, calls=%fused_computation.21.clone.1 | convolution fusion | flops 1090912256 | bytes 21766144 | tf_op jit(solution)/shard_map/while/body/eval_jaxpr/hqk,khd->qhd/dot_general | solution.py:23
  239.0 20.8 %all_to_all.70 = bf16[16,128,256]{2,1,0:T(8,128)(2,1)S(1)} all-to-all(bf16[16,128,256]{2,1,0:T(8,128)(2,1)} %bitcast.95), channel_id=1, replica_groups=mesh['span'=16,'chip'=8,'core'=2] {'chip','core'}, dimensions={0} | all-to-all | bytes 2097152 | tf_op jit(solution)/shard_map/all_to_all | solution.py:88
  260.4 1.3 copy.40
  (72 shorter events, 14.0 us)
Async XLA Ops:
  6.5 10.0 %copy-start = (bf16[1,128,4096]{2,1,0:T(8,128)(2,1)S(1)}, bf16[1,128,4096]{2,1,0:T(8,128)(2,1)}, u32[]{:S(2)}) copy-start(bf16[1,128,4096]{2,1,0:T(8,128)(2,1)} %param.12) | copy-start | bytes 3145732
  8.9 22.6 %all-to-all-start.2 = ((bf16[128,32,128]{0,2,1:T(8,128)(2,1)}), bf16[128,32,128]{0,2,1:T(8,128)(2,1)S(1)}, u32[]{:S(2)}, u32[]{:S(2)}) async-start(bf16[128,32,128]{0,2,1:T(8,128)(2,1)} %bitcast.12), calls=%async_computation.2 | async-start | bytes 2097152 | tf_op jit(solution)/shard_map/all_to_all | solution.py:37
  15.8 52.0 %copy-start.1 = (bf16[1,128,4096]{2,1,0:T(8,128)(2,1)S(1)}, bf16[1,128,4096]{2,1,0:T(8,128)(2,1)}, u32[]{:S(2)}) copy-start(bf16[1,128,4096]{2,1,0:T(8,128)(2,1)} %param.11) | copy-start | bytes 3145732
  15.8 46.1 %all-gather.5.cloned.1.call-start = ((), (), s32[]{:S(2)}) async-start(), calls=%async_computation.4 | async-start | bytes 1179648 | tf_op jit(solution)/shard_map/all_gather | solution.py:44
  31.4 37.7 %all-to-all-start.1 = ((bf16[128,32,128]{0,2,1:T(8,128)(2,1)}), bf16[128,32,128]{0,2,1:T(8,128)(2,1)S(1)}, u32[]{:S(2)}, u32[]{:S(2)}) async-start(bf16[128,32,128]{0,2,1:T(8,128)(2,1)} %bitcast.7), calls=%async_computation.1 | async-start | bytes 2097152 | tf_op jit(solution)/shard_map/all_to_all | solution.py:36
  35.9 100.7 %all-gather.7.cloned.1.call-start = ((), (), s32[]{:S(2)}) async-start(), calls=%async_computation.5 | async-start | bytes 3145728 | tf_op jit(solution)/shard_map/all_gather | solution.py:45
  61.9 20.9 %copy-start.4 = (s32[1,16,2]{1,2,0:T(2,128)S(1)}, s32[1,16,2]{1,2,0:T(2,128)}, u32[]{:S(2)}) copy-start(s32[1,16,2]{1,2,0:T(2,128)} %param.18) | copy-start | bytes 388
  61.9 20.9 %copy-start.3 = (s32[1,2048]{1,0:T(1,128)S(1)}, s32[1,2048]{1,0:T(1,128)}, u32[]{:S(2)}) copy-start(s32[1,2048]{1,0:T(1,128)} %param.17) | copy-start | bytes 24580
  63.2 65.7 %collective-permute-start.1 = (bf16[2048,2,128]{2,0,1:T(8,128)(2,1)}, bf16[2048,2,128]{2,0,1:T(8,128)(2,1)}, u32[]{:S(2)}, u32[]{:S(2)}) collective-permute-start(bf16[2048,2,128]{2,0,1:T(8,128)(2,1)} %bitcast.16), channel_id=1, source_target_pairs={{0,16},{16,32},{32,48},{48,64},{64,80},{80,96},{96,112},{112,128},... | collective-permute-start | bytes 3145736 | tf_op jit(solution)/shard_map/ppermute | solution.py:14
  69.1 59.2 %all-to-all-start = ((bf16[128,32,128]{0,2,1:T(8,128)(2,1)}), bf16[128,32,128]{0,2,1:T(8,128)(2,1)S(1)}, u32[]{:S(2)}, u32[]{:S(2)}) async-start(bf16[128,32,128]{0,2,1:T(8,128)(2,1)} %bitcast.2), calls=%async_computation | async-start | bytes 2097152 | tf_op jit(solution)/shard_map/all_to_all | solution.py:38
  78.6 54.8 %collective-permute-start = (bf16[2048,2,128]{2,0,1:T(8,128)(2,1)}, bf16[2048,2,128]{2,0,1:T(8,128)(2,1)}, u32[]{:S(2)}, u32[]{:S(2)}) collective-permute-start(bf16[2048,2,128]{2,0,1:T(8,128)(2,1)} %bitcast.11), channel_id=1, source_target_pairs={{0,16},{16,32},{32,48},{48,64},{64,80},{80,96},{96,112},{112,128},... | collective-permute-start | bytes 3145736 | tf_op jit(solution)/shard_map/ppermute | solution.py:14
  133.5 3.1 %copy-start.5 = (bf16[1024,256]{1,0:T(8,128)(2,1)S(1)}, bf16[1024,256]{1,0:T(8,128)(2,1)}, u32[]{:S(2)}) copy-start(bf16[1024,256]{1,0:T(8,128)(2,1)} %param.16) | copy-start | bytes 1572868
  133.5 3.1 %copy-start.6 = (bf16[1024,256]{1,0:T(8,128)(2,1)S(1)}, bf16[1024,256]{1,0:T(8,128)(2,1)}, u32[]{:S(2)}) copy-start(bf16[1024,256]{1,0:T(8,128)(2,1)} %param.15) | copy-start | bytes 1572868
  144.0 2.3 copy-start.2
  168.5 2.3 copy-start.2
  193.0 2.3 copy-start.2
  217.6 2.3 copy-start.2
Sparse Core Ops, SparseCore 0:
  18.4 43.4 all-gather.4
  63.7 21.0 all-gather.6

commit v8 on v7

--- a/solution.py
+++ b/solution.py
@@ -65,27 +65,33 @@
     order = jnp.arange(aud_rows, dtype=jnp.int32)
     held_core, held_chip, row = order // (chips * piece), (order // piece) % chips, order % piece
     positions = (held_chip * cores + held_core) * piece + row
-    block = min(512, span_rows)
+    block = min(1024, span_rows)
+    groups = HEADS // head_count
+    outs = []
+    for g in range(head_count):
+        q_g, k_g, v_g = q_heads[:, g : g + 1], all_keys[:, g : g + 1], all_vals[:, g : g + 1]
+        ak_g, av_g = audio_keys[:, g : g + 1], audio_vals[:, g : g + 1]
 
-    def one_block(index):
-        begin = index * block
-        q_block = lax.dynamic_slice_in_dim(q_heads, begin, block, 0)
-        f_block = lax.dynamic_slice_in_dim(frames, begin, block, 0)
-        lo_block = lax.dynamic_slice_in_dim(lower, begin, block, 0)
-        hi_block = lax.dynamic_slice_in_dim(upper, begin, block, 0)
-        own = frames[None, :] <= f_block[:, None]
-        before = jnp.broadcast_to(has_prev, (block, span_rows))
-        self_mask = jnp.concatenate([before, own], axis=1)
-        audio_mask = jnp.logical_and(
-            positions[None, :] >= lo_block[:, None], positions[None, :] < hi_block[:, None]
-        )
-        self_out = attend(q_block, all_keys, all_vals, self_mask, scale)
-        audio_out = attend(q_block, audio_keys, audio_vals, audio_mask, scale)
-        return (self_out + audio_out).astype(jnp.bfloat16).reshape(block, head_count * HD)
+        def one_block(index, q_g=q_g, k_g=k_g, v_g=v_g, ak_g=ak_g, av_g=av_g):
+            begin = index * block
+            q_block = lax.dynamic_slice_in_dim(q_g, begin, block, 0)
+            f_block = lax.dynamic_slice_in_dim(frames, begin, block, 0)
+            lo_block = lax.dynamic_slice_in_dim(lower, begin, block, 0)
+            hi_block = lax.dynamic_slice_in_dim(upper, begin, block, 0)
+            own = frames[None, :] <= f_block[:, None]
+            before = jnp.broadcast_to(has_prev, (block, span_rows))
+            self_mask = jnp.concatenate([before, own], axis=1)
+            audio_mask = jnp.logical_and(
+                positions[None, :] >= lo_block[:, None], positions[None, :] < hi_block[:, None]
+            )
+            self_out = attend(q_block, k_g, v_g, self_mask, scale)
+            audio_out = attend(q_block, ak_g, av_g, audio_mask, scale)
+            return (self_out + audio_out).astype(jnp.bfloat16).reshape(block, HD)
 
-    blocks = lax.map(one_block, jnp.arange(span_rows // block, dtype=jnp.int32))
-    mixed = blocks.reshape(span_rows, head_count * HD)
-    back = lax.all_to_all(mixed, SEQ, split_axis=0, concat_axis=1, tiled=True)
+        blocks = lax.map(one_block, jnp.arange(span_rows // block, dtype=jnp.int32))
+        mixed = blocks.reshape(span_rows, HD)
+        outs.append(lax.all_to_all(mixed, SEQ, split_axis=0, concat_axis=1, tiled=True).reshape(tok_rows, groups, 1, HD))
+    back = jnp.concatenate(outs, axis=2)
     return back.reshape(1, tok_rows, HEADS * HD)
 
 

time: 269 us -> 250 us (0.929)
  blocking collectives: 20.8 us -> 0 us
  matrix products: 61.5 us -> 55.3 us
  starting transfers between devices: 27.6 us -> 33.7 us
  waiting for transfers between devices: 85.6 us -> 91.1 us
  local copies, waits for them, and re-layouts: 23.3 us -> 19.7 us
    all_gather x1, waiting for transfers between devices: 26 us -> 1.28 us  [local(): own = lax.all_gather(audio[0], 'chip', axis=0, tiled=True)]
    all_to_all x1 -> x0, blocking collectives: 20.8 us -> none  [local(): back = lax.all_to_all(mixed, SEQ, split_axis=0, concat_axis=1, tiled=True)]
    all_to_all x1, waiting for transfers between devices: 0.01 us -> 13.6 us  [local(): lax.all_to_all(k_local, SEQ, split_axis=1, concat_axis=0, tiled=True)]
    all_to_all x0 -> x2, starting transfers between devices: none -> 10.1 us  [local(): lax.all_to_all(mixed, SEQ, split_axis=0, concat_axis=1, tiled=True)]
    all_to_all x0 -> x2, waiting for transfers between devices: none -> 9.32 us  [local(): lax.all_to_all(mixed, SEQ, split_axis=0, concat_axis=1, tiled=True)]
    dot_general x8, matrix products: 32.8 us -> 28.3 us  [attend(): jnp.einsum('hqk,khd->qhd', weights.astype(jnp.bfloat16), value_rows, pref...]
    all_to_all x1, waiting for transfers between devices: 13.6 us -> 17.7 us  [local(): lax.all_to_all(v_local, SEQ, split_axis=1, concat_axis=0, tiled=True)]
    all_to_all x1, starting transfers between devices: 8.19 us -> 4.74 us  [local(): lax.all_to_all(q_local, SEQ, split_axis=1, concat_axis=0, tiled=True)]
  transfers between devices with their start and end apart: 7 -> 9, of which waited for: 3 -> 5; matrix products, arithmetic and copies ran while one was open for 5% -> 22% of each run, Pallas kernels for 0% -> 0%
where the time goes in v8:
time: 250 us; the launch traced here: 249 us
  waiting for transfers between devices  91.1 us (36%)
  matrix products  55.3 us (22%)
  starting transfers between devices  33.7 us (13%)
  other arithmetic  32.5 us (13%)
  local copies, waits for them, and re-layouts  19.7 us (8%)
  between operations  14.2 us (6%)
  loops' own time  2.73 us (1%)
    all_to_all x1, waiting for transfers between devices, local(): lax.all_to_all(q_local, SEQ, split_axis=1, concat_axis=0, tiled=True)  48.5 us
    dot_general x8, matrix products, attend(): jnp.einsum('hqk,khd->qhd', weights.astype(jnp.bfloat16), value_rows, pref...  28.3 us
    dot_general x8, matrix products, attend(): jnp.einsum('qhd,khd->hqk', query, key_rows, preferred_element_type=jnp.fl...  24.1 us
    reduce_sum x8, other arithmetic, attend(): den = jnp.sum(weights, axis=-1, keepdims=True)  20.6 us
    all_to_all x1, waiting for transfers between devices, local(): lax.all_to_all(v_local, SEQ, split_axis=1, concat_axis=0, tiled=True)  17.7 us
    all_to_all x1, waiting for transfers between devices, local(): lax.all_to_all(k_local, SEQ, split_axis=1, concat_axis=0, tiled=True)  13.6 us
    all_to_all x2, starting transfers between devices, local(): lax.all_to_all(mixed, SEQ, split_axis=0, concat_axis=1, tiled=True)  10.1 us
    all_to_all x2, waiting for transfers between devices, local(): lax.all_to_all(mixed, SEQ, split_axis=0, concat_axis=1, tiled=True)  9.32 us
  transfers between devices with their start and end apart: 9, of which 5 were waited for; matrix products, arithmetic and copies ran while one was open for 22% of the time, Pallas kernels for 0%

profile of v8, /device:TPU:1, one launch (start us, length us, event | category | flops | bytes accessed | tf_op | source)
XLA Modules:
  0.0 249.1 jit_solution(7690353412100997692)
XLA Ops:
  6.5 2.3 copy.40
  8.9 6.9 %all-to-all-start.1 = ((bf16[128,32,128]{0,2,1:T(8,128)(2,1)}), bf16[128,32,128]{0,2,1:T(8,128)(2,1)S(1)}, u32[]{:S(2)}, u32[]{:S(2)}) async-start(bf16[128,32,128]{0,2,1:T(8,128)(2,1)} %bitcast.7), calls=%async_computation.1 | async-start | bytes 2097152 | tf_op jit(solution)/shard_map/all_to_all | solution.py:36
  16.5 1.3 copy.43
  17.8 13.6 %all-to-all-done.1 = bf16[128,32,128]{0,2,1:T(8,128)(2,1)S(1)} async-done(((bf16[128,32,128]{0,2,1:T(8,128)(2,1)}), bf16[128,32,128]{0,2,1:T(8,128)(2,1)S(1)}, u32[]{:S(2)}, u32[]{:S(2)}) %all-to-all-start.1) | async-done | bytes 1048608 | tf_op jit(solution)/shard_map/all_to_all | solution.py:36
  31.5 4.4 %all-to-all-start.2 = ((bf16[128,32,128]{0,2,1:T(8,128)(2,1)}), bf16[128,32,128]{0,2,1:T(8,128)(2,1)S(1)}, u32[]{:S(2)}, u32[]{:S(2)}) async-start(bf16[128,32,128]{0,2,1:T(8,128)(2,1)} %bitcast.12), calls=%async_computation.2 | async-start | bytes 2097152 | tf_op jit(solution)/shard_map/all_to_all | solution.py:37
  35.9 2.3 copy.37
  38.1 17.7 %all-to-all-done.2 = bf16[128,32,128]{0,2,1:T(8,128)(2,1)S(1)} async-done(((bf16[128,32,128]{0,2,1:T(8,128)(2,1)}), bf16[128,32,128]{0,2,1:T(8,128)(2,1)S(1)}, u32[]{:S(2)}, u32[]{:S(2)}) %all-to-all-start.2) | async-done | bytes 1048608 | tf_op jit(solution)/shard_map/all_to_all | solution.py:37
  55.8 4.7 %all-to-all-start = ((bf16[128,32,128]{0,2,1:T(8,128)(2,1)}), bf16[128,32,128]{0,2,1:T(8,128)(2,1)S(1)}, u32[]{:S(2)}, u32[]{:S(2)}) async-start(bf16[128,32,128]{0,2,1:T(8,128)(2,1)} %bitcast.2), calls=%async_computation | async-start | bytes 2097152 | tf_op jit(solution)/shard_map/all_to_all | solution.py:38
  60.6 1.3 all-gather.5.cloned.1.call-done
  61.9 1.3 copy.42
  63.2 4.5 %collective-permute-start = (bf16[2048,2,128]{2,0,1:T(8,128)(2,1)}, bf16[2048,2,128]{2,0,1:T(8,128)(2,1)}, u32[]{:S(2)}, u32[]{:S(2)}) collective-permute-start(bf16[2048,2,128]{2,0,1:T(8,128)(2,1)} %bitcast.203), channel_id=1, source_target_pairs={{0,16},{16,32},{32,48},{48,64},{64,80},{80,96},{96,112},{112,128},... | collective-permute-start | bytes 3145736 | tf_op jit(solution)/shard_map/ppermute | solution.py:14
  67.8 1.3 copy.45
  69.1 2.9 %collective-permute-start.1 = (bf16[2048,2,128]{2,0,1:T(8,128)(2,1)}, bf16[2048,2,128]{2,0,1:T(8,128)(2,1)}, u32[]{:S(2)}, u32[]{:S(2)}) collective-permute-start(bf16[2048,2,128]{2,0,1:T(8,128)(2,1)} %bitcast.16), channel_id=1, source_target_pairs={{0,16},{16,32},{32,48},{48,64},{64,80},{80,96},{96,112},{112,128},... | collective-permute-start | bytes 3145736 | tf_op jit(solution)/shard_map/ppermute | solution.py:14
  72.8 48.5 %all-to-all-done = bf16[128,32,128]{0,2,1:T(8,128)(2,1)S(1)} async-done(((bf16[128,32,128]{0,2,1:T(8,128)(2,1)}), bf16[128,32,128]{0,2,1:T(8,128)(2,1)S(1)}, u32[]{:S(2)}, u32[]{:S(2)}) %all-to-all-start) | async-done | bytes 1048608 | tf_op jit(solution)/shard_map/all_to_all | solution.py:38
  121.9 1.1 fusion.146
  123.1 2.7 %fusion.139 = (bf16[4096,1,128]{2,0,1:T(8,128)(2,1)}, bf16[4096,1,128]{2,0,1:T(8,128)(2,1)}) fusion(bf16[2048,2,128]{2,0,1:T(8,128)(2,1)} %collective-permute-done, bf16[2048,2,128]{2,0,1:T(8,128)(2,1)S(1)} %bitcast.204), kind=kLoop, calls=%fused_computation.127 | loop fusion | flops 4194304 | bytes 4194304 | tf_op jit(solution)/shard_map/concatenate | solution.py:60
  125.8 3.0 %fusion.138 = (bf16[4096,1,128]{2,0,1:T(8,128)(2,1)}, bf16[4096,1,128]{2,0,1:T(8,128)(2,1)}) fusion(bf16[2048,2,128]{2,0,1:T(8,128)(2,1)} %collective-permute-done.1, bf16[2048,2,128]{2,0,1:T(8,128)(2,1)} %bitcast.16), kind=kLoop, calls=%fused_computation.126 | loop fusion | flops 4194304 | bytes 4194304 | tf_op jit(solution)/shard_map/concatenate | solution.py:61
  128.8 2.9 %fusion.135 = bf16[1024,512]{0,1:T(8,128)(2,1)S(1)} fusion(bf16[1,1024,1024]{2,1,0:T(8,128)(2,1)} %all-gather.7.cloned.1.call-done, bf16[1024,256]{1,0:T(8,128)(2,1)S(1)} %copy-done.11, bf16[1024,256]{1,0:T(8,128)(2,1)S(1)} %copy-done.12), kind=kOutput, calls=%fused_computation.125 | convolution fusion | flops 1076363264 | bytes 4194304 | tf_op jit(solution)/shard_map/dot_general | solution.py:46
  133.8 43.3 %while.24 = (s32[]{:T(128)}, bf16[2,1024,128]{2,1,0:T(8,128)(2,1)}, s32[1,2048]{1,0:T(1,128)S(1)}, s32[2]{0:T(128)S(1)}, s32[2048]{0:T(1024)S(1)}, /*index=5*/pr...) while((s32[]{:T(128)}, bf16[2,1024,128]{2,1,0:T(8,128)(2,1)}, ...), condition=%wide.region_7.8_spmd.clone.clone, body=%wide.region_2.7_spmd.clone.clone.sunk | while | flops 2743628800 | bytes 81097496 | solution.py:91
  135.1 1.5 broadcast_compare_fusion.4
  136.5 5.6 %fusion.176 = (f32[1024]{0:T(1024)S(1)}, f32[1024,4096]{1,0:T(8,128)S(1)}) fusion(pred[1024,2048]{1,0:T(32,128)(4,1)S(1)} %broadcast_compare_fusion.4, pred[]{:T(512)} %get-tuple-element.617, bf16[4096,1,128]{2,0,1:T(8,128)(2,1)} %get-tuple-element.619, bf16[2048,1,128]{2,0,1:T(8,128)(2,1)S(1)} %get-tuple-element.618, s32[]{:T(128)S(6)} %select_n.373), kind=kOutput, calls=%fused_computation.6.clone.1 | convolution fusion | flops 1086323712 | bytes 20189188 | tf_op jit(solution)/shard_map/while/body/eval_jaxpr/qhd,khd->hqk/dot_general | solution.py:18
  142.2 4.5 %fusion.177 = f32[1024]{0:T(1024)S(1)} fusion(f32[1024,4096]{1,0:T(8,128)S(1)} %get-tuple-element.506, pred[1024,2048]{1,0:T(32,128)(4,1)S(1)} %broadcast_compare_fusion.4, pred[]{:T(512)} %get-tuple-element.617, f32[1024]{0:T(1024)S(1)} %get-tuple-element.507), kind=kLoop, calls=%fused_computation.4.clone.1 | loop fusion | flops 16776192 | bytes 18882560 | tf_op jit(solution)/shard_map/while/body/eval_jaxpr/reduce_sum | solution.py:22
  146.7 5.5 %fusion.178 = f32[1,128,1024]{1,2,0:T(8,128)S(1)} fusion(bf16[4096,1,128]{2,0,1:T(8,128)(2,1)S(1)} %copy-done.5, f32[1024,4096]{1,0:T(8,128)S(1)} %get-tuple-element.506, pred[1024,2048]{1,0:T(32,128)(4,1)S(1)} %broadcast_compare_fusion.4, pred[]{:T(512)} %get-tuple-element.617, f32[1024]{0:T(1024)S(1)} %get-tuple-element.507, f32[1024]{0:T(1024)S(1)} %fusion.177), kind=kOutput, calls=%fused_computation.25.clone.1 | convolution fusion | flops 1090650112 | bytes 20455424 | tf_op jit(solution)/shard_map/while/body/eval_jaxpr/hqk,khd->qhd/dot_general | solution.py:23
  152.3 1.0 fusion.180
  154.0 1.5 fusion.182
  156.7 1.5 broadcast_compare_fusion.4
  158.2 5.6 %fusion.176 = (f32[1024]{0:T(1024)S(1)}, f32[1024,4096]{1,0:T(8,128)S(1)}) fusion(pred[1024,2048]{1,0:T(32,128)(4,1)S(1)} %broadcast_compare_fusion.4, pred[]{:T(512)} %get-tuple-element.617, bf16[4096,1,128]{2,0,1:T(8,128)(2,1)} %get-tuple-element.619, bf16[2048,1,128]{2,0,1:T(8,128)(2,1)S(1)} %get-tuple-element.618, s32[]{:T(128)S(6)} %select_n.373), kind=kOutput, calls=%fused_computation.6.clone.1 | convolution fusion | flops 1086323712 | bytes 20189188 | tf_op jit(solution)/shard_map/while/body/eval_jaxpr/qhd,khd->hqk/dot_general | solution.py:18
  163.8 4.5 %fusion.177 = f32[1024]{0:T(1024)S(1)} fusion(f32[1024,4096]{1,0:T(8,128)S(1)} %get-tuple-element.506, pred[1024,2048]{1,0:T(32,128)(4,1)S(1)} %broadcast_compare_fusion.4, pred[]{:T(512)} %get-tuple-element.617, f32[1024]{0:T(1024)S(1)} %get-tuple-element.507), kind=kLoop, calls=%fused_computation.4.clone.1 | loop fusion | flops 16776192 | bytes 18882560 | tf_op jit(solution)/shard_map/while/body/eval_jaxpr/reduce_sum | solution.py:22
  168.3 5.5 %fusion.178 = f32[1,128,1024]{1,2,0:T(8,128)S(1)} fusion(bf16[4096,1,128]{2,0,1:T(8,128)(2,1)S(1)} %copy-done.5, f32[1024,4096]{1,0:T(8,128)S(1)} %get-tuple-element.506, pred[1024,2048]{1,0:T(32,128)(4,1)S(1)} %broadcast_compare_fusion.4, pred[]{:T(512)} %get-tuple-element.617, f32[1024]{0:T(1024)S(1)} %get-tuple-element.507, f32[1024]{0:T(1024)S(1)} %fusion.177), kind=kOutput, calls=%fused_computation.25.clone.1 | convolution fusion | flops 1090650112 | bytes 20455424 | tf_op jit(solution)/shard_map/while/body/eval_jaxpr/hqk,khd->qhd/dot_general | solution.py:23
  173.9 1.0 fusion.180
  175.6 1.5 fusion.182
  177.1 4.3 %all-to-all-start.3 = ((bf16[16,128,128]{2,1,0:T(8,128)(2,1)}), bf16[16,128,128]{2,1,0:T(8,128)(2,1)S(1)}, u32[]{:S(2)}, u32[]{:S(2)}) async-start(bf16[16,128,128]{2,1,0:T(8,128)(2,1)} %bitcast.24), calls=%async_computation.3 | async-start | bytes 1048576 | tf_op jit(solution)/shard_map/all_to_all | solution.py:93
  183.3 40.8 %while.25 = (s32[]{:T(128)}, bf16[2,1024,128]{2,1,0:T(8,128)(2,1)}, s32[1,2048]{1,0:T(1,128)S(1)}, s32[2]{0:T(128)S(1)}, s32[2048]{0:T(1024)S(1)}, /*index=5*/pr...) while((s32[]{:T(128)}, bf16[2,1024,128]{2,1,0:T(8,128)(2,1)}, ...), condition=%wide.region_13.14_spmd.clone.clone, body=%wide.region_8.13_spmd.clone.clone.sunk | while | flops 2743628800 | bytes 79000872 | solution.py:91
  184.5 1.5 broadcast_compare_fusion.5
  186.0 4.3 %fusion.187 = (f32[1024]{0:T(1024)S(1)}, f32[1024,4096]{1,0:T(8,128)S(1)}) fusion(pred[1024,2048]{1,0:T(32,128)(4,1)S(1)} %broadcast_compare_fusion.5, pred[]{:T(512)} %get-tuple-element.566, bf16[4096,1,128]{2,0,1:T(8,128)(2,1)S(1)} %get-tuple-element.568, bf16[2048,1,128]{2,0,1:T(8,128)(2,1)} %get-tuple-element.567, s32[]{:T(128)S(6)} %select_n.381), kind=kOutput, calls=%fused_computation.64.clone.1 | convolution fusion | flops 1086323712 | bytes 20189700 | tf_op jit(solution)/shard_map/while/body/eval_jaxpr/qhd,khd->hqk/dot_general | solution.py:18
  190.3 4.5 %fusion.188 = f32[1024]{0:T(1024)S(1)} fusion(f32[1024,4096]{1,0:T(8,128)S(1)} %get-tuple-element.523, pred[1024,2048]{1,0:T(32,128)(4,1)S(1)} %broadcast_compare_fusion.5, pred[]{:T(512)} %get-tuple-element.566, f32[1024]{0:T(1024)S(1)} %get-tuple-element.524), kind=kLoop, calls=%fused_computation.62.clone.1 | loop fusion | flops 16776192 | bytes 18882560 | tf_op jit(solution)/shard_map/while/body/eval_jaxpr/reduce_sum | solution.py:22
  194.9 5.6 %fusion.189 = f32[1,128,1024]{1,2,0:T(8,128)S(1)} fusion(bf16[4096,1,128]{2,0,1:T(8,128)(2,1)S(1)} %get-tuple-element.569, f32[1024,4096]{1,0:T(8,128)S(1)} %get-tuple-element.523, pred[1024,2048]{1,0:T(32,128)(4,1)S(1)} %broadcast_compare_fusion.5, pred[]{:T(512)} %get-tuple-element.566, f32[1024]{0:T(1024)S(1)} %get-tuple-element.524, ...), kind=kOutput, calls=%fused_computation.83.clone.1 | convolution fusion | flops 1090650112 | bytes 20455424 | tf_op jit(solution)/shard_map/while/body/eval_jaxpr/hqk,khd->qhd/dot_general | solution.py:23
  200.5 1.1 fusion.191
  202.2 1.5 fusion.193
  204.9 1.5 broadcast_compare_fusion.5
  206.4 4.3 %fusion.187 = (f32[1024]{0:T(1024)S(1)}, f32[1024,4096]{1,0:T(8,128)S(1)}) fusion(pred[1024,2048]{1,0:T(32,128)(4,1)S(1)} %broadcast_compare_fusion.5, pred[]{:T(512)} %get-tuple-element.566, bf16[4096,1,128]{2,0,1:T(8,128)(2,1)S(1)} %get-tuple-element.568, bf16[2048,1,128]{2,0,1:T(8,128)(2,1)} %get-tuple-element.567, s32[]{:T(128)S(6)} %select_n.381), kind=kOutput, calls=%fused_computation.64.clone.1 | convolution fusion | flops 1086323712 | bytes 20189700 | tf_op jit(solution)/shard_map/while/body/eval_jaxpr/qhd,khd->hqk/dot_general | solution.py:18
  210.7 4.5 %fusion.188 = f32[1024]{0:T(1024)S(1)} fusion(f32[1024,4096]{1,0:T(8,128)S(1)} %get-tuple-element.523, pred[1024,2048]{1,0:T(32,128)(4,1)S(1)} %broadcast_compare_fusion.5, pred[]{:T(512)} %get-tuple-element.566, f32[1024]{0:T(1024)S(1)} %get-tuple-element.524), kind=kLoop, calls=%fused_computation.62.clone.1 | loop fusion | flops 16776192 | bytes 18882560 | tf_op jit(solution)/shard_map/while/body/eval_jaxpr/reduce_sum | solution.py:22
  215.3 5.6 %fusion.189 = f32[1,128,1024]{1,2,0:T(8,128)S(1)} fusion(bf16[4096,1,128]{2,0,1:T(8,128)(2,1)S(1)} %get-tuple-element.569, f32[1024,4096]{1,0:T(8,128)S(1)} %get-tuple-element.523, pred[1024,2048]{1,0:T(32,128)(4,1)S(1)} %broadcast_compare_fusion.5, pred[]{:T(512)} %get-tuple-element.566, f32[1024]{0:T(1024)S(1)} %get-tuple-element.524, ...), kind=kOutput, calls=%fused_computation.83.clone.1 | convolution fusion | flops 1090650112 | bytes 20455424 | tf_op jit(solution)/shard_map/while/body/eval_jaxpr/hqk,khd->qhd/dot_general | solution.py:23
  220.9 1.1 fusion.191
  222.6 1.5 fusion.193
  224.1 5.8 %all-to-all-start.4 = ((bf16[16,128,128]{2,1,0:T(8,128)(2,1)}), bf16[16,128,128]{2,1,0:T(8,128)(2,1)S(1)}, u32[]{:S(2)}, u32[]{:S(2)}) async-start(bf16[16,128,128]{2,1,0:T(8,128)(2,1)} %bitcast.27), calls=%async_computation.4 | async-start | bytes 1048576 | tf_op jit(solution)/shard_map/all_to_all | solution.py:93
  230.3 9.3 %all-to-all-done.4 = bf16[16,128,128]{2,1,0:T(8,128)(2,1)S(1)} async-done(((bf16[16,128,128]{2,1,0:T(8,128)(2,1)}), bf16[16,128,128]{2,1,0:T(8,128)(2,1)S(1)}, u32[]{:S(2)}, u32[]{:S(2)}) %all-to-all-start.4) | async-done | bytes 524320 | tf_op jit(solution)/shard_map/all_to_all | solution.py:93
  241.0 1.3 copy.53
  (84 shorter events, 12.2 us)
Async XLA Ops:
  6.5 10.0 %copy-start.2 = (bf16[1,128,4096]{2,1,0:T(8,128)(2,1)S(1)}, bf16[1,128,4096]{2,1,0:T(8,128)(2,1)}, u32[]{:S(2)}) copy-start(bf16[1,128,4096]{2,1,0:T(8,128)(2,1)} %param.15) | copy-start | bytes 3145732
  8.9 22.6 %all-to-all-start.1 = ((bf16[128,32,128]{0,2,1:T(8,128)(2,1)}), bf16[128,32,128]{0,2,1:T(8,128)(2,1)S(1)}, u32[]{:S(2)}, u32[]{:S(2)}) async-start(bf16[128,32,128]{0,2,1:T(8,128)(2,1)} %bitcast.7), calls=%async_computation.1 | async-start | bytes 2097152 | tf_op jit(solution)/shard_map/all_to_all | solution.py:36
  15.8 46.1 %all-gather.5.cloned.1.call-start = ((), (), s32[]{:S(2)}) async-start(), calls=%async_computation.5 | async-start | bytes 1179648 | tf_op jit(solution)/shard_map/all_gather | solution.py:44
  31.5 24.4 %all-to-all-start.2 = ((bf16[128,32,128]{0,2,1:T(8,128)(2,1)}), bf16[128,32,128]{0,2,1:T(8,128)(2,1)S(1)}, u32[]{:S(2)}, u32[]{:S(2)}) async-start(bf16[128,32,128]{0,2,1:T(8,128)(2,1)} %bitcast.12), calls=%async_computation.2 | async-start | bytes 2097152 | tf_op jit(solution)/shard_map/all_to_all | solution.py:37
  35.9 31.9 %copy-start.10 = (s32[1,16,2]{1,2,0:T(2,128)S(1)}, s32[1,16,2]{1,2,0:T(2,128)}, u32[]{:S(2)}) copy-start(s32[1,16,2]{1,2,0:T(2,128)} %param.20) | copy-start | bytes 388
  38.1 33.9 %copy-start.1 = (s32[1,2048]{1,0:T(1,128)S(1)}, s32[1,2048]{1,0:T(1,128)}, u32[]{:S(2)}) copy-start(s32[1,2048]{1,0:T(1,128)} %param.19) | copy-start | bytes 24580
  55.8 65.4 %all-to-all-start = ((bf16[128,32,128]{0,2,1:T(8,128)(2,1)}), bf16[128,32,128]{0,2,1:T(8,128)(2,1)S(1)}, u32[]{:S(2)}, u32[]{:S(2)}) async-start(bf16[128,32,128]{0,2,1:T(8,128)(2,1)} %bitcast.2), calls=%async_computation | async-start | bytes 2097152 | tf_op jit(solution)/shard_map/all_to_all | solution.py:38
  60.6 68.3 %all-gather.7.cloned.1.call-start = ((), (), s32[]{:S(2)}) async-start(), calls=%async_computation.6 | async-start | bytes 3145728 | tf_op jit(solution)/shard_map/all_gather | solution.py:45
  63.2 59.8 %collective-permute-start = (bf16[2048,2,128]{2,0,1:T(8,128)(2,1)}, bf16[2048,2,128]{2,0,1:T(8,128)(2,1)}, u32[]{:S(2)}, u32[]{:S(2)}) collective-permute-start(bf16[2048,2,128]{2,0,1:T(8,128)(2,1)} %bitcast.203), channel_id=1, source_target_pairs={{0,16},{16,32},{32,48},{48,64},{64,80},{80,96},{96,112},{112,128},... | collective-permute-start | bytes 3145736 | tf_op jit(solution)/shard_map/ppermute | solution.py:14
  69.1 54.0 %copy-start = (bf16[16,128,2,128]{3,1,0,2:T(8,128)(2,1)S(1)}, bf16[16,128,2,128]{3,1,0,2:T(8,128)(2,1)}, u32[]{:S(2)}) copy-start(bf16[16,128,2,128]{3,1,0,2:T(8,128)(2,1)} %copy.42) | copy-start | bytes 3145732
  69.1 56.7 %collective-permute-start.1 = (bf16[2048,2,128]{2,0,1:T(8,128)(2,1)}, bf16[2048,2,128]{2,0,1:T(8,128)(2,1)}, u32[]{:S(2)}, u32[]{:S(2)}) collective-permute-start(bf16[2048,2,128]{2,0,1:T(8,128)(2,1)} %bitcast.16), channel_id=1, source_target_pairs={{0,16},{16,32},{32,48},{48,64},{64,80},{80,96},{96,112},{112,128},... | collective-permute-start | bytes 3145736 | tf_op jit(solution)/shard_map/ppermute | solution.py:14
  123.0 5.8 %copy-start.11 = (bf16[1024,256]{1,0:T(8,128)(2,1)S(1)}, bf16[1024,256]{1,0:T(8,128)(2,1)}, u32[]{:S(2)}) copy-start(bf16[1024,256]{1,0:T(8,128)(2,1)} %param.18) | copy-start | bytes 1572868
  123.0 5.8 %copy-start.12 = (bf16[1024,256]{1,0:T(8,128)(2,1)S(1)}, bf16[1024,256]{1,0:T(8,128)(2,1)}, u32[]{:S(2)}) copy-start(bf16[1024,256]{1,0:T(8,128)(2,1)} %param.17) | copy-start | bytes 1572868
  131.8 2.1 copy-start.7
  133.8 49.5 %copy-start.3 = (bf16[4096,1,128]{2,0,1:T(8,128)(2,1)S(1)}, bf16[4096,1,128]{2,0,1:T(8,128)(2,1)}, u32[]{:S(2)}) copy-start(bf16[4096,1,128]{2,0,1:T(8,128)(2,1)} %get-tuple-element.534) | copy-start | bytes 3145732
  133.8 49.5 %copy-start.4 = (bf16[4096,1,128]{2,0,1:T(8,128)(2,1)S(1)}, bf16[4096,1,128]{2,0,1:T(8,128)(2,1)}, u32[]{:S(2)}) copy-start(bf16[4096,1,128]{2,0,1:T(8,128)(2,1)} %get-tuple-element.535) | copy-start | bytes 3145732
  142.2 4.5 %copy-start.5 = (bf16[4096,1,128]{2,0,1:T(8,128)(2,1)S(1)}, bf16[4096,1,128]{2,0,1:T(8,128)(2,1)}, u32[]{:S(2)}) copy-start(bf16[4096,1,128]{2,0,1:T(8,128)(2,1)} %get-tuple-element.620) | copy-start | bytes 3145732 | tf_op jit(solution)/shard_map/while
  152.3 1.7 copy-start.9
  163.8 4.5 %copy-start.5 = (bf16[4096,1,128]{2,0,1:T(8,128)(2,1)S(1)}, bf16[4096,1,128]{2,0,1:T(8,128)(2,1)}, u32[]{:S(2)}) copy-start(bf16[4096,1,128]{2,0,1:T(8,128)(2,1)} %get-tuple-element.620) | copy-start | bytes 3145732 | tf_op jit(solution)/shard_map/while
  173.9 1.7 copy-start.9
  177.1 47.0 %all-to-all-start.3 = ((bf16[16,128,128]{2,1,0:T(8,128)(2,1)}), bf16[16,128,128]{2,1,0:T(8,128)(2,1)S(1)}, u32[]{:S(2)}, u32[]{:S(2)}) async-start(bf16[16,128,128]{2,1,0:T(8,128)(2,1)} %bitcast.24), calls=%async_computation.3 | async-start | bytes 1048576 | tf_op jit(solution)/shard_map/all_to_all | solution.py:93
  194.8 5.7 %copy-start.6 = (bf16[2048,1,128]{2,0,1:T(8,128)(2,1)S(1)}, bf16[2048,1,128]{2,0,1:T(8,128)(2,1)}, u32[]{:S(2)}) copy-start(bf16[2048,1,128]{2,0,1:T(8,128)(2,1)} %get-tuple-element.567) | copy-start | bytes 1572868 | tf_op jit(solution)/shard_map/while
  200.5 1.7 copy-start.8
  215.3 5.7 %copy-start.6 = (bf16[2048,1,128]{2,0,1:T(8,128)(2,1)S(1)}, bf16[2048,1,128]{2,0,1:T(8,128)(2,1)}, u32[]{:S(2)}) copy-start(bf16[2048,1,128]{2,0,1:T(8,128)(2,1)} %get-tuple-element.567) | copy-start | bytes 1572868 | tf_op jit(solution)/shard_map/while
  220.9 1.7 copy-start.8
  224.1 15.5 %all-to-all-start.4 = ((bf16[16,128,128]{2,1,0:T(8,128)(2,1)}), bf16[16,128,128]{2,1,0:T(8,128)(2,1)S(1)}, u32[]{:S(2)}, u32[]{:S(2)}) async-start(bf16[16,128,128]{2,1,0:T(8,128)(2,1)} %bitcast.27), calls=%async_computation.4 | async-start | bytes 1048576 | tf_op jit(solution)/shard_map/all_to_all | solution.py:93
Sparse Core Ops, SparseCore 0:
  18.4 43.4 all-gather.4
  63.7 21.3 all-gather.6

commit v9 on v8

--- a/solution.py
+++ b/solution.py
@@ -2,6 +2,7 @@
 import jax.numpy as jnp
 from jax import lax
 from jax.sharding import PartitionSpec as P
+
 
 HEADS = 32
 SEQ = ("chip", "core")
@@ -26,7 +27,7 @@
     return numer / jnp.transpose(den, (1, 0, 2))
 
 
-def local(queries, keys, values, audio, audio_wk, audio_wv, frame_ids, windows, video_start):
+def step(queries, keys, values, audio, audio_wk, audio_wv, frame_ids, windows, video_start):
     tok_rows = queries.shape[1]
     scale = HD ** (-0.5)
     q_local = queries.reshape(tok_rows, HEADS, HD)
@@ -37,7 +38,6 @@
         lax.all_to_all(v_local, SEQ, split_axis=1, concat_axis=0, tiled=True),
         lax.all_to_all(q_local, SEQ, split_axis=1, concat_axis=0, tiled=True),
     )
-    prev_kh, prev_vh = shifted((k_heads, v_heads), "span", 1)
     span_rows = q_heads.shape[0]
     head_count = q_heads.shape[1]
     joint_w = jnp.concatenate([audio_wk, audio_wv], axis=1)
@@ -57,8 +57,6 @@
     onehot = frames[:, None] == jnp.arange(table.shape[0], dtype=jnp.int32)[None, :]
     lower = jnp.sum(jnp.where(onehot, table[None, :, 0], 0), axis=1)
     upper = jnp.sum(jnp.where(onehot, table[None, :, 1], 0), axis=1)
-    all_keys = jnp.concatenate([prev_kh, k_heads], axis=0)
-    all_vals = jnp.concatenate([prev_vh, v_heads], axis=0)
     cores = lax.axis_size("core")
     chips = lax.axis_size("chip")
     piece = aud_rows // (cores * chips)
@@ -69,7 +67,11 @@
     groups = HEADS // head_count
     outs = []
     for g in range(head_count):
-        q_g, k_g, v_g = q_heads[:, g : g + 1], all_keys[:, g : g + 1], all_vals[:, g : g + 1]
+        cur_k, cur_v = k_heads[:, g : g + 1], v_heads[:, g : g + 1]
+        prev_k, prev_v = shifted(jnp.stack([cur_k, cur_v]), "span", 1)
+        q_g = q_heads[:, g : g + 1]
+        k_g = jnp.concatenate([prev_k, cur_k], axis=0)
+        v_g = jnp.concatenate([prev_v, cur_v], axis=0)
         ak_g, av_g = audio_keys[:, g : g + 1], audio_vals[:, g : g + 1]
 
         def one_block(index, q_g=q_g, k_g=k_g, v_g=v_g, ak_g=ak_g, av_g=av_g):
@@ -110,5 +112,5 @@
     span, seq = mesh.devices.shape
     split = jax.sharding.Mesh(mesh.devices.reshape(span, seq // 2, 2), ("span", "chip", "core"))
     return jax.shard_map(
-        local, mesh=split, in_specs=placed, out_specs=P("span", SEQ, None), check_vma=False
+        step, mesh=split, in_specs=placed, out_specs=P("span", SEQ, None), check_vma=False
     )

time: 250 us -> 273 us (1.092)
  waiting for transfers between devices: 91.1 us -> 108 us
  local copies, waits for them, and re-layouts: 19.7 us -> 24.1 us
    ppermute x2, waiting for transfers between devices: 0.01 us -> 15.8 us  [shifted(): lax.ppermute(value, axis, [(source, source + steps) for source in range(l...]
    another operation x2 -> x5, local copies, waits for them, and re-layouts: 1.72 us -> 7.43 us  [the longest x3 5.7 us: step(): prev_k, prev_v = shifted(jnp.stack([cur_k, cur_v]), 'span', 1)]
    concatenate x3 -> x5, other arithmetic: 5.87 us -> 4.3 us  [the longest x2 2.1 us: step(): k_g = jnp.concatenate([prev_k, cur_k], axis=0)]
    unnamed x25 -> x35, local copies, waits for them, and re-layouts: 8 us -> 7.13 us
where the time goes in v9:
time: 273 us; the launch traced here: 272 us
  waiting for transfers between devices  108 us (40%)
  matrix products  55.1 us (20%)
  starting transfers between devices  34.4 us (13%)
  other arithmetic  33.1 us (12%)
  local copies, waits for them, and re-layouts  24.1 us (9%)
  between operations  14.3 us (5%)
  loops' own time  2.91 us (1%)
    all_to_all x1, waiting for transfers between devices, step(): lax.all_to_all(q_local, SEQ, split_axis=1, concat_axis=0, tiled=True)  55.2 us
    dot_general x8, matrix products, attend(): jnp.einsum('hqk,khd->qhd', weights.astype(jnp.bfloat16), value_rows, pref...  28.2 us
    dot_general x8, matrix products, attend(): jnp.einsum('qhd,khd->hqk', query, key_rows, preferred_element_type=jnp.fl...  24 us
    reduce_sum x8, other arithmetic, attend(): den = jnp.sum(weights, axis=-1, keepdims=True)  20.6 us
    ppermute x2, waiting for transfers between devices, shifted(): lax.ppermute(value, axis, [(source, source + steps) for source in range(l...  15.8 us
    all_to_all x1, waiting for transfers between devices, step(): lax.all_to_all(k_local, SEQ, split_axis=1, concat_axis=0, tiled=True)  14.3 us
    all_to_all x1, waiting for transfers between devices, step(): lax.all_to_all(v_local, SEQ, split_axis=1, concat_axis=0, tiled=True)  12.4 us
    all_to_all x2, starting transfers between devices, step(): lax.all_to_all(mixed, SEQ, split_axis=0, concat_axis=1, tiled=True)  11.7 us
  transfers between devices with their start and end apart: 9, of which 5 were waited for; matrix products, arithmetic and copies ran while one was open for 22% of the time, Pallas kernels for 0%

profile of v9, /device:TPU:1, one launch (start us, length us, event | category | flops | bytes accessed | tf_op | source)
XLA Modules:
  0.0 271.6 jit_solution(2608135943762325023)
XLA Ops:
  6.5 2.4 copy.45
  8.9 6.9 %all-to-all-start.1 = ((bf16[128,32,128]{0,2,1:T(8,128)(2,1)}), bf16[128,32,128]{0,2,1:T(8,128)(2,1)S(1)}, u32[]{:S(2)}, u32[]{:S(2)}) async-start(bf16[128,32,128]{0,2,1:T(8,128)(2,1)} %bitcast.7), calls=%async_computation.1 | async-start | bytes 2097152 | tf_op jit(solution)/shard_map/all_to_all | solution.py:37
  15.9 1.3 copy.48
  17.2 14.3 %all-to-all-done.1 = bf16[128,32,128]{0,2,1:T(8,128)(2,1)S(1)} async-done(((bf16[128,32,128]{0,2,1:T(8,128)(2,1)}), bf16[128,32,128]{0,2,1:T(8,128)(2,1)S(1)}, u32[]{:S(2)}, u32[]{:S(2)}) %all-to-all-start.1) | async-done | bytes 1048608 | tf_op jit(solution)/shard_map/all_to_all | solution.py:37
  31.5 4.4 %all-to-all-start.2 = ((bf16[128,32,128]{0,2,1:T(8,128)(2,1)}), bf16[128,32,128]{0,2,1:T(8,128)(2,1)S(1)}, u32[]{:S(2)}, u32[]{:S(2)}) async-start(bf16[128,32,128]{0,2,1:T(8,128)(2,1)} %bitcast.13), calls=%async_computation.2 | async-start | bytes 2097152 | tf_op jit(solution)/shard_map/all_to_all | solution.py:38
  36.7 1.3 copy.42
  39.3 12.4 %all-to-all-done.2 = bf16[128,32,128]{0,2,1:T(8,128)(2,1)S(1)} async-done(((bf16[128,32,128]{0,2,1:T(8,128)(2,1)}), bf16[128,32,128]{0,2,1:T(8,128)(2,1)S(1)}, u32[]{:S(2)}, u32[]{:S(2)}) %all-to-all-start.2) | async-done | bytes 1048608 | tf_op jit(solution)/shard_map/all_to_all | solution.py:38
  51.7 4.4 %all-to-all-start = ((bf16[128,32,128]{0,2,1:T(8,128)(2,1)}), bf16[128,32,128]{0,2,1:T(8,128)(2,1)S(1)}, u32[]{:S(2)}, u32[]{:S(2)}) async-start(bf16[128,32,128]{0,2,1:T(8,128)(2,1)} %bitcast.2), calls=%async_computation | async-start | bytes 2097152 | tf_op jit(solution)/shard_map/all_to_all | solution.py:39
  56.1 1.3 copy.50
  57.5 3.1 %slice_bitcast_fusion.9 = (bf16[1,2048,1,128]{3,1,2,0:T(8,128)(2,1)S(1)}, bf16[1,2048,1,128]{3,1,2,0:T(8,128)(2,1)}, bf16[2048,1,128]{2,0,1:T(8,128)(2,1)}, bf16...) fusion(bf16[2048,2,128]{2,0,1:T(8,128)(2,1)S(1)} %bitcast.219, ...), kind=kLoop, calls=%fused_computation.147 | loop fusion | bytes 6291456 | tf_op jit(solution)/shard_map/stack | solution.py:71
  60.6 1.1 pad_maximum_fusion
  61.7 4.5 %collective-permute-start = (bf16[2,2048,1,128]{3,1,2,0:T(8,128)(2,1)}, bf16[2,2048,1,128]{3,1,2,0:T(8,128)(2,1)}, u32[]{:S(2)}, u32[]{:S(2)}) collective-permute-start(bf16[2,2048,1,128]{3,1,2,0:T(8,128)(2,1)} %pad_maximum_fusion), channel_id=1, source_target_pairs={{0,16},{16,32},{32,48},{48,64},{64,80},{80,96},{96,112},{112,128},... | collective-permute-start | bytes 3145736 | tf_op jit(solution)/shard_map/ppermute | solution.py:15
  66.3 55.2 %all-to-all-done = bf16[128,32,128]{0,2,1:T(8,128)(2,1)S(1)} async-done(((bf16[128,32,128]{0,2,1:T(8,128)(2,1)}), bf16[128,32,128]{0,2,1:T(8,128)(2,1)S(1)}, u32[]{:S(2)}, u32[]{:S(2)}) %all-to-all-start) | async-done | bytes 1048608 | tf_op jit(solution)/shard_map/all_to_all | solution.py:39
  122.2 1.1 pad_maximum_fusion.3
  123.3 2.4 collective-permute-start.1
  125.7 1.1 fusion.145
  126.9 1.3 slice_bitcast_fusion.2
  128.2 1.1 pad_maximum_fusion.2
  130.3 15.8 %collective-permute-done.1 = bf16[2,2048,1,128]{3,1,2,0:T(8,128)(2,1)} collective-permute-done((bf16[2,2048,1,128]{3,1,2,0:T(8,128)(2,1)}, bf16[2,2048,1,128]{3,1,2,0:T(8,128)(2,1)}, u32[]{:S(2)}, u32[]{:S(2)}) %collective-permute-start.1) | collective-permute-done | bytes 1048608 | tf_op jit(solution)/shard_map/ppermute | solution.py:15
  146.2 1.3 slice_bitcast_fusion
  148.5 1.1 pad_maximum_fusion.4
  149.6 2.9 %fusion.135 = bf16[1024,512]{0,1:T(8,128)(2,1)S(1)} fusion(bf16[1,1024,1024]{2,1,0:T(8,128)(2,1)} %all-gather.7.cloned.1.call-done, bf16[1024,256]{1,0:T(8,128)(2,1)S(1)} %copy-done.17, bf16[1024,256]{1,0:T(8,128)(2,1)S(1)} %copy-done.18), kind=kOutput, calls=%fused_computation.121 | convolution fusion | flops 1076363264 | bytes 4194304 | tf_op jit(solution)/shard_map/dot_general | solution.py:46
  154.5 43.4 %while.24 = (s32[]{:T(128)}, bf16[2,1024,128]{2,1,0:T(8,128)(2,1)}, s32[1,2048]{1,0:T(1,128)S(1)}, s32[2]{0:T(128)S(1)}, s32[2048]{0:T(1024)S(1)}, /*index=5*/pr...) while((s32[]{:T(128)}, bf16[2,1024,128]{2,1,0:T(8,128)(2,1)}, ...), condition=%wide.region_7.8_spmd.clone.clone, body=%wide.region_2.7_spmd.clone.clone.sunk | while | flops 2743628800 | bytes 83195192 | solution.py:93
  155.8 1.5 broadcast_compare_fusion.4
  157.3 5.6 %fusion.175 = (f32[1024]{0:T(1024)S(1)}, f32[1024,4096]{1,0:T(8,128)S(1)}) fusion(pred[1024,2048]{1,0:T(32,128)(4,1)S(1)} %broadcast_compare_fusion.4, pred[]{:T(512)} %get-tuple-element.655, bf16[4096,1,128]{2,0,1:T(8,128)(2,1)} %get-tuple-element.657, bf16[2048,1,128]{2,0,1:T(8,128)(2,1)} %get-tuple-element.656, s32[]{:T(128)S(6)} %select_n.373), kind=kOutput, calls=%fused_computation.6.clone.1 | convolution fusion | flops 1086323712 | bytes 20189700 | tf_op jit(solution)/shard_map/while/body/eval_jaxpr/qhd,khd->hqk/dot_general | solution.py:19
  162.9 4.5 %fusion.176 = f32[1024]{0:T(1024)S(1)} fusion(f32[1024,4096]{1,0:T(8,128)S(1)} %get-tuple-element.544, pred[1024,2048]{1,0:T(32,128)(4,1)S(1)} %broadcast_compare_fusion.4, pred[]{:T(512)} %get-tuple-element.655, f32[1024]{0:T(1024)S(1)} %get-tuple-element.545), kind=kLoop, calls=%fused_computation.4.clone.1 | loop fusion | flops 16776192 | bytes 18882560 | tf_op jit(solution)/shard_map/while/body/eval_jaxpr/reduce_sum | solution.py:23
  167.5 5.5 %fusion.177 = f32[1,128,1024]{1,2,0:T(8,128)S(1)} fusion(bf16[4096,1,128]{2,0,1:T(8,128)(2,1)S(1)} %copy-done.11, f32[1024,4096]{1,0:T(8,128)S(1)} %get-tuple-element.544, pred[1024,2048]{1,0:T(32,128)(4,1)S(1)} %broadcast_compare_fusion.4, pred[]{:T(512)} %get-tuple-element.655, f32[1024]{0:T(1024)S(1)} %get-tuple-element.545, f32[1024]{0:T(1024)S(1)} %fusion.176), kind=kOutput, calls=%fused_computation.25.clone.1 | convolution fusion | flops 1090650112 | bytes 20455424 | tf_op jit(solution)/shard_map/while/body/eval_jaxpr/hqk,khd->qhd/dot_general | solution.py:24
  174.7 1.5 fusion.181
  177.5 1.5 broadcast_compare_fusion.4
  179.0 5.6 %fusion.175 = (f32[1024]{0:T(1024)S(1)}, f32[1024,4096]{1,0:T(8,128)S(1)}) fusion(pred[1024,2048]{1,0:T(32,128)(4,1)S(1)} %broadcast_compare_fusion.4, pred[]{:T(512)} %get-tuple-element.655, bf16[4096,1,128]{2,0,1:T(8,128)(2,1)} %get-tuple-element.657, bf16[2048,1,128]{2,0,1:T(8,128)(2,1)} %get-tuple-element.656, s32[]{:T(128)S(6)} %select_n.373), kind=kOutput, calls=%fused_computation.6.clone.1 | convolution fusion | flops 1086323712 | bytes 20189700 | tf_op jit(solution)/shard_map/while/body/eval_jaxpr/qhd,khd->hqk/dot_general | solution.py:19
  184.6 4.5 %fusion.176 = f32[1024]{0:T(1024)S(1)} fusion(f32[1024,4096]{1,0:T(8,128)S(1)} %get-tuple-element.544, pred[1024,2048]{1,0:T(32,128)(4,1)S(1)} %broadcast_compare_fusion.4, pred[]{:T(512)} %get-tuple-element.655, f32[1024]{0:T(1024)S(1)} %get-tuple-element.545), kind=kLoop, calls=%fused_computation.4.clone.1 | loop fusion | flops 16776192 | bytes 18882560 | tf_op jit(solution)/shard_map/while/body/eval_jaxpr/reduce_sum | solution.py:23
  189.2 5.5 %fusion.177 = f32[1,128,1024]{1,2,0:T(8,128)S(1)} fusion(bf16[4096,1,128]{2,0,1:T(8,128)(2,1)S(1)} %copy-done.11, f32[1024,4096]{1,0:T(8,128)S(1)} %get-tuple-element.544, pred[1024,2048]{1,0:T(32,128)(4,1)S(1)} %broadcast_compare_fusion.4, pred[]{:T(512)} %get-tuple-element.655, f32[1024]{0:T(1024)S(1)} %get-tuple-element.545, f32[1024]{0:T(1024)S(1)} %fusion.176), kind=kOutput, calls=%fused_computation.25.clone.1 | convolution fusion | flops 1090650112 | bytes 20455424 | tf_op jit(solution)/shard_map/while/body/eval_jaxpr/hqk,khd->qhd/dot_general | solution.py:24
  196.4 1.5 fusion.181
  198.0 6.0 %all-to-all-start.3 = ((bf16[16,128,128]{2,1,0:T(8,128)(2,1)}), bf16[16,128,128]{2,1,0:T(8,128)(2,1)S(1)}, u32[]{:S(2)}, u32[]{:S(2)}) async-start(bf16[16,128,128]{2,1,0:T(8,128)(2,1)} %bitcast.28), calls=%async_computation.3 | async-start | bytes 1048576 | tf_op jit(solution)/shard_map/all_to_all | solution.py:95
  205.8 40.9 %while.25 = (s32[]{:T(128)}, bf16[2,1024,128]{2,1,0:T(8,128)(2,1)}, s32[1,2048]{1,0:T(1,128)S(1)}, s32[2]{0:T(128)S(1)}, s32[2048]{0:T(1024)S(1)}, /*index=5*/pr...) while((s32[]{:T(128)}, bf16[2,1024,128]{2,1,0:T(8,128)(2,1)}, ...), condition=%wide.region_13.14_spmd.clone.clone, body=%wide.region_8.13_spmd.clone.clone.sunk | while | flops 2743628800 | bytes 79000872 | solution.py:93
  207.1 1.5 broadcast_compare_fusion.5
  208.6 4.3 %fusion.186 = (f32[1024]{0:T(1024)S(1)}, f32[1024,4096]{1,0:T(8,128)S(1)}) fusion(pred[1024,2048]{1,0:T(32,128)(4,1)S(1)} %broadcast_compare_fusion.5, pred[]{:T(512)} %get-tuple-element.604, bf16[4096,1,128]{2,0,1:T(8,128)(2,1)S(1)} %get-tuple-element.606, bf16[2048,1,128]{2,0,1:T(8,128)(2,1)} %get-tuple-element.605, s32[]{:T(128)S(6)} %select_n.381), kind=kOutput, calls=%fused_computation.64.clone.1 | convolution fusion | flops 1086323712 | bytes 20189700 | tf_op jit(solution)/shard_map/while/body/eval_jaxpr/qhd,khd->hqk/dot_general | solution.py:19
  212.9 4.5 %fusion.187 = f32[1024]{0:T(1024)S(1)} fusion(f32[1024,4096]{1,0:T(8,128)S(1)} %get-tuple-element.561, pred[1024,2048]{1,0:T(32,128)(4,1)S(1)} %broadcast_compare_fusion.5, pred[]{:T(512)} %get-tuple-element.604, f32[1024]{0:T(1024)S(1)} %get-tuple-element.562), kind=kLoop, calls=%fused_computation.62.clone.1 | loop fusion | flops 16776192 | bytes 18882560 | tf_op jit(solution)/shard_map/while/body/eval_jaxpr/reduce_sum | solution.py:23
  217.4 5.6 %fusion.188 = f32[1,128,1024]{1,2,0:T(8,128)S(1)} fusion(bf16[4096,1,128]{2,0,1:T(8,128)(2,1)S(1)} %get-tuple-element.607, f32[1024,4096]{1,0:T(8,128)S(1)} %get-tuple-element.561, pred[1024,2048]{1,0:T(32,128)(4,1)S(1)} %broadcast_compare_fusion.5, pred[]{:T(512)} %get-tuple-element.604, f32[1024]{0:T(1024)S(1)} %get-tuple-element.562, ...), kind=kOutput, calls=%fused_computation.83.clone.1 | convolution fusion | flops 1090650112 | bytes 20455424 | tf_op jit(solution)/shard_map/while/body/eval_jaxpr/hqk,khd->qhd/dot_general | solution.py:24
  224.8 1.5 fusion.192
  227.6 1.5 broadcast_compare_fusion.5
  229.1 4.3 %fusion.186 = (f32[1024]{0:T(1024)S(1)}, f32[1024,4096]{1,0:T(8,128)S(1)}) fusion(pred[1024,2048]{1,0:T(32,128)(4,1)S(1)} %broadcast_compare_fusion.5, pred[]{:T(512)} %get-tuple-element.604, bf16[4096,1,128]{2,0,1:T(8,128)(2,1)S(1)} %get-tuple-element.606, bf16[2048,1,128]{2,0,1:T(8,128)(2,1)} %get-tuple-element.605, s32[]{:T(128)S(6)} %select_n.381), kind=kOutput, calls=%fused_computation.64.clone.1 | convolution fusion | flops 1086323712 | bytes 20189700 | tf_op jit(solution)/shard_map/while/body/eval_jaxpr/qhd,khd->hqk/dot_general | solution.py:19
  233.4 4.5 %fusion.187 = f32[1024]{0:T(1024)S(1)} fusion(f32[1024,4096]{1,0:T(8,128)S(1)} %get-tuple-element.561, pred[1024,2048]{1,0:T(32,128)(4,1)S(1)} %broadcast_compare_fusion.5, pred[]{:T(512)} %get-tuple-element.604, f32[1024]{0:T(1024)S(1)} %get-tuple-element.562), kind=kLoop, calls=%fused_computation.62.clone.1 | loop fusion | flops 16776192 | bytes 18882560 | tf_op jit(solution)/shard_map/while/body/eval_jaxpr/reduce_sum | solution.py:23
  237.9 5.6 %fusion.188 = f32[1,128,1024]{1,2,0:T(8,128)S(1)} fusion(bf16[4096,1,128]{2,0,1:T(8,128)(2,1)S(1)} %get-tuple-element.607, f32[1024,4096]{1,0:T(8,128)S(1)} %get-tuple-element.561, pred[1024,2048]{1,0:T(32,128)(4,1)S(1)} %broadcast_compare_fusion.5, pred[]{:T(512)} %get-tuple-element.604, f32[1024]{0:T(1024)S(1)} %get-tuple-element.562, ...), kind=kOutput, calls=%fused_computation.83.clone.1 | convolution fusion | flops 1090650112 | bytes 20455424 | tf_op jit(solution)/shard_map/while/body/eval_jaxpr/hqk,khd->qhd/dot_general | solution.py:24
  245.2 1.5 fusion.192
  246.7 5.7 %all-to-all-start.4 = ((bf16[16,128,128]{2,1,0:T(8,128)(2,1)}), bf16[16,128,128]{2,1,0:T(8,128)(2,1)S(1)}, u32[]{:S(2)}, u32[]{:S(2)}) async-start(bf16[16,128,128]{2,1,0:T(8,128)(2,1)} %bitcast.35), calls=%async_computation.4 | async-start | bytes 1048576 | tf_op jit(solution)/shard_map/all_to_all | solution.py:95
  252.8 9.3 %all-to-all-done.4 = bf16[16,128,128]{2,1,0:T(8,128)(2,1)S(1)} async-done(((bf16[16,128,128]{2,1,0:T(8,128)(2,1)}), bf16[16,128,128]{2,1,0:T(8,128)(2,1)S(1)}, u32[]{:S(2)}, u32[]{:S(2)}) %all-to-all-start.4) | async-done | bytes 524320 | tf_op jit(solution)/shard_map/all_to_all | solution.py:95
  263.5 1.3 copy.58
  (105 shorter events, 19.4 us)
Async XLA Ops:
  6.5 9.3 %copy-start.7 = (bf16[1,128,4096]{2,1,0:T(8,128)(2,1)S(1)}, bf16[1,128,4096]{2,1,0:T(8,128)(2,1)}, u32[]{:S(2)}) copy-start(bf16[1,128,4096]{2,1,0:T(8,128)(2,1)} %param.15) | copy-start | bytes 3145732
  6.5 30.1 %copy-start.8 = (bf16[1,128,4096]{2,1,0:T(8,128)(2,1)S(1)}, bf16[1,128,4096]{2,1,0:T(8,128)(2,1)}, u32[]{:S(2)}) copy-start(bf16[1,128,4096]{2,1,0:T(8,128)(2,1)} %param.13) | copy-start | bytes 3145732
  8.9 22.6 %all-to-all-start.1 = ((bf16[128,32,128]{0,2,1:T(8,128)(2,1)}), bf16[128,32,128]{0,2,1:T(8,128)(2,1)S(1)}, u32[]{:S(2)}, u32[]{:S(2)}) async-start(bf16[128,32,128]{0,2,1:T(8,128)(2,1)} %bitcast.7), calls=%async_computation.1 | async-start | bytes 2097152 | tf_op jit(solution)/shard_map/all_to_all | solution.py:37
  31.5 20.2 %all-to-all-start.2 = ((bf16[128,32,128]{0,2,1:T(8,128)(2,1)}), bf16[128,32,128]{0,2,1:T(8,128)(2,1)S(1)}, u32[]{:S(2)}, u32[]{:S(2)}) async-start(bf16[128,32,128]{0,2,1:T(8,128)(2,1)} %bitcast.13), calls=%async_computation.2 | async-start | bytes 2097152 | tf_op jit(solution)/shard_map/all_to_all | solution.py:38
  35.9 90.9 %all-gather.5.cloned.1.call-start = ((), (), s32[]{:S(2)}) async-start(), calls=%async_computation.5 | async-start | bytes 1179648 | tf_op jit(solution)/shard_map/all_gather | solution.py:44
  51.7 69.8 %all-to-all-start = ((bf16[128,32,128]{0,2,1:T(8,128)(2,1)}), bf16[128,32,128]{0,2,1:T(8,128)(2,1)S(1)}, u32[]{:S(2)}, u32[]{:S(2)}) async-start(bf16[128,32,128]{0,2,1:T(8,128)(2,1)} %bitcast.2), calls=%async_computation | async-start | bytes 2097152 | tf_op jit(solution)/shard_map/all_to_all | solution.py:39
  56.1 93.5 %all-gather.7.cloned.1.call-start = ((), (), s32[]{:S(2)}) async-start(), calls=%async_computation.6 | async-start | bytes 3145728 | tf_op jit(solution)/shard_map/all_gather | solution.py:45
  57.5 8.7 %copy-start.16 = (s32[1,16,2]{1,2,0:T(2,128)S(1)}, s32[1,16,2]{1,2,0:T(2,128)}, u32[]{:S(2)}) copy-start(s32[1,16,2]{1,2,0:T(2,128)} %param.20) | copy-start | bytes 388
  57.5 8.7 %copy-start = (s32[1,2048]{1,0:T(1,128)S(1)}, s32[1,2048]{1,0:T(1,128)}, u32[]{:S(2)}) copy-start(s32[1,2048]{1,0:T(1,128)} %param.19) | copy-start | bytes 24580
  60.6 61.6 %copy-start.5 = (bf16[1,2048,1,128]{3,1,2,0:T(8,128)(2,1)S(1)}, bf16[1,2048,1,128]{3,1,2,0:T(8,128)(2,1)}, u32[]{:S(2)}) copy-start(bf16[1,2048,1,128]{3,1,2,0:T(8,128)(2,1)} %get-tuple-element.372) | copy-start | bytes 1572868
  60.6 61.6 %copy-start.6 = (bf16[1,2048,1,128]{3,1,2,0:T(8,128)(2,1)S(1)}, bf16[1,2048,1,128]{3,1,2,0:T(8,128)(2,1)}, u32[]{:S(2)}) copy-start(bf16[1,2048,1,128]{3,1,2,0:T(8,128)(2,1)} %get-tuple-element.388) | copy-start | bytes 1572868
  61.7 65.2 %collective-permute-start = (bf16[2,2048,1,128]{3,1,2,0:T(8,128)(2,1)}, bf16[2,2048,1,128]{3,1,2,0:T(8,128)(2,1)}, u32[]{:S(2)}, u32[]{:S(2)}) collective-permute-start(bf16[2,2048,1,128]{3,1,2,0:T(8,128)(2,1)} %pad_maximum_fusion), channel_id=1, source_target_pairs={{0,16},{16,32},{32,48},{48,64},{64,80},{80,96},{96,112},{112,128},... | collective-permute-start | bytes 3145736 | tf_op jit(solution)/shard_map/ppermute | solution.py:15
  122.2 6.0 %copy-start.4 = (bf16[2048,1,128]{2,0,1:T(8,128)(2,1)S(1)}, bf16[2048,1,128]{2,0,1:T(8,128)(2,1)}, u32[]{:S(2)}) copy-start(bf16[2048,1,128]{2,0,1:T(8,128)(2,1)} %get-tuple-element.390) | copy-start | bytes 1572868
  123.3 6.0 %copy-start.3 = (bf16[2048,1,128]{2,0,1:T(8,128)(2,1)S(1)}, bf16[2048,1,128]{2,0,1:T(8,128)(2,1)}, u32[]{:S(2)}) copy-start(bf16[2048,1,128]{2,0,1:T(8,128)(2,1)} %get-tuple-element.374) | copy-start | bytes 1572868
  123.3 22.9 %collective-permute-start.1 = (bf16[2,2048,1,128]{3,1,2,0:T(8,128)(2,1)}, bf16[2,2048,1,128]{3,1,2,0:T(8,128)(2,1)}, u32[]{:S(2)}, u32[]{:S(2)}) collective-permute-start(bf16[2,2048,1,128]{3,1,2,0:T(8,128)(2,1)} %pad_maximum_fusion.3), channel_id=1, source_target_pairs={{0,16},{16,32},{32,48},{48,64},{64,80},{80,96},{96,112},{112,128},... | collective-permute-start | bytes 3145736 | tf_op jit(solution)/shard_map/ppermute | solution.py:15
  126.9 20.6 %copy-start.2 = (bf16[2048,1,128]{2,0,1:T(8,128)(2,1)S(1)}, bf16[2048,1,128]{2,0,1:T(8,128)(2,1)}, u32[]{:S(2)}) copy-start(bf16[2048,1,128]{2,0,1:T(8,128)(2,1)} %get-tuple-element.387) | copy-start | bytes 1572868
  128.2 20.3 %copy-start.1 = (bf16[2048,1,128]{2,0,1:T(8,128)(2,1)S(1)}, bf16[2048,1,128]{2,0,1:T(8,128)(2,1)}, u32[]{:S(2)}) copy-start(bf16[2048,1,128]{2,0,1:T(8,128)(2,1)} %get-tuple-element.373) | copy-start | bytes 1572868
  129.3 20.3 %copy-start.17 = (bf16[1024,256]{1,0:T(8,128)(2,1)S(1)}, bf16[1024,256]{1,0:T(8,128)(2,1)}, u32[]{:S(2)}) copy-start(bf16[1024,256]{1,0:T(8,128)(2,1)} %param.18) | copy-start | bytes 1572868
  129.3 20.3 %copy-start.18 = (bf16[1024,256]{1,0:T(8,128)(2,1)S(1)}, bf16[1024,256]{1,0:T(8,128)(2,1)}, u32[]{:S(2)}) copy-start(bf16[1024,256]{1,0:T(8,128)(2,1)} %param.17) | copy-start | bytes 1572868
  154.5 51.3 %copy-start.9 = (bf16[4096,1,128]{2,0,1:T(8,128)(2,1)S(1)}, bf16[4096,1,128]{2,0,1:T(8,128)(2,1)}, u32[]{:S(2)}) copy-start(bf16[4096,1,128]{2,0,1:T(8,128)(2,1)} %pad_maximum_fusion.5) | copy-start | bytes 3145732
  154.5 51.3 %copy-start.10 = (bf16[4096,1,128]{2,0,1:T(8,128)(2,1)S(1)}, bf16[4096,1,128]{2,0,1:T(8,128)(2,1)}, u32[]{:S(2)}) copy-start(bf16[4096,1,128]{2,0,1:T(8,128)(2,1)} %pad_maximum_fusion.4) | copy-start | bytes 3145732
  162.9 4.5 %copy-start.11 = (bf16[4096,1,128]{2,0,1:T(8,128)(2,1)S(1)}, bf16[4096,1,128]{2,0,1:T(8,128)(2,1)}, u32[]{:S(2)}) copy-start(bf16[4096,1,128]{2,0,1:T(8,128)(2,1)} %get-tuple-element.658) | copy-start | bytes 3145732 | tf_op jit(solution)/shard_map/while
  167.5 5.6 %copy-start.13 = (bf16[2048,1,128]{2,0,1:T(8,128)(2,1)S(1)}, bf16[2048,1,128]{2,0,1:T(8,128)(2,1)}, u32[]{:S(2)}) copy-start(bf16[2048,1,128]{2,0,1:T(8,128)(2,1)} %get-tuple-element.656) | copy-start | bytes 1572868 | tf_op jit(solution)/shard_map/while
  173.0 1.7 copy-start.15
  184.6 4.5 %copy-start.11 = (bf16[4096,1,128]{2,0,1:T(8,128)(2,1)S(1)}, bf16[4096,1,128]{2,0,1:T(8,128)(2,1)}, u32[]{:S(2)}) copy-start(bf16[4096,1,128]{2,0,1:T(8,128)(2,1)} %get-tuple-element.658) | copy-start | bytes 3145732 | tf_op jit(solution)/shard_map/while
  189.2 5.6 %copy-start.13 = (bf16[2048,1,128]{2,0,1:T(8,128)(2,1)S(1)}, bf16[2048,1,128]{2,0,1:T(8,128)(2,1)}, u32[]{:S(2)}) copy-start(bf16[2048,1,128]{2,0,1:T(8,128)(2,1)} %get-tuple-element.656) | copy-start | bytes 1572868 | tf_op jit(solution)/shard_map/while
  194.8 1.7 copy-start.15
  198.0 48.8 %all-to-all-start.3 = ((bf16[16,128,128]{2,1,0:T(8,128)(2,1)}), bf16[16,128,128]{2,1,0:T(8,128)(2,1)S(1)}, u32[]{:S(2)}, u32[]{:S(2)}) async-start(bf16[16,128,128]{2,1,0:T(8,128)(2,1)} %bitcast.28), calls=%async_computation.3 | async-start | bytes 1048576 | tf_op jit(solution)/shard_map/all_to_all | solution.py:95
  217.4 5.6 %copy-start.12 = (bf16[2048,1,128]{2,0,1:T(8,128)(2,1)S(1)}, bf16[2048,1,128]{2,0,1:T(8,128)(2,1)}, u32[]{:S(2)}) copy-start(bf16[2048,1,128]{2,0,1:T(8,128)(2,1)} %get-tuple-element.605) | copy-start | bytes 1572868 | tf_op jit(solution)/shard_map/while
  223.1 1.7 copy-start.14
  237.9 5.6 %copy-start.12 = (bf16[2048,1,128]{2,0,1:T(8,128)(2,1)S(1)}, bf16[2048,1,128]{2,0,1:T(8,128)(2,1)}, u32[]{:S(2)}) copy-start(bf16[2048,1,128]{2,0,1:T(8,128)(2,1)} %get-tuple-element.605) | copy-start | bytes 1572868 | tf_op jit(solution)/shard_map/while
  243.5 1.7 copy-start.14
  246.7 15.4 %all-to-all-start.4 = ((bf16[16,128,128]{2,1,0:T(8,128)(2,1)}), bf16[16,128,128]{2,1,0:T(8,128)(2,1)S(1)}, u32[]{:S(2)}, u32[]{:S(2)}) async-start(bf16[16,128,128]{2,1,0:T(8,128)(2,1)} %bitcast.35), calls=%async_computation.4 | async-start | bytes 1048576 | tf_op jit(solution)/shard_map/all_to_all | solution.py:95
Sparse Core Ops, SparseCore 0:
  38.5 86.5 all-gather.4
  127.0 14.0 all-gather.6
